TPU v7x, 32 devices: a whole 2x2x4 slice. The times are simulated.
32 devices in a mesh: seq: 8 (over y, x, core), wt: 4 (over z).
Axes of the slice: x: 2, y: 2, z: 4, core: 2. Of those that a mesh axis runs over, the one named last changes fastest.
Arguments:
- block_in: bfloat16 [8192, 768], P(('seq', 'wt')), may hold values from -6 to 6
- in_gain: bfloat16 [768], P('wt'), may hold values from 0.5 to 1.5
- proj_gate: bfloat16 [768, 1536], P(None, 'wt'), may hold values from -0.21875 to 0.21875
- proj_inner: bfloat16 [768, 1536], P(None, 'wt'), may hold values from -0.21875 to 0.21875
- proj_bcoef: bfloat16 [768, 256], P(None, 'wt'), may hold values from -0.21875 to 0.21875
- proj_step: bfloat16 [768, 24], P(None, 'wt'), may hold values from -0.21875 to 0.21875
- conv_inner: float32 [4, 1536], P(None, 'wt'), may hold values from -3 to 3
- conv_inner_bias: float32 [1536], P('wt'), may hold values from -0.5 to 0.5
- conv_bcoef: float32 [4, 256], P(None, 'wt'), may hold values from -3 to 3
- conv_bcoef_bias: float32 [256], P('wt'), may hold values from -0.5 to 0.5
- step_bias: float32 [24], P('wt'), may hold values from -6 to -2
- decay_log: float32 [24], P('wt'), may hold values from -4 to 1
- skip_gain: float32 [24], P('wt'), may hold values from 0.5 to 1.5
- norm_gain: float32 [1536], P('wt'), may hold values from 0.5 to 1.5
- proj_out: bfloat16 [1536, 768], P('wt'), may hold values from -0.15625 to 0.15625
- out_grad: bfloat16 [8192, 768], P(('seq', 'wt')), may hold values from -6 to 6
- doc_starts: int32 [1], replicated, may hold values from 0 to 0, as said below
Outputs:
- block_out: bfloat16 [8192, 768], P(('seq', 'wt'))
- input_grad: float32 [8192, 768], P(('seq', 'wt'))
- grad_in_gain: float32 [768], P('wt')
- grad_proj_gate: float32 [768, 1536], P(None, 'wt')
- grad_proj_inner: float32 [768, 1536], P(None, 'wt')
- grad_proj_bcoef: float32 [768, 256], P(None, 'wt')
- grad_proj_step: float32 [768, 24], P(None, 'wt')
- grad_conv_inner: float32 [4, 1536], P(None, 'wt')
- grad_conv_bcoef: float32 [4, 256], P(None, 'wt')
- grad_conv_inner_bias: float32 [1536], P('wt')
- grad_conv_bcoef_bias: float32 [256], P('wt')
- grad_step_bias: float32 [24], P('wt')
- grad_decay_log: float32 [24], P('wt')
- grad_skip_gain: float32 [24], P('wt')
- grad_norm_gain: float32 [1536], P('wt')
- grad_proj_out: float32 [1536, 768], P('wt')
Inputs may be any that keep to these rules, and one draw needn't show every extreme that they name: `doc_starts`: document starts in rising order; the first is 0 and two consecutive starts are 4096 apart or more.
All inputs are finite; a program needn't handle non-finite values.
Results may differ from a plain program's by a relative error of at most 0.012.
The roundings to bfloat16 on the way count: a program that leaves them out, or rounds other values in their place, can miss the bound.
Values may be sent and summed in bfloat16 or wider, within the bound.
No kernel may reach another device: no remote copies, remote signals or barrier semaphores. Data moves between devices by JAX's collectives and lax.ppermute only.
A program may use at most 128 MiB of HBM per device.

v0:
```python
import functools

import jax
import jax.numpy as jnp
import numpy as np
from jax import lax
from jax.experimental import pallas as pl
from jax.experimental.pallas import tpu as pltpu
from jax.sharding import PartitionSpec as P

VMEM = pl.BlockSpec(memory_space=pltpu.VMEM)
LIMIT = 16 << 20
Q = 256
HALF = Q // 2
STEP, ENTER, END, CUMS, SIG = 0, 1, 2, 4, 5
EPSILON = 1e-05
F32 = jnp.float32
B16 = jnp.bfloat16


def nn(a, b):
    return lax.dot_general(a, b, (((1,), (0,)), ((), ())), preferred_element_type=F32)


def nt(a, b):
    return lax.dot_general(a, b, (((1,), (1,)), ((), ())), preferred_element_type=F32)


def tn(a, b):
    return lax.dot_general(a, b, (((0,), (0,)), ((), ())), preferred_element_type=F32)


def split(a):
    high = a.astype(B16)
    return high, (a - high.astype(F32))


def exact_dot(ones, a):
    high, rest = split(a)
    mid, rest = split(rest)
    return nn(ones, high) + nn(ones, mid) + nn(ones, rest.astype(B16))


def two_dot(a, ones):
    high, rest = split(a)
    return nn(high, ones) + nn(rest.astype(B16), ones)


def iota(shape, dim):
    return lax.broadcasted_iota(jnp.int32, shape, dim)


def softplus(a):
    return jnp.maximum(a, 0.0) + jnp.log1p(jnp.exp(-jnp.abs(a)))


def three(a, b):
    ah, al = split(a)
    bh, bl = split(b)
    return nt(ah, bh) + nt(al.astype(B16), bh) + nt(ah, bl.astype(B16))


def silu(a):
    return a * jax.nn.sigmoid(a)


def silu_grad(a):
    sig = jax.nn.sigmoid(a)
    return sig * (1.0 + a * (1.0 - sig))


def rms_scale(x):
    return lax.rsqrt(jnp.mean(x * x, axis=1, keepdims=True) + EPSILON)


def total(refs):
    out = refs[0][...].astype(F32)
    for extra in refs[1:]:
        out = out + extra[...].astype(F32)
    return out


def boundary(starts, base):
    found = False
    for k in range(starts.shape[0]):
        at = starts[k]
        found = found | ((at > 0) & (at > base - 3) & (at < base + Q + 3))
    return found


def prep_kernel(place, w_bt, conv, bias, gain, out):
    span, d = w_bt.shape
    quarter = span // 4
    side = lax.rem(lax.div(place[1], 2), 4)
    out[0:quarter, :] = w_bt[pl.ds(pl.multiple_of(side * quarter, quarter), quarter), :]
    rows = jnp.concatenate([conv[...], bias[...].reshape(1, span), jnp.zeros((11, span), F32)], axis=0)
    high, rest = split(rows)
    mid, rest = split(rest)
    wide = jnp.concatenate(
        [high.astype(F32), mid.astype(F32), rest, jnp.zeros((16, d - 3 * span), F32)], axis=1
    )
    row = jnp.concatenate(
        [gain[...].astype(F32).reshape(1, gain.shape[0]), jnp.zeros((1, d - gain.shape[0]), F32)],
        axis=1,
    )
    wide = jnp.where(iota((16, d), 0) == 5, row, wide)
    out[quarter:, :] = wide.astype(B16)


def stack_kernel(*refs):
    *ins, out = refs
    rows = out.shape[0] // len(ins)
    for k, ref in enumerate(ins):
        out[k * rows : (k + 1) * rows, :] = ref[0:rows, :]


def front_kernel(heads, n, place, starts, *refs):
    xs, halos, earlies = refs[:n], refs[n : 2 * n], refs[2 * n : 3 * n]
    bts = refs[3 * n : 3 * n + 4]
    (
        w_in, w_step, conv_i, bias_i, sbias, dlog, skips, ngain, tri, e_step, e_enter, e_end,
        normed_o, vals_o, bvals_o, pre_o, bpre_o, bc_o, pk_o, pk2_o, cumt_o, scaled_o, sent_o,
        dp_o, fin_o, hv_o, hn_o, tok_o, docrow_o, taps, gain, hp, w_s, vec,
        ext, state, prod, w_bt, x,
    ) = refs[3 * n + 4 :]
    c = pl.program_id(0)
    inner = w_in.shape[1]
    full = ext.shape[1]
    span = w_bt.shape[0] // n
    quarter = span // 4
    gain_own = gain.shape[1] // n
    w = place[0]
    side = lax.rem(lax.div(place[1], 2), 4)

    def project(values):
        wide = values.astype(F32)
        return (wide * rms_scale(wide) * gain[0:1, :]).astype(B16)

    @pl.when(c == 0)
    def _():
        taps[0:4, 0:inner] = conv_i[...]
        taps[4:5, 0:inner] = bias_i[...].reshape(1, inner)
        taps[5:8, :] = jnp.zeros((3, full), F32)
        hp[...] = jnp.zeros_like(hp)
        for g in range(16):
            lanes = slice(8 * g, 8 * g + heads)
            hp[0:1, lanes] = sbias[...].reshape(1, heads)
            hp[1:2, lanes] = jnp.exp(dlog[...].reshape(1, heads))
        low = iota((1, 128), 1) < 64
        for p in range(heads // 2):
            one, two = (jnp.broadcast_to(skips[...].reshape(1, heads)[:, h : h + 1], (1, 128)) for h in (2 * p, 2 * p + 1))
            vec[0:1, p * 128 : (p + 1) * 128] = jnp.where(low, one, two)
        vec[1:2, :] = ngain[...].reshape(1, inner)
        copies = (iota((heads, 128), 0) == lax.rem(iota((heads, 128), 1), 8)).astype(F32)
        w_s[...] = nn(w_step[...], copies.astype(B16)).astype(B16)
        for k in range(n):
            v = lax.rem(w - k + n, n)
            for q in range(4):
                at = v * span + (side ^ q) * quarter
                w_bt[pl.ds(pl.multiple_of(at, quarter), quarter), :] = bts[q][
                    k * quarter : (k + 1) * quarter, :
                ]
        for v in range(n):
            for k in range(n):

                @pl.when(lax.rem(w - v + n, n) == k)
                def _(v=v, k=k):
                    low = inner + v * span
                    small = earlies[k][quarter:, :].astype(F32)
                    taps[0:5, low : low + span] = (
                        small[0:5, 0:span] + small[0:5, span : 2 * span]
                    ) + small[0:5, 2 * span : 3 * span]
                    gain[0:1, v * gain_own : (v + 1) * gain_own] = small[5:6, 0:gain_own]

        hn = project(total(halos))
        hn_o[...] = hn
        ext[0:8, 0:inner] = nn(hn, w_in[...])
        ext[0:8, inner:full] = nt(hn, w_bt[...])
        hv_o[...] = ext[0:8, :]
        state[...] = jnp.zeros_like(state)
        prod[...] = jnp.ones_like(prod)

    @pl.when(c > 0)
    def _():
        ext[0:8, :] = ext[Q : Q + 8, :]

    for k in range(n):

        @pl.when(lax.rem(w - c + n, n) == k)
        def _(k=k):
            x[...] = xs[k][...]

    def docs_at(positions):
        found = jnp.zeros(positions.shape, jnp.int32)
        for k in range(starts.shape[0]):
            found = found + (starts[k] <= positions).astype(jnp.int32)
        return found - 1

    base = (place[1] * pl.num_programs(0) + c) * Q
    here = base + iota((Q, 8), 0)
    lane = iota((Q, 8), 1)
    other = jnp.where(lane < 3, here - 3 + lane, jnp.where(lane == 3, base - 1, base + Q - 1))
    docs = docs_at(here)
    tok = jnp.where(lane == 5, docs, (docs_at(other) == docs).astype(jnp.int32)).astype(F32)
    tok_o[...] = tok
    docrow_o[...] = docs_at(base + iota((8, Q), 1)).astype(F32)

    normed = project(x[...])
    normed_o[...] = normed
    ext[8 : Q + 8, 0:inner] = nn(normed, w_in[...])
    ext[8 : Q + 8, inner:full] = nt(normed, w_bt[...])
    vals_o[...] = ext[8 : Q + 8, 0:inner].astype(B16)
    bvals_o[...] = ext[8 : Q + 8, inner:full].astype(B16)
    pre = taps[4:5, :] + taps[3:4, :] * ext[8 : Q + 8, :]
    for k in range(3):
        pre = pre + taps[k : k + 1, :] * ext[5 + k : 5 + k + Q, :]
    pre_o[...] = pre[:, :inner]
    bpre_o[...] = pre[:, inner:]

    @pl.when(boundary(starts, base))
    def _():
        again = taps[4:5, :] + taps[3:4, :] * ext[8 : Q + 8, :]
        for k in range(3):
            again = again + taps[k : k + 1, :] * ext[5 + k : 5 + k + Q, :] * tok_o[:, k : k + 1]
        pre_o[...] = again[:, :inner]
        bpre_o[...] = again[:, inner:]

    act = silu(pre_o[...])
    bc = silu(bpre_o[...]).astype(B16)
    bc_o[...] = bc
    sr = nn(normed, w_s[...]) + hp[0:1, :]
    step = softplus(sr)
    cums = exact_dot(tri[...], -hp[1:2, :] * step)
    enter = jnp.exp(cums) * tok[:, 3:4]
    end = jnp.exp(cums[Q - 1 : Q, :] - cums) * tok[:, 4:5]
    lane = iota((Q, 128), 1)
    group = lax.rem(lane, 64) // 8
    pk = jnp.where(
        group == STEP, step,
        jnp.where(
            group == ENTER, enter,
            jnp.where(group == END, end, jnp.where(group == SIG, jax.nn.sigmoid(sr), cums)),
        ),
    )
    pk_o[...] = pk
    high, low = split(pk)
    pk2 = jnp.where(lane < 64, high.astype(F32), low).astype(B16)
    pk2_o[...] = pk2
    cumt_o[...] = cums.T[0:8, :]
    scaled = nn(pk2, e_step[...]) * act
    scaled_o[...] = scaled.astype(B16)
    x16, x_lo = split(nn(pk2, e_end[...]) * scaled)
    x_lo = x_lo.astype(B16)
    carry = nn(pk2[Q - 16 :], e_enter[...])[15:16, :]
    sent_o[0] = state[...]
    dp_o[0] = prod[...]
    state[...] = carry * state[...] + tn(bc[:, :128], x16) + tn(bc[:, :128], x_lo)
    prod[...] = prod[...] * carry
    fin_o[0:128, :] = state[...].astype(B16)
    fin_o[128:144, :] = jnp.concatenate([prod[...], prod[...]], axis=0).astype(B16)


def intra_kernel(heads, normed, w_gate, pre, bc, pk, cumt, scaled, tok, docrow, vec, gate_o, y_o):
    gate_o[...] = nn(normed[...], w_gate[...])
    low = iota((HALF, 128), 1) < 64
    for block in range(2):
        rows = slice(block * HALF, (block + 1) * HALF)
        wide = (block + 1) * HALF
        scores = nt(bc[rows, 128:], bc[:wide, :128])
        mask = (block * HALF + iota((HALF, wide), 0) >= iota((HALF, wide), 1)) & (
            tok[rows, 5:6] == docrow[0:1, :wide]
        )
        for pair in range(heads // 2):
            cols = slice(pair * 128, (pair + 1) * 128)
            values = scaled[:wide, cols]
            outs = []
            for h in (2 * pair, 2 * pair + 1):
                diff = pk[rows, 8 * CUMS + h : 8 * CUMS + h + 1] - cumt[h : h + 1, :wide]
                mix = scores * jnp.where(mask, jnp.exp(diff), 0.0)
                outs.append(nn(mix.astype(B16), values))
            y_o[rows, cols] = jnp.where(low, *outs) + vec[0:1, cols] * silu(pre[rows, cols])


def fold_states(keep, others, out):
    state = jnp.zeros(out.shape, F32)
    for ref in reversed(others):
        state = ref[128:129, :].astype(F32) * state + ref[0:128, :].astype(F32)
    out[...] = keep[128:129, :] * state + keep[0:128, :]


def pair_kernel(reverse, place, own, other, keep_o, total_o):
    mine, theirs = own[...].astype(F32), other[...].astype(F32)
    earlier = lax.rem(place[1], 2) == (0 if reverse else 1)
    keep_o[0:128, :] = jnp.where(earlier, theirs[0:128, :], 0.0)
    keep_o[128:, :] = jnp.where(earlier, theirs[128:136, :], 1.0)
    total_o[0:128, :] = jnp.where(
        earlier,
        mine[128:129, :] * theirs[0:128, :] + mine[0:128, :],
        theirs[128:129, :] * mine[0:128, :] + theirs[0:128, :],
    ).astype(B16)
    total_o[128:, :] = (mine[128:, :] * theirs[128:, :]).astype(B16)


def join_kernel(n, m, place, y, gate, bc, pk2, sent, dp, keep, *refs):
    others, cots = refs[:m], refs[m : m + n]
    (w_out, vec, e_enter, ssd_o, inter_o, gn_o, stats_o, s_in, cot_o) = refs[m + n :]
    c = pl.program_id(0)
    inner = y.shape[1]

    @pl.when(c == 0)
    def _():
        fold_states(keep, others, s_in)

    for k in range(n):

        @pl.when(lax.rem(place[0] - c + n, n) == k)
        def _(k=k):
            cot_o[...] = cots[k][...]

    entering = sent[0] + dp[0, 0:1, :] * s_in[...]
    inter = nn(pk2[...], e_enter[...]) * nn(bc[:, 128:], entering.astype(B16))
    inter_o[...] = inter
    ssd = y[...] + inter
    ssd_o[...] = ssd
    gated = ssd * silu(gate[...])
    gn = nt(cot_o[...], w_out[...])
    gn_o[...] = gn
    lane = iota((inner, 128), 1)
    first = (lane == 0).astype(F32).astype(B16)
    second = (lane == 1).astype(F32).astype(B16)
    both = two_dot(gated * gated, first)
    both = both + two_dot(vec[1:2, :] * gn * gated, second)
    stats_o[...] = both.T[0:8, :]


def gate_kernel(n, width_all, ssd, gate, gn, vec, pre, bc, pk2, e_enter, *refs):
    stats = refs[:n]
    norm_o, gate_o, gs_o, sums_o, sb_o, db_o, fin_o, state, prod = refs[n:]
    i = pl.program_id(0)

    @pl.when(i == 0)
    def _():
        state[...] = jnp.zeros_like(state)
        prod[...] = jnp.ones_like(prod)
        sums_o[...] = jnp.zeros_like(sums_o)

    st = total(stats)
    rms = lax.rsqrt(st[0:1, :] / width_all + EPSILON)
    pull = rms * rms * rms * st[1:2, :] / width_all
    st = jnp.concatenate([rms, pull, jnp.zeros((126, Q), F32)], axis=0).T
    rms, pull = st[:, 0:1], st[:, 1:2]
    g = gate[...]
    sig = jax.nn.sigmoid(g)
    s = ssd[...]
    act_g = g * sig
    gated = s * act_g
    scaled = gated * rms
    ngain = vec[1:2, :]
    norm_o[...] = (scaled * ngain).astype(B16)
    gn_ = gn[...]
    grad_gated = rms * (ngain * gn_) - gated * pull
    gs = grad_gated * act_g
    gs_o[...] = gs
    gate_o[...] = (grad_gated * s * (sig * (1.0 + g * (1.0 - sig)))).astype(B16)
    sums_o[0:1, :] += jnp.sum(gn_ * scaled, axis=0, keepdims=True)
    sums_o[1:2, :] += jnp.sum(gs * silu(pre[...]), axis=0, keepdims=True)
    enter = nn(pk2[...], e_enter[...])
    carry = enter[Q - 1 : Q, :]
    sb_o[0] = state[...]
    db_o[0] = prod[...]
    state[...] = carry * state[...] + tn(bc[:, 128:], (enter * gs).astype(B16)) + tn(bc[:, 128:], split(enter * gs)[1].astype(B16))
    prod[...] = prod[...] * carry
    fin_o[0:128, :] = state[...].astype(B16)
    fin_o[128:144, :] = jnp.concatenate([prod[...], prod[...]], axis=0).astype(B16)


def intra_back_kernel(
    heads, gs, bc, pk, pk2, cumt, scaled, tok, docrow, sent, dp, s_in, e_enter,
    gsc_o, rc_o, gbc_o, tot, plus, minus,
):
    low = iota((HALF, 128), 1) < 64
    g16 = gs[...].astype(B16)
    plus[...] = jnp.zeros_like(plus)
    for block in range(2):
        rows = slice(block * HALF, (block + 1) * HALF)
        wide = slice(block * HALF, Q)
        width = Q - block * HALF
        scores = nt(bc[rows, :128], bc[wide, 128:])
        mask = (iota((HALF, width), 0) <= iota((HALF, width), 1)) & (
            tok[rows, 5:6] == docrow[0:1, wide]
        )
        sums = jnp.zeros((HALF, width), F32)
        lane = iota((HALF, 128), 1)
        minus_acc = jnp.zeros((HALF, 128), F32)
        for pair in range(heads // 2):
            cols = slice(pair * 128, (pair + 1) * 128)
            mine = scaled[rows, cols]
            grads = g16[wide, cols]
            outs = []
            for h in (2 * pair, 2 * pair + 1):
                diff = cumt[h : h + 1, wide] - pk[rows, 8 * CUMS + h : 8 * CUMS + h + 1]
                decay = jnp.where(mask, jnp.exp(diff), 0.0)
                keep = low if h % 2 == 0 else ~low
                masked = jnp.where(keep, mine.astype(F32), 0.0).astype(B16)
                weighted = decay * nt(masked, grads)
                sums = sums + weighted
                ws = scores * weighted
                plus[h : h + 1, wide] += jnp.sum(ws, axis=0, keepdims=True)
                minus_acc = jnp.where(
                    lax.rem(lane, 8) == h, jnp.sum(ws, axis=1, keepdims=True), minus_acc
                )
                outs.append(nn((scores * decay).astype(B16), grads))
            gsc_o[rows, cols] = jnp.where(low, *outs)
        minus[rows, :] = minus_acc
        tot[rows, wide] = sums.astype(B16)
    tot[HALF:, :HALF] = jnp.zeros((HALF, HALF), B16)
    rc_o[...] = jnp.concatenate([plus[...]] * 16, axis=0).T - minus[...]
    entering = sent[0] + dp[0, 0:1, :] * s_in[...]
    t16 = tot[...]
    enter = nn(pk2[...], e_enter[...]) * gs[...]
    gbc_o[:, :128] = nn(t16, bc[:, 128:])
    gbc_o[:, 128:] = tn(t16, bc[:, :128]) + three(enter, entering)


def conv_back(i, count, masked, gp, tok, taps, vals, hv, ext, mext, shift, out, sums_o, rim_o):
    ch = gp.shape[1]

    @pl.when(i == 0)
    def _():
        ext[Q : Q + 8, :] = jnp.zeros((8, ch), F32)
        mext[Q : Q + 8, :] = jnp.zeros((8, 8), F32)
        sums_o[...] = jnp.zeros_like(sums_o)

    @pl.when(i > 0)
    def _():
        ext[Q : Q + 8, :] = ext[0:8, :]
        mext[Q : Q + 8, :] = mext[0:8, :]

    ext[0:Q, :] = gp
    mext[0:Q, :] = tok
    sums_o[4:5, :] += jnp.sum(gp, axis=0, keepdims=True)

    def sweep(use_mask):
        vals_ = vals.astype(F32)
        acc = jnp.zeros((Q, ch), F32)
        for k in range(4):
            z = ext[3 - k : 3 - k + Q, :]
            if k < 3 and use_mask:
                z = z * mext[3 - k : 3 - k + Q, k : k + 1]
            acc = acc + taps[k : k + 1, :] * z
            sums_o[k : k + 1, :] += jnp.sum(vals_ * z, axis=0, keepdims=True)
        out[...] = acc.astype(B16)

    @pl.when(masked)
    def _():
        sweep(True)

    @pl.when(jnp.logical_not(masked))
    def _():
        sweep(False)

    @pl.when(i == count - 1)
    def _():
        rim = jnp.zeros((8, ch), F32)
        shift[0:8, :] = jnp.zeros((8, ch), F32)
        for k in range(3):
            shift[8:16, :] = ext[0:8, :] * mext[0:8, k : k + 1]
            moved = shift[3 - k : 11 - k, :]
            rim = rim + taps[k : k + 1, :] * moved
            sums_o[k : k + 1, :] += jnp.sum(hv * moved, axis=0, keepdims=True)
        rim_o[...] = rim


def chunk_base(place, count, i):
    return (place[1] * count + (count - 1 - i)) * Q


def bcoef_back_kernel(
    count, n, m, place, starts, gbc, pre, vals, pk2, scaled, tok, sb, db, taps, hv, e_end,
    keep, *refs
):
    others, packs = refs[:m], refs[m : m + n]
    sums_o, s_after, ext, mext, shift, rim_o, out, pieces = refs[m + n :]
    i = pl.program_id(0)
    inner = scaled.shape[1]

    @pl.when(i == 0)
    def _():
        fold_states(keep, others, s_after)

    after_ = sb[0] + db[0, 0:1, :] * s_after[...]
    x16 = nn(pk2[...], e_end[...]) * scaled[...].astype(F32)
    gbm = gbc[:, :128] + three(x16, after_)
    gp = jnp.concatenate([gbm, gbc[:, 128:]], axis=1) * silu_grad(pre[...])
    conv_back(
        i, count, boundary(starts, chunk_base(place, count, i)), gp, tok[...],
        taps[:, inner:], vals[...], hv[:, inner:], ext, mext, shift, out, sums_o, rim_o,
    )
    span = 256 // n
    row = pl.multiple_of((count - 1 - i) * HALF, HALF)
    for v in range(n):
        piece = out[:, v * span : (v + 1) * span]
        pieces[v] = jnp.concatenate([piece[:HALF], piece[HALF:]], axis=1)
    for k in range(n):
        packs[k][pl.ds(row, HALF), :] = pieces[lax.rem(place[0] + k, n)]

    @pl.when(i == count - 1)
    def _():
        for v in range(n):
            edge = rim_o[:, v * span : (v + 1) * span]
            pieces[v, 0:16, 0:span] = jnp.concatenate([edge, edge], axis=0).astype(B16)
        for k in range(n):
            packs[k][count * HALF :, :] = pieces[lax.rem(place[0] + k, n), 0:16, :]


def inner_back_kernel(
    count, place, starts, gs, gsc, rc, inter, pre, vals, bc, pk, pk2, scaled, tok, sent,
    dp, s_in, sb, db, s_after, taps, hp, hv, vec, tri, e_step, e_enter, e_end, hmap,
    gv_o, step_o, rim_o, sums_o, small_o, ext, mext, shift,
):
    i = pl.program_id(0)
    entering = sent[0] + dp[0, 0:1, :] * s_in[...]
    after_ = sb[0] + db[0, 0:1, :] * s_after[...]
    p = pre[...]
    sig_p = jax.nn.sigmoid(p)
    act = p * sig_p
    weights = pk2[...]
    end_state = nn(weights, e_end[...]) * nn(bc[:, :128], after_.astype(B16))
    gsc_ = gsc[...] + end_state
    grad = gs[...]
    end_terms = scaled[...].astype(F32) * end_state
    carry = nn(weights[Q - 16 :], e_enter[...])[15:16, :]
    closing = jnp.sum(end_terms, axis=0, keepdims=True) + carry * jnp.sum(
        after_ * entering, axis=0, keepdims=True
    )
    closing = two_dot(jnp.broadcast_to(closing, (8, closing.shape[1])), hmap[...])[0:1, :]
    grad_cums = rc[...] + two_dot(grad * inter[...] - end_terms, hmap[...])
    grad_cums = grad_cums + jnp.where(iota((Q, 128), 0) == Q - 1, closing, 0.0)
    high, low = split(grad_cums)
    grad_decay = tn(tri[...], high) + tn(tri[...], low.astype(B16))
    drive = hp[1:2, :] * grad_decay
    raw = (nn((gsc_ * act).astype(B16), hmap[...]) - drive) * pk[...]
    lane = iota((Q, 128), 1)
    step_o[...] = jnp.where(lane // 8 == SIG, raw, 0.0).astype(B16)

    @pl.when(i == 0)
    def _():
        small_o[...] = jnp.zeros_like(small_o)

    small_o[0:1, :] += jnp.sum(raw, axis=0, keepdims=True)
    small_o[1:2, :] -= jnp.sum(drive * pk[...], axis=0, keepdims=True)
    gp = (nn(weights, e_step[...]) * gsc_ + vec[0:1, :] * grad) * (
        sig_p * (1.0 + p * (1.0 - sig_p))
    )
    conv_back(
        i, count, boundary(starts, chunk_base(place, count, i)), gp, tok[...], taps[...],
        vals[...], hv[...], ext, mext, shift, gv_o, sums_o, rim_o,
    )


def mix_kernel(n, gnorm, w_out, *mixes):
    mixed = nn(gnorm[...], w_out[...]).astype(B16)
    for k in range(n):

        @pl.when(pl.program_id(0) == k)
        def _(k=k):
            mixes[k][...] = mixed


def gate_grads_kernel(place, gnorm, normed, gate16, cot, keep_o, send_o):
    r = pl.program_id(0)
    core = lax.rem(place[1], 2)
    inner = gate16.shape[1]
    left = tn(normed[...], gate16[...]).astype(B16)
    right = tn(gnorm[...], cot[...]).astype(B16)

    @pl.when(r == core)
    def _():
        keep_o[:, 0:inner] = left
        keep_o[:, inner:] = right

    @pl.when(r != core)
    def _():
        send_o[:, 0:inner] = left
        send_o[:, inner:] = right


def inner_grads_kernel(
    place, gv, gv_all, rim, hn, gate16, step16, normed, w_in, w_gate, w_s, part_o, keep_o, send_o
):
    r = pl.program_id(0)
    core = lax.rem(place[1], 2)
    part_o[...] = nt(gv[...], w_in[...]) + nt(gate16[...], w_gate[...]) + nt(step16[...], w_s[...])
    grads = (tn(normed[...], gv_all[...]) + tn(hn[...], rim[...].astype(B16))).astype(B16)

    @pl.when(r == core)
    def _():
        keep_o[...] = grads

    @pl.when(r != core)
    def _():
        send_o[...] = grads


def bcoef_grads_kernel(count, n, pack_view, tail_view, place, *refs):
    packs = [pack_view(ref, pl.program_id(0), (place,)) for ref in refs[:n]]
    tails = [tail_view(ref, 0, (place,)) for ref in refs[:n]]
    (
        rim_i, hn, part, normed, w_bt, w_in, step16, gain, csum_b, csum_i, ssum, nsums,
    ) = refs[n : n + 12]
    parts = refs[n + 12 : 2 * n + 12]
    keep_o, send_o, small_o, local_o, acc, gsum = refs[2 * n + 12 :]
    i = pl.program_id(0)
    span, d = w_bt.shape
    inner = w_in.shape[1]

    @pl.when(i == 0)
    def _():
        rim16 = total(tails)[0:8, :span].astype(B16)
        edge = nn(rim16, w_bt[...]) + nt(rim_i[...].astype(B16), w_in[...])
        small_o[3:8, :] = edge[3:8, :]
        gsum[...] = jnp.sum(edge * hn[...].astype(F32), axis=0, keepdims=True)
        acc[...] = tn(jnp.concatenate([rim16, jnp.zeros((8, span), B16)], axis=1), hn[...])

    packed = total(packs)
    v16 = jnp.concatenate([packed[:, :span], packed[:, span:]], axis=0).astype(B16)
    sums = part[...] + nn(v16, w_bt[...])
    for k in range(n):

        @pl.when(i == k)
        def _(k=k):
            parts[k][...] = sums.astype(B16)

    x16 = normed[...]
    gsum[...] += jnp.sum(sums * x16.astype(F32), axis=0, keepdims=True)
    acc[...] += tn(jnp.concatenate([v16, step16[:, :span]], axis=1), x16)

    @pl.when(i == count - 1)
    def _():
        turned = acc[...].T.astype(B16)
        core = lax.rem(place[1], 2)
        half = d // 2

        @pl.when(core == 0)
        def _():
            keep_o[...] = turned[:half]
            send_o[...] = turned[half:]

        @pl.when(core == 1)
        def _():
            keep_o[...] = turned[half:]
            send_o[...] = turned[:half]

        small_o[0:1, :] = gsum[...] / gain[0:1, :]
        for k in range(3):
            small_o[1:2, k * 256 : (k + 1) * 256] = csum_b[k : k + 1, :]
            local_o[3 + k : 4 + k, 0:inner] = csum_i[2 * k : 2 * k + 1, :]
        for k in range(2):
            small_o[2:3, k * 256 : (k + 1) * 256] = csum_b[3 + k : 4 + k, :]
            local_o[3 + k : 4 + k, inner:] = csum_i[2 * k + 1 : 2 * k + 2, :]
        local_o[5:6, inner:] = nsums[1:2, :]
        local_o[6:7, 0:inner] = nsums[0:1, :]
        local_o[6:7, inner : inner + 128] = ssum[0:1, :]
        local_o[6:7, inner + 128 : inner + 256] = ssum[1:2, :]


def small_kernel(local, *refs):
    *ins, small_o, edge_o = refs
    both = total(ins)
    small_o[0:3, :] = both[0:3, :]
    small_o[3:8, :] = local[3:8, :]
    edge_o[0:3, :] = jnp.zeros((3, both.shape[1]), F32)
    edge_o[3:8, :] = both[3:8, :]


def last_kernel(n, x, cot, gain, edge, *refs):
    parts, mixes, (grad_o, block_o) = refs[:n], refs[n : 2 * n], refs[2 * n :]
    sums = total(parts)
    rows = sums.shape[0]
    sums = jnp.concatenate([sums[: rows - 8], sums[rows - 8 :] + edge[...]], axis=0)
    wide = x[...].astype(F32)
    block_o[...] = (wide + total(mixes)).astype(B16)
    scale = rms_scale(wide)
    scaled = gain[0:1, :] * sums
    dot = jnp.sum(scaled * wide, axis=1, keepdims=True)
    width = wide.shape[1]
    grad_o[...] = (
        cot[...].astype(F32) + scale * scaled - wide * (scale * scale * scale * dot / width)
    )


def add_kernel(a, b, out):
    out[...] = a[...] + b[...]


def ends_kernel(n, heads, place, *refs):
    smalls = refs[:n]
    gain_o, taps_i_o, taps_b_o, bias_i_o, bias_b_o, sbias_o, dlog_o, skip_o, ngain_o = refs[n:]
    sums = total(smalls)
    inner, span = ngain_o.shape[0], bias_b_o.shape[0]
    count, own = 256 // span, gain_o.shape[0]
    for v in range(count):

        @pl.when(place[0] == v)
        def _(v=v):
            gain_o[...] = sums[0:1, v * own : (v + 1) * own].reshape(own)
            low = v * span
            for k in range(4):
                row, at = (1, 256 * k) if k < 3 else (2, 0)
                taps_b_o[k : k + 1, :] = sums[row : row + 1, at + low : at + low + span]
            bias_b_o[...] = sums[2:3, 256 + low : 256 + low + span].reshape(span)

    taps_i_o[0:1, :] = sums[3:4, :inner]
    taps_i_o[1:2, :] = sums[3:4, inner:]
    taps_i_o[2:3, :] = sums[4:5, :inner]
    taps_i_o[3:4, :] = sums[4:5, inner:]
    bias_i_o[...] = sums[5:6, :inner].reshape(inner)
    ngain_o[...] = sums[6:7, :inner].reshape(inner)
    raw_at, decay_at = inner + 8 * SIG, inner + 128 + 8 * STEP
    sbias_o[...] = sums[6:7, raw_at : raw_at + heads].reshape(heads)
    dlog_o[...] = sums[6:7, decay_at : decay_at + heads].reshape(heads)
    hit = iota((8, inner), 1) // (inner // heads) == iota((8, inner), 0)
    rows = jnp.where(hit, sums[5:6, inner:], 0.0)
    column = jnp.sum(rows, axis=1, keepdims=True)
    skip_o[...] = jnp.broadcast_to(column, (8, 128)).T[0:1, 0:heads].reshape(heads)


def halves_kernel(n, place, *refs):
    ins, outs = refs[:6], refs[6:]
    rows = outs[0].shape[0]
    for k in range(n):
        piece = pl.ds(pl.multiple_of(lax.rem(lax.div(place[1], 2) + k, n) * rows, rows), rows)
        at = 0
        for j in range(3):
            mine, theirs = ins[2 * j], ins[2 * j + 1]
            cols = slice(at, at + mine.shape[1])
            at += mine.shape[1]
            outs[k][:, cols] = (
                mine[piece, :].astype(F32) + theirs[piece, :].astype(F32)
            ).astype(B16)


def pieces_kernel(*refs):
    refs[-1][...] = total(refs[:-1]).astype(B16)


def unpack_kernel(n, place, *refs):
    pieces = refs[: 2 * n]
    gate_o, inner_o, bcoef_o, step_o, out_o, late = refs[2 * n :]
    rows = pieces[0].shape[0]
    inner = gate_o.shape[1]
    span = bcoef_o.shape[0]
    heads = step_o.shape[0]
    for side in range(2):
        for k in range(n):
            piece = pieces[side * n + k][...].astype(F32)
            whole_half = lax.rem(lax.div(place[1], 2) - k + n, n)
            core = lax.rem(place[1] + side, 2)
            at = pl.multiple_of(core * (n * rows) + whole_half * rows, rows)
            dst = pl.ds(at, rows)
            gate_o[dst, :] = piece[:, 0:inner]
            inner_o[dst, :] = piece[:, 2 * inner : 3 * inner]
            late[dst, :] = piece[:, 3 * inner :]
            low = pl.ds(pl.multiple_of(whole_half * rows, rows), rows)

            @pl.when(core == 0)
            def _():
                out_o[low, 0:inner] = piece[:, inner : 2 * inner]

            @pl.when(core == 1)
            def _():
                out_o[low, inner:] = piece[:, inner : 2 * inner]

    turned = late[...].T
    bcoef_o[...] = turned[:span, :]
    step_o[...] = turned[span + 8 * SIG : span + 8 * SIG + heads, :]


def shape(dims, dtype=F32):
    return jax.ShapeDtypeStruct(dims, dtype)


def call(kernel, grid, ins, in_specs, outs, out_specs, scratch=(), scalars=(), flops=0):
    size = sum(a.size * a.dtype.itemsize for a in ins) + sum(
        o.size * o.dtype.itemsize for o in outs
    )
    views = list(in_specs) + list(out_specs)

    def body(*refs):
        first = len(scalars)
        step = pl.program_id(0) if grid else 0
        seen = [
            view(ref, step, refs[:first]) if view else ref
            for view, ref in zip(views, refs[first:])
        ]
        kernel(*refs[:first], *seen, *refs[first + len(views) :])

    return pl.pallas_call(
        body,
        out_shape=outs,
        grid_spec=pltpu.PrefetchScalarGridSpec(
            num_scalar_prefetch=len(scalars),
            grid=grid,
            in_specs=[VMEM] * len(ins),
            out_specs=[VMEM] * len(outs),
            scratch_shapes=list(scratch),
        ),
        compiler_params=pltpu.CompilerParams(
            dimension_semantics=("arbitrary",) * len(grid) or None,
            vmem_limit_bytes=LIMIT,
        ),
        cost_estimate=pl.CostEstimate(
            flops=int(flops), bytes_accessed=size, transcendentals=0
        ),
    )(*scalars, *ins)


def ring(value, axis, distance):
    count = lax.axis_size(axis)
    return lax.ppermute(value, axis, [(i, (i + distance) % count) for i in range(count)])


def swap(value, axis, bit):
    count = lax.axis_size(axis)
    return lax.ppermute(value, axis, [(i, i ^ (1 << bit)) for i in range(count)])


def spread(value, axis):
    count = lax.axis_size(axis)
    return [value] + [ring(value, axis, k) for k in range(1, count)]


def reduce_parts(parts, axis):
    return [ring(p, axis, k) if k else p for k, p in enumerate(parts)]


def states(fin, place, reverse):
    rows, inner = fin.shape
    count = lax.axis_size("seq")
    other = swap(fin, "seq", 0)
    keep, both = call(
        functools.partial(pair_kernel, reverse), (), [fin, other], [None] * 2,
        [shape((rows - 8, inner)), shape((rows, inner), B16)], [None] * 2,
        scalars=(place,),
    )
    got = []
    for k in range(1, count // 2):
        if reverse:
            pairs = [(i + 2 * k, i) for i in range(count - 2 * k)]
        else:
            pairs = [(i, i + 2 * k) for i in range(count - 2 * k)]
        got.append(lax.ppermute(both, "seq", pairs))
    return keep, got


def per_device(
    block_in,
    in_gain,
    proj_gate,
    proj_inner,
    proj_bcoef,
    proj_step,
    conv_inner,
    conv_inner_bias,
    conv_bcoef,
    conv_bcoef_bias,
    step_bias,
    decay_log,
    skip_gain,
    norm_gain,
    proj_out,
    out_grad,
    doc_starts,
):
    n_wt, n_seq = lax.axis_size("wt"), lax.axis_size("seq")
    w, seq = lax.axis_index("wt"), lax.axis_index("seq")
    rows_own, d = block_in.shape
    length = rows_own * n_wt
    inner = proj_inner.shape[1]
    heads = step_bias.shape[0]
    span = proj_bcoef.shape[1]
    full = inner + span * n_wt
    width_all = inner * n_wt
    count = length // Q
    pairs = n_seq // 2
    place = jnp.stack([w, seq]).astype(jnp.int32)
    scalars = (place, doc_starts)

    w_bt_own = proj_bcoef.T
    quarter = span // 4
    (early,) = call(
        prep_kernel, (), [w_bt_own, conv_bcoef, conv_bcoef_bias, in_gain], [None] * 4,
        [shape((quarter + 16, d), B16)], [None], scalars=(place,),
    )
    earlies = spread(early, "wt")
    rows = spread(block_in, "wt")
    (bts,) = call(
        stack_kernel, (), earlies, [None] * n_wt, [shape((quarter * n_wt, d), B16)], [None],
    )
    bts_x = swap(bts, "seq", 1)
    bts_y = [swap(b, "seq", 2) for b in (bts, bts_x)]
    tail = block_in[rows_own - 8 :]
    halos = []
    for v in range(n_wt):
        halos.append(
            lax.ppermute(
                tail, ("seq", "wt"),
                [((s - 1) * n_wt + n_wt - 1, s * n_wt + v) for s in range(1, n_seq)],
            )
        )
    cots = spread(out_grad, "wt")

    lanes, chans = np.arange(128), np.arange(inner) // (inner // heads)

    def one_hot(group):
        hit = ((lanes % 64) // 8 == group)[:, None] & ((lanes % 8)[:, None] == chans[None, :])
        return jnp.asarray(hit.astype(np.float32), B16)

    e_step, e_enter, e_end = one_hot(STEP), one_hot(ENTER), one_hot(END)
    hmap = jnp.asarray((chans[:, None] == (lanes % 8)[None, :]).astype(np.float32), B16)
    tri = jnp.asarray((np.arange(Q)[:, None] >= np.arange(Q)[None, :]).astype(np.float32), B16)

    grid = (count,)

    def at_rows(ref, index, rows=Q):
        return ref.at[pl.ds(pl.multiple_of(index * rows, rows), rows), :]

    def by_rows(reverse=False):
        if reverse:
            return lambda ref, i, p: at_rows(ref, count - 1 - i)
        return lambda ref, i, p: at_rows(ref, i)

    def by_turn():
        return lambda ref, i, p: at_rows(ref, lax.rem(i + p[0][0], count))

    def whole(*dims):
        return None

    def by_chunk(*dims, reverse=False):
        if reverse:
            return lambda ref, i, p: ref.at[pl.ds(count - 1 - i, 1)]
        return lambda ref, i, p: ref.at[pl.ds(i, 1)]

    def by_lanes(width, reverse=False):
        def view(ref, i, p):
            index = count - 1 - i if reverse else i
            return ref.at[:, pl.ds(pl.multiple_of(index * width, width), width)]

        return view

    def lead(ref, i, p):
        return ref.at[:, :inner]

    by_cols = by_lanes(Q)
    by_cols_back = by_lanes(Q, True)
    fin_spec, state_spec = whole(144, inner), whole(128, inner)
    e_spec = whole(128, inner)
    states_out = [shape((count, 128, inner)), shape((count, 8, inner)), shape((144, inner), B16)]
    (normed, vals, bvals, pre, bpre, bc, pk, pk2, cumt, scaled, sent, dp, fin, hv, hn, tok,
     docrow, taps, gain, hp, w_s, vec) = call(
        functools.partial(front_kernel, heads, n_wt), grid,
        [*rows, *halos, *earlies, bts, bts_x, *bts_y, proj_inner, proj_step, conv_inner,
         conv_inner_bias, step_bias, decay_log, skip_gain, norm_gain, tri, e_step, e_enter,
         e_end],
        [None] * (3 * n_wt + 16),
        [shape((length, d), B16), shape((length, inner), B16), shape((length, 256), B16),
         shape((length, inner)), shape((length, 256)),
         shape((length, 256), B16), shape((length, 128)), shape((length, 128), B16),
         shape((8, length)), shape((length, inner), B16), *states_out,
         shape((8, full)), shape((8, d), B16), shape((length, 8)), shape((8, length)),
         shape((8, full)), shape((8, d)), shape((8, 128)), shape((d, 128), B16),
         shape((8, inner))],
        [by_rows(), by_rows(), by_rows(), by_rows(), by_rows(), by_rows(),
         by_rows(), by_rows(),
         by_cols, by_rows(), by_chunk(128, inner), by_chunk(8, inner), fin_spec,
         whole(8, full), whole(8, d), by_rows(), by_cols, whole(8, full), whole(8, d),
         None, None, None],
        scratch=[pltpu.VMEM((Q + 8, full), F32), pltpu.VMEM((128, inner), F32),
                 pltpu.VMEM((8, inner), F32), pltpu.VMEM((span * n_wt, d), B16),
                 pltpu.VMEM((Q, d), B16)],
        scalars=scalars, flops=2e9,
    )
    keep, got = states(fin, place, False)
    gate, y = call(
        functools.partial(intra_kernel, heads), grid,
        [normed, proj_gate, pre, bc, pk, cumt, scaled, tok, docrow, vec],
        [by_rows(), whole(d, inner), by_rows(), by_rows(), by_rows(), by_cols,
         by_rows(), by_rows(), by_cols, whole(1, inner)],
        [shape((length, inner)), shape((length, inner))],
        [by_rows(), by_rows()], flops=2e9,
    )
    got_spec = [whole(136, inner)] + [fin_spec] * (pairs - 1)
    ssd, inter, gn, stats, s_in, cot = call(
        functools.partial(join_kernel, n_wt, pairs - 1), grid,
        [y, gate, bc, pk2, sent, dp, keep, *got, *cots, proj_out, vec, e_enter],
        [by_rows(), by_rows(), by_rows(), by_rows(),
         by_chunk(128, inner), by_chunk(8, inner), *got_spec]
        + [whole(Q, d)] * n_wt + [whole(inner, d), whole(1, inner), e_spec],
        [shape((length, inner))] * 3
        + [shape((8, length)), shape((128, inner)), shape((length, d), B16)],
        [by_rows()] * 3 + [by_cols, state_spec, by_rows()],
        scalars=(place,), flops=2e9,
    )
    gnorm, gate16, gs, nsums, sb, db, back_fin = call(
        functools.partial(gate_kernel, n_wt, width_all), grid,
        [ssd, gate, gn, vec, pre, bc, pk2, e_enter, *spread(stats, "wt")],
        [by_rows(True)] * 3
        + [whole(1, inner), by_rows(True), by_rows(True), by_rows(True), e_spec]
        + [by_cols_back] * n_wt,
        [shape((length, inner), B16), shape((length, inner), B16), shape((length, inner)),
         shape((8, inner)), *states_out],
        [by_rows(True)] * 3
        + [whole(8, inner), by_chunk(128, inner, reverse=True), by_chunk(8, inner, reverse=True),
           fin_spec],
        scratch=[pltpu.VMEM((128, inner), F32), pltpu.VMEM((8, inner), F32)],
        flops=1e9,
    )
    keep_b, got_b = states(back_fin, place, True)
    gsc, rc, gbc = call(
        functools.partial(intra_back_kernel, heads), grid,
        [gs, bc, pk, pk2, cumt, scaled, tok, docrow, sent, dp, s_in, e_enter],
        [by_rows(), by_rows(), by_rows(), by_rows(), by_cols, by_rows(),
         by_rows(), by_cols, by_chunk(128, inner), by_chunk(8, inner), state_spec, e_spec],
        [shape((length, inner)), shape((length, 128)), shape((length, 256))],
        [by_rows(), by_rows(), by_rows()],
        scratch=[pltpu.VMEM((Q, Q), B16), pltpu.VMEM((8, Q), F32), pltpu.VMEM((Q, 128), F32)],
        flops=4e9,
    )

    half = d // 2
    d_half = by_lanes(half)
    mixes = call(
        lambda p, *refs: mix_kernel(n_wt, *refs), grid, [gnorm, proj_out],
        [by_turn(), whole(inner, d)], [shape((Q, d), B16)] * n_wt, [whole(Q, d)] * n_wt,
        scalars=(place,), flops=1e9,
    )
    keep_a, send_a = call(
        gate_grads_kernel, (2,), [gnorm, normed, gate16, cot],
        [whole(length, inner), d_half, whole(length, inner), d_half],
        [shape((half, 2 * inner), B16)] * 2, [whole(half, 2 * inner)] * 2,
        scalars=(place,), flops=2e9,
    )
    got_a = swap(send_a, "seq", 0)
    mixes = reduce_parts(mixes, "wt")

    rows_pack = length // 2 + 16
    *packs, csum_b, s_after = call(
        functools.partial(bcoef_back_kernel, count, n_wt, pairs - 1), grid,
        [gbc, bpre, bvals, pk2, scaled, tok, sb, db, taps, hv, e_end,
         keep_b, *got_b],
        [by_rows(True), by_rows(True), by_rows(True), by_rows(True),
         by_rows(True), by_rows(True), by_chunk(128, inner, reverse=True),
         by_chunk(8, inner, reverse=True), whole(8, full), whole(8, full), e_spec, *got_spec],
        [shape((rows_pack, 128), B16)] * n_wt + [shape((8, 256)), shape((128, inner))],
        [whole(rows_pack, 128)] * n_wt + [whole(8, 256), state_spec],
        scratch=[pltpu.VMEM((Q + 8, 256), F32), pltpu.VMEM((Q + 8, 8), F32),
                 pltpu.VMEM((16, 256), F32), pltpu.VMEM((8, 256), F32),
                 pltpu.VMEM((Q, 256), B16), pltpu.VMEM((n_wt, HALF, 128), B16)],
        scalars=scalars, flops=1e9,
    )
    packs = reduce_parts(packs, "wt")
    gv, step16, rim_i, csum_i, ssum = call(
        functools.partial(inner_back_kernel, count), grid,
        [gs, gsc, rc, inter, pre, vals, bc, pk, pk2, scaled, tok, sent, dp, s_in, sb, db,
         s_after, taps, hp, hv, vec, tri, e_step, e_enter, e_end, hmap],
        [by_rows(True), by_rows(True), by_rows(True), by_rows(True),
         by_rows(True), by_rows(True), by_rows(True), by_rows(True),
         by_rows(True), by_rows(True), by_rows(True),
         by_chunk(128, inner, reverse=True), by_chunk(8, inner, reverse=True), state_spec,
         by_chunk(128, inner, reverse=True), by_chunk(8, inner, reverse=True), state_spec,
         lead, whole(8, 128), lead, whole(1, inner), whole(Q, Q), e_spec,
         e_spec, e_spec, whole(inner, 128)],
        [shape((length, inner), B16), shape((length, 128), B16), shape((8, inner)),
         shape((8, inner)), shape((8, 128))],
        [by_rows(True), by_rows(True), whole(8, inner), whole(8, inner),
         whole(8, 128)],
        scratch=[pltpu.VMEM((Q + 8, inner), F32), pltpu.VMEM((Q + 8, 8), F32),
                 pltpu.VMEM((16, inner), F32)],
        scalars=scalars, flops=1e9,
    )
    t_half = lambda: lambda ref, r, p: at_rows(ref, r, length // 2)
    part, keep_i, send_i = call(
        inner_grads_kernel, (2,),
        [gv, gv, rim_i, hn, gate16, step16, normed, proj_inner, proj_gate, w_s],
        [t_half(), whole(length, inner), whole(8, inner),
         d_half, t_half(), t_half(), d_half,
         whole(d, inner), whole(d, inner), whole(d, 128)],
        [shape((length, d)), shape((half, inner), B16), shape((half, inner), B16)],
        [t_half(), whole(half, inner), whole(half, inner)],
        scalars=(place,), flops=2e9,
    )
    got_i = swap(send_i, "seq", 0)
    pack_spec = lambda ref, i, p: at_rows(ref, lax.rem(i + p[0][0], count), HALF)
    tail_spec = lambda ref, i, p: ref.at[length // 2 : length // 2 + 16, :]
    *parts, keep_p, send_p, small, local = call(
        functools.partial(bcoef_grads_kernel, count, n_wt, pack_spec, tail_spec), grid,
        [*packs, rim_i, hn, part, normed, w_bt_own, proj_inner, step16, gain, csum_b,
         csum_i, ssum, nsums],
        [None] * n_wt
        + [whole(8, inner), whole(8, d), by_turn(), by_turn(), whole(span, d),
           whole(d, inner), by_turn(), whole(8, d), whole(8, 256), whole(8, inner),
           whole(8, 128), whole(8, inner)],
        [shape((Q, d), B16)] * n_wt
        + [shape((half, 2 * span), B16)] * 2 + [shape((8, d))] * 2,
        [whole(Q, d)] * n_wt + [whole(half, 2 * span)] * 2 + [whole(8, d)] * 2,
        scratch=[pltpu.VMEM((2 * span, d), F32), pltpu.VMEM((1, d), F32)],
        scalars=(place,), flops=1e9,
    )
    parts = reduce_parts(parts, "wt")
    got_p = swap(send_p, "seq", 0)
    small, edge = call(
        small_kernel, (), [local, *spread(small, "wt")], [None] * (n_wt + 1),
        [shape((8, d))] * 2, [None] * 2,
    )
    edge = lax.ppermute(
        edge, ("seq", "wt"),
        [(s * n_wt + n_wt - 1, (s - 1) * n_wt + n_wt - 1) for s in range(1, n_seq)],
    )
    input_grad, block_out = call(
        functools.partial(last_kernel, n_wt), (),
        [block_in, out_grad, gain, edge, *parts, *mixes], [None] * (4 + 2 * n_wt),
        [shape((rows_own, d)), shape((rows_own, d), B16)], [None] * 2,
    )

    def pair_ring(value, k):
        return lax.ppermute(
            value, "seq", [(i, (i + 2 * k) % n_seq) for i in range(n_seq)]
        )

    wide = 3 * inner + 2 * span
    piece_rows = half // pairs
    pieces = call(
        functools.partial(halves_kernel, pairs), (),
        [keep_a, got_a, keep_i, got_i, keep_p, got_p], [None] * 6,
        [shape((piece_rows, wide), B16)] * pairs, [None] * pairs,
        scalars=(place,),
    )
    pieces = [pair_ring(p, k) if k else p for k, p in enumerate(pieces)]
    (piece,) = call(
        pieces_kernel, (), pieces, [None] * pairs, [shape((piece_rows, wide), B16)], [None],
    )
    own = [pair_ring(piece, k) if k else piece for k in range(pairs)]
    theirs = [swap(p, "seq", 0) for p in own]
    g_gate, g_inner, g_bcoef, g_step, g_out = call(
        functools.partial(unpack_kernel, pairs), (1,), [*own, *theirs],
        [whole(piece_rows, wide)] * (2 * pairs),
        [shape((d, inner)), shape((d, inner)), shape((span, d)), shape((heads, d)),
         shape((inner, d))],
        [whole(d, inner), whole(d, inner), whole(span, d), whole(heads, d), whole(inner, d)],
        scratch=[pltpu.VMEM((d, 2 * span), F32)], scalars=(place,),
    )
    (small,) = call(
        add_kernel, (), [small, swap(small, "seq", 0)], [None] * 2,
        [shape((8, d))], [None],
    )
    smalls = [pair_ring(small, k) if k else small for k in range(pairs)]
    (g_gain, g_ci, g_cb, g_cib, g_cbb, g_sbias, g_dlog, g_skip, g_norm) = call(
        functools.partial(ends_kernel, pairs, heads), (), smalls, [None] * pairs,
        [shape((in_gain.shape[0],)), shape((4, inner)), shape((4, span)), shape((inner,)),
         shape((span,)), shape((heads,)), shape((heads,)), shape((heads,)), shape((inner,))],
        [None] * 9, scalars=(place,),
    )
    return (
        block_out,
        input_grad,
        g_gain,
        g_gate,
        g_inner,
        g_bcoef.T,
        g_step.T,
        g_ci,
        g_cb,
        g_cib,
        g_cbb,
        g_sbias,
        g_dlog,
        g_skip,
        g_norm,
        g_out,
    )


def solution(mesh):
    tokens = P(("seq", "wt"), None)
    cols, vec = P(None, "wt"), P("wt")
    return jax.shard_map(
        per_device,
        mesh=mesh,
        in_specs=(
            tokens, vec, cols, cols, cols, cols, cols, vec, cols, vec, vec, vec, vec, vec,
            P("wt", None), tokens, P(),
        ),
        out_specs=(
            tokens, tokens, vec, cols, cols, cols, cols, cols, cols, vec, vec, vec, vec, vec,
            vec, P("wt", None),
        ),
        check_vma=False,
    )
```

profile of v0, /device:TPU:0, one launch (start us, length us, event | category | flops | bytes accessed | tf_op | source)
XLA Modules:
  0.0 236.9 jit_solution(9423299105020563226)
XLA Ops:
  0.6 5.1 %collective-permute-start.2 = (bf16[256,768]{1,0:T(8,128)(2,1)}, bf16[256,768]{1,0:T(8,128)(2,1)S(1)}, u32[]{:S(2)}, u32[]{:S(2)}) collective-permute-start(bf16[256,768]{1,0:T(8,128)(2,1)} %refs_0_.1), channel_id=1, source_target_pairs={{0,3},{1,0},{2,1},{3,2},{4,7},{5,4},{6,5},{7,6},{8,11},{9,8},{10,9... | collective-permute-start | bytes 1179656 | tf_op jit(solution)/shard_map/ppermute | solution.py:820
  16.4 15.9 %collective-permute-done.9.refs_3_.refs_13_ = bf16[32,768]{1,0:T(8,128)(2,1)S(1)} collective-permute-done((bf16[32,768]{1,0:T(8,128)(2,1)S(1)}, bf16[32,768]{1,0:T(8,128)(2,1)S(1)}, u32[]{:S(2)}, u32[]{:S(2)}) %collective-permute-start.9) | collective-permute-done | bytes 49184 | tf_op jit(solution)/shard_map/ppermute | solution.py:820
  32.4 11.4 %collective-permute-start.7 = (bf16[32,768]{1,0:T(8,128)(2,1)S(1)}, bf16[32,768]{1,0:T(8,128)(2,1)S(1)}, u32[]{:S(2)}, u32[]{:S(2)}) collective-permute-start(bf16[32,768]{1,0:T(8,128)(2,1)S(1)} %shard_map.333.refs_0_.refs_10_), channel_id=1, source_target_pairs={{0,1},{1,2},{2,3},{3,0},{4,5},{5,6},{6,7},{7,4},{8,9},{9,10},{10,1... | collective-permute-start | bytes 147464 | tf_op jit(solution)/shard_map/ppermute | solution.py:820
  48.4 7.3 %collective-permute-start.11 = (bf16[64,768]{1,0:T(8,128)(2,1)S(1)}, bf16[64,768]{1,0:T(8,128)(2,1)S(1)}, u32[]{:S(2)}, u32[]{:S(2)}) collective-permute-start(bf16[64,768]{1,0:T(8,128)(2,1)S(1)} %shard_map.334.refs_14_), channel_id=1, source_target_pairs={{0,16},{4,20},{8,24},{12,28},{16,0},{20,4},{24,8},{28,12},{1,17},{... | collective-permute-start | bytes 294920 | tf_op jit(solution)/shard_map/ppermute | solution.py:825
  71.8 10.2 %shard_map.335 = (bf16[1024,768]{1,0:T(8,128)(2,1)S(1)}, bf16[1024,384]{1,0:T(8,128)(2,1)S(1)}, bf16[1024,256]{1,0:T(8,128)(2,1)S(1)}, f32[1024,384]{1,0:T(8,128...) custom-call(s32[2]{0:T(128)S(1)} %pad_add_fusion.refs_0_, ...), custom_call_target="tpu_custom_call" | custom-call | flops 2000000000 | bytes 12183624 | tf_op jit(solution)/shard_map/pallas_call | solution.py:798
  83.9 3.9 %collective-permute-start.16 = (bf16[144,384]{1,0:T(8,128)(2,1)S(1)}, bf16[144,384]{1,0:T(8,128)(2,1)S(1)}, u32[]{:S(2)}, u32[]{:S(2)}) collective-permute-start(bf16[144,384]{1,0:T(8,128)(2,1)S(1)} %get-tuple-element.127), channel_id=1, source_target_pairs={{0,24},{4,28},{1,25},{5,29},{2,26},{6,30},{3,27},{7,31}} | collective-permute-start | bytes 331784 | tf_op jit(solution)/shard_map/ppermute | solution.py:852
  91.7 3.5 %shard_map.336 = (f32[1024,384]{1,0:T(8,128)S(1)}, f32[1024,384]{1,0:T(8,128)S(1)}) custom-call(bf16[1024,768]{1,0:T(8,128)(2,1)S(1)} %get-tuple-element.111.refs_0_.refs_7_.refs_8_.refs_2_, bf16[768,384]{1,0:T(8,128)(2,1)S(1)} %copy-done.20, f32[1024,384]{1,0:T(8,128)S(1)} %get-tuple-element.112.refs_2_.refs_4_.refs_6_, ...), custom_call_target="tpu_custom_call" | custom-call | flops 2000000000 | bytes 8826880 | tf_op jit(solution)/shard_map/pallas_call | solution.py:798
  95.3 3.8 %shard_map.338 = (f32[1024,384]{1,0:T(8,128)S(1)}, f32[1024,384]{1,0:T(8,128)S(1)}, f32[1024,384]{1,0:T(8,128)S(1)}, f32[8,1024]{1,0:T(8,128)S(1)}, f32[128,384]...) custom-call(s32[2]{0:T(128)S(1)} %pad_add_fusion.refs_0_, f32[1024,384]{1,0:T(8,128)S(1)} %get-tuple-element.120.refs_1_, ...), custom_call_target="tpu_custom_call" | custom-call | flops 2000000000 | bytes 14102528 | tf_op jit(solution)/shard_map/pallas_call | solution.py:798
  99.1 3.0 %collective-permute-start.22 = (f32[8,1024]{1,0:T(8,128)S(1)}, f32[8,1024]{1,0:T(8,128)S(1)}, u32[]{:S(2)}, u32[]{:S(2)}) collective-permute-start(f32[8,1024]{1,0:T(8,128)S(1)} %get-tuple-element.130.refs_8_), channel_id=1, source_target_pairs={{0,3},{1,0},{2,1},{3,2},{4,7},{5,4},{6,5},{7,6},{8,11},{9,8},{10,9... | collective-permute-start | bytes 98312 | tf_op jit(solution)/shard_map/ppermute | solution.py:820
  107.8 3.1 %shard_map.339 = (bf16[1024,384]{1,0:T(8,128)(2,1)S(1)}, bf16[1024,384]{1,0:T(8,128)(2,1)S(1)}, f32[1024,384]{1,0:T(8,128)S(1)}, f32[8,384]{1,0:T(8,128)S(1)}, f...) custom-call(f32[1024,384]{1,0:T(8,128)S(1)} %get-tuple-element.128.refs_0_, ...), custom_call_target="tpu_custom_call" | custom-call | flops 1000000000 | bytes 11423744 | tf_op jit(solution)/shard_map/pallas_call | solution.py:798
  118.9 4.8 %shard_map.340 = (f32[1024,384]{1,0:T(8,128)S(1)}, f32[1024,128]{1,0:T(8,128)S(1)}, f32[1024,256]{1,0:T(8,128)S(1)}) custom-call(f32[1024,384]{1,0:T(8,128)S(1)} %get-tuple-element.131.refs_0_.refs_2_, bf16[1024,256]{1,0:T(8,128)(2,1)S(1)} %get-tuple-element.113.refs_3_.refs_5_.refs_1_.refs_8_, f32[1024,128]{1,0:T(8,128)S(1)} %get-tuple-element.114.refs_4_.refs_2_.refs_9_, ...), custom_call_target="tpu_custom_call" | custom-call | flops 4000000000 | bytes 8044544 | tf_op jit(solution)/shard_map/pallas_call | solution.py:798
  125.2 4.8 %shard_map.342 = (bf16[528,128]{1,0:T(8,128)(2,1)S(1)}, bf16[528,128]{1,0:T(8,128)(2,1)S(1)}, bf16[528,128]{1,0:T(8,128)(2,1)S(1)}, bf16[528,128]{1,0:T(8,128)(2...) custom-call(s32[2]{0:T(128)S(1)} %pad_add_fusion.refs_0_, s32[1]{0:T(128)S(6)} %copy.39.refs_1_, ...), custom_call_target="tpu_custom_call" | custom-call | flops 1000000000 | bytes 5963776 | tf_op jit(solution)/shard_map/pallas_call | solution.py:798
  134.1 8.3 %shard_map.343 = (bf16[1024,384]{1,0:T(8,128)(2,1)S(1)}, bf16[1024,128]{1,0:T(8,128)(2,1)S(1)}, f32[8,384]{1,0:T(8,128)S(1)}, f32[8,384]{1,0:T(8,128)S(1)}, f32[8,128]{1,0:T(8,128)S(1)}) custom-call(s32[2]{0:T(128)S(1)} %pad_add_fusion.refs_0_, s32[1]{0:T(128)S(6)} %copy.39.refs_1_, f32[1024,384]{1,0:T(8,128)S(1)} %get-tuple-element.131.refs_0_.refs_2_, ...), custom_call_target="tpu_custom_call" | custom-call | flops 1000000000 | bytes 13455360 | tf_op jit(solution)/shard_map/pallas_call | solution.py:798
  142.4 4.0 %shard_map.344 = (f32[1024,768]{1,0:T(8,128)S(1)}, bf16[384,384]{1,0:T(8,128)(2,1)S(1)}, bf16[384,384]{1,0:T(8,128)(2,1)S(1)}) custom-call(s32[2]{0:T(128)S(1)} %pad_add_fusion.refs_0_, bf16[1024,384]{1,0:T(8,128)(2,1)S(1)} %get-tuple-element.155.refs_1_.refs_2_, bf16[1024,384]{1,0:T(8,128)(2,1)S(1)} %get-tuple-element.155.refs_1_.refs_2_, ...), custom_call_target="tpu_custom_call" | custom-call | flops 2000000000 | bytes 9330688 | tf_op jit(solution)/shard_map/pallas_call | solution.py:798
  146.4 3.8 %shard_map.345 = (bf16[256,768]{1,0:T(8,128)(2,1)S(1)}, bf16[256,768]{1,0:T(8,128)(2,1)S(1)}, bf16[256,768]{1,0:T(8,128)(2,1)S(1)}, bf16[256,768]{1,0:T(8,128)(2...) custom-call(s32[2]{0:T(128)S(1)} %pad_add_fusion.refs_0_, ...), custom_call_target="tpu_custom_call" | custom-call | flops 1000000000 | bytes 8114176 | tf_op jit(solution)/shard_map/pallas_call | solution.py:798
  157.3 13.7 %collective-permute-done.32.refs_4_ = f32[8,768]{1,0:T(8,128)S(1)} collective-permute-done((f32[8,768]{1,0:T(8,128)S(1)}, f32[8,768]{1,0:T(8,128)S(1)}, u32[]{:S(2)}, u32[]{:S(2)}) %collective-permute-start.32) | collective-permute-done | bytes 24608 | tf_op jit(solution)/shard_map/ppermute | solution.py:820
  171.0 11.3 %collective-permute-start.31 = (f32[8,768]{1,0:T(8,128)S(1)}, f32[8,768]{1,0:T(8,128)S(1)}, u32[]{:S(2)}, u32[]{:S(2)}) collective-permute-start(f32[8,768]{1,0:T(8,128)S(1)} %get-tuple-element.165.refs_1_), channel_id=1, source_target_pairs={{0,2},{1,3},{2,0},{3,1},{4,6},{5,7},{6,4},{7,5},{8,10},{9,11},{10,... | collective-permute-start | bytes 73736 | tf_op jit(solution)/shard_map/ppermute | solution.py:820
  184.1 3.4 %collective-permute-start.39 = (bf16[256,768]{1,0:T(8,128)(2,1)S(1)}, bf16[256,768]{1,0:T(8,128)(2,1)S(1)}, u32[]{:S(2)}, u32[]{:S(2)}) collective-permute-start(bf16[256,768]{1,0:T(8,128)(2,1)S(1)} %get-tuple-element.175), channel_id=1, source_target_pairs={{0,3},{1,0},{2,1},{3,2},{4,7},{5,4},{6,5},{7,6},{8,11},{9,8},{10,9... | collective-permute-start | bytes 1179656 | tf_op jit(solution)/shard_map/ppermute | solution.py:820
  192.7 5.7 %collective-permute-done.30.refs_2_ = f32[8,768]{1,0:T(8,128)S(1)} collective-permute-done((f32[8,768]{1,0:T(8,128)S(1)}, f32[8,768]{1,0:T(8,128)S(1)}, u32[]{:S(2)}, u32[]{:S(2)}) %collective-permute-start.30) | collective-permute-done | bytes 24608 | tf_op jit(solution)/shard_map/ppermute | solution.py:820
  206.6 3.3 %collective-permute-start.43 = (f32[8,768]{1,0:T(8,128)S(1)}, f32[8,768]{1,0:T(8,128)S(1)}, u32[]{:S(2)}, u32[]{:S(2)}) collective-permute-start(f32[8,768]{1,0:T(8,128)S(1)} %shard_map.349.refs_1_), channel_id=1, source_target_pairs={{0,24},{4,28},{8,0},{12,4},{16,8},{20,12},{24,16},{28,20},{1,25},{... | collective-permute-start | bytes 73736 | tf_op jit(solution)/shard_map/ppermute | solution.py:1126
  211.5 3.2 %collective-permute-start.52 = (bf16[96,1280]{1,0:T(8,128)(2,1)S(1)}, bf16[96,1280]{1,0:T(8,128)(2,1)S(1)}, u32[]{:S(2)}, u32[]{:S(2)}) collective-permute-start(bf16[96,1280]{1,0:T(8,128)(2,1)S(1)} %shard_map.353.refs_1_), channel_id=1, source_target_pairs={{0,24},{4,28},{8,0},{12,4},{16,8},{20,12},{24,16},{28,20},{1,25},{... | collective-permute-start | bytes 737288 | tf_op jit(solution)/shard_map/ppermute | solution.py:1126
  215.3 5.3 %collective-permute-start.36 = (bf16[256,768]{1,0:T(8,128)(2,1)S(1)}, bf16[256,768]{1,0:T(8,128)(2,1)S(1)}, u32[]{:S(2)}, u32[]{:S(2)}) collective-permute-start(bf16[256,768]{1,0:T(8,128)(2,1)S(1)} %get-tuple-element.170), channel_id=1, source_target_pairs={{0,3},{1,0},{2,1},{3,2},{4,7},{5,4},{6,5},{7,6},{8,11},{9,8},{10,9... | collective-permute-start | bytes 1179656 | tf_op jit(solution)/shard_map/ppermute | solution.py:820
  220.6 5.9 %collective-permute-done.35.refs_6_ = bf16[256,768]{1,0:T(8,128)(2,1)S(1)} collective-permute-done((bf16[256,768]{1,0:T(8,128)(2,1)S(1)}, bf16[256,768]{1,0:T(8,128)(2,1)S(1)}, u32[]{:S(2)}, u32[]{:S(2)}) %collective-permute-start.35) | collective-permute-done | bytes 393248 | tf_op jit(solution)/shard_map/ppermute | solution.py:820
  228.9 3.7 %collective-permute-done.36.refs_7_ = bf16[256,768]{1,0:T(8,128)(2,1)S(1)} collective-permute-done((bf16[256,768]{1,0:T(8,128)(2,1)S(1)}, bf16[256,768]{1,0:T(8,128)(2,1)S(1)}, u32[]{:S(2)}, u32[]{:S(2)}) %collective-permute-start.36) | collective-permute-done | bytes 393248 | tf_op jit(solution)/shard_map/ppermute | solution.py:820
  (169 shorter events, 86.5 us)
Async XLA Ops:
  0.6 60.4 %collective-permute-start.2 = (bf16[256,768]{1,0:T(8,128)(2,1)}, bf16[256,768]{1,0:T(8,128)(2,1)S(1)}, u32[]{:S(2)}, u32[]{:S(2)}) collective-permute-start(bf16[256,768]{1,0:T(8,128)(2,1)} %refs_0_.1), channel_id=1, source_target_pairs={{0,3},{1,0},{2,1},{3,2},{4,7},{5,4},{6,5},{7,6},{8,11},{9,8},{10,9... | collective-permute-start | bytes 1179656 | tf_op jit(solution)/shard_map/ppermute | solution.py:820
  5.8 56.3 %collective-permute-start.1 = (bf16[256,768]{1,0:T(8,128)(2,1)}, bf16[256,768]{1,0:T(8,128)(2,1)S(1)}, u32[]{:S(2)}, u32[]{:S(2)}) collective-permute-start(bf16[256,768]{1,0:T(8,128)(2,1)} %refs_0_.1), channel_id=1, source_target_pairs={{0,2},{1,3},{2,0},{3,1},{4,6},{5,7},{6,4},{7,5},{8,10},{9,11},{10,... | collective-permute-start | bytes 1179656 | tf_op jit(solution)/shard_map/ppermute | solution.py:820
  5.8 56.3 %collective-permute-start = (bf16[256,768]{1,0:T(8,128)(2,1)}, bf16[256,768]{1,0:T(8,128)(2,1)S(1)}, u32[]{:S(2)}, u32[]{:S(2)}) collective-permute-start(bf16[256,768]{1,0:T(8,128)(2,1)} %refs_0_.1), channel_id=1, source_target_pairs={{0,1},{1,2},{2,3},{3,0},{4,5},{5,6},{6,7},{7,4},{8,9},{9,10},{10,1... | collective-permute-start | bytes 1179656 | tf_op jit(solution)/shard_map/ppermute | solution.py:820
  10.4 22.0 %collective-permute-start.9 = (bf16[32,768]{1,0:T(8,128)(2,1)S(1)}, bf16[32,768]{1,0:T(8,128)(2,1)S(1)}, u32[]{:S(2)}, u32[]{:S(2)}) collective-permute-start(bf16[32,768]{1,0:T(8,128)(2,1)S(1)} %shard_map.333.refs_0_.refs_10_), channel_id=1, source_target_pairs={{0,3},{1,0},{2,1},{3,2},{4,7},{5,4},{6,5},{7,6},{8,11},{9,8},{10,9... | collective-permute-start | bytes 147464 | tf_op jit(solution)/shard_map/ppermute | solution.py:820
  15.2 28.5 %collective-permute-start.8 = (bf16[32,768]{1,0:T(8,128)(2,1)S(1)}, bf16[32,768]{1,0:T(8,128)(2,1)S(1)}, u32[]{:S(2)}, u32[]{:S(2)}) collective-permute-start(bf16[32,768]{1,0:T(8,128)(2,1)S(1)} %shard_map.333.refs_0_.refs_10_), channel_id=1, source_target_pairs={{0,2},{1,3},{2,0},{3,1},{4,6},{5,7},{6,4},{7,5},{8,10},{9,11},{10,... | collective-permute-start | bytes 147464 | tf_op jit(solution)/shard_map/ppermute | solution.py:820
  32.4 13.2 %collective-permute-start.7 = (bf16[32,768]{1,0:T(8,128)(2,1)S(1)}, bf16[32,768]{1,0:T(8,128)(2,1)S(1)}, u32[]{:S(2)}, u32[]{:S(2)}) collective-permute-start(bf16[32,768]{1,0:T(8,128)(2,1)S(1)} %shard_map.333.refs_0_.refs_10_), channel_id=1, source_target_pairs={{0,1},{1,2},{2,3},{3,0},{4,5},{5,6},{6,7},{7,4},{8,9},{9,10},{10,1... | collective-permute-start | bytes 147464 | tf_op jit(solution)/shard_map/ppermute | solution.py:820
  58.3 30.8 %collective-permute-start.19 = (bf16[256,768]{1,0:T(8,128)(2,1)}, bf16[256,768]{1,0:T(8,128)(2,1)S(1)}, u32[]{:S(2)}, u32[]{:S(2)}) collective-permute-start(bf16[256,768]{1,0:T(8,128)(2,1)} %refs_1_.6), channel_id=1, source_target_pairs={{0,3},{1,0},{2,1},{3,2},{4,7},{5,4},{6,5},{7,6},{8,11},{9,8},{10,9... | collective-permute-start | bytes 1179656 | tf_op jit(solution)/shard_map/ppermute | solution.py:820
  60.4 34.8 %collective-permute-start.18 = (bf16[256,768]{1,0:T(8,128)(2,1)}, bf16[256,768]{1,0:T(8,128)(2,1)S(1)}, u32[]{:S(2)}, u32[]{:S(2)}) collective-permute-start(bf16[256,768]{1,0:T(8,128)(2,1)} %refs_1_.6), channel_id=1, source_target_pairs={{0,2},{1,3},{2,0},{3,1},{4,6},{5,7},{6,4},{7,5},{8,10},{9,11},{10,... | collective-permute-start | bytes 1179656 | tf_op jit(solution)/shard_map/ppermute | solution.py:820
  61.0 34.2 %collective-permute-start.17 = (bf16[256,768]{1,0:T(8,128)(2,1)}, bf16[256,768]{1,0:T(8,128)(2,1)S(1)}, u32[]{:S(2)}, u32[]{:S(2)}) collective-permute-start(bf16[256,768]{1,0:T(8,128)(2,1)} %refs_1_.6), channel_id=1, source_target_pairs={{0,1},{1,2},{2,3},{3,0},{4,5},{5,6},{6,7},{7,4},{8,9},{9,10},{10,1... | collective-permute-start | bytes 1179656 | tf_op jit(solution)/shard_map/ppermute | solution.py:820
  113.8 76.1 %collective-permute-start.44 = (bf16[384,768]{1,0:T(8,128)(2,1)S(1)}, bf16[384,768]{1,0:T(8,128)(2,1)S(1)}, u32[]{:S(2)}, u32[]{:S(2)}) collective-permute-start(bf16[384,768]{1,0:T(8,128)(2,1)S(1)} %get-tuple-element.182), channel_id=1, source_target_pairs={{0,4},{4,0},{8,12},{12,8},{16,20},{20,16},{24,28},{28,24},{1,5},{5... | collective-permute-start | bytes 1769480 | tf_op jit(solution)/shard_map/ppermute | solution.py:825
  130.0 16.4 %collective-permute-start.27 = (bf16[528,128]{1,0:T(8,128)(2,1)S(1)}, bf16[528,128]{1,0:T(8,128)(2,1)S(1)}, u32[]{:S(2)}, u32[]{:S(2)}) collective-permute-start(bf16[528,128]{1,0:T(8,128)(2,1)S(1)} %get-tuple-element.144), channel_id=1, source_target_pairs={{0,1},{1,2},{2,3},{3,0},{4,5},{5,6},{6,7},{7,4},{8,9},{9,10},{10,1... | collective-permute-start | bytes 405512 | tf_op jit(solution)/shard_map/ppermute | solution.py:820
  130.2 16.2 %collective-permute-start.28 = (bf16[528,128]{1,0:T(8,128)(2,1)S(1)}, bf16[528,128]{1,0:T(8,128)(2,1)S(1)}, u32[]{:S(2)}, u32[]{:S(2)}) collective-permute-start(bf16[528,128]{1,0:T(8,128)(2,1)S(1)} %get-tuple-element.145), channel_id=1, source_target_pairs={{0,2},{1,3},{2,0},{3,1},{4,6},{5,7},{6,4},{7,5},{8,10},{9,11},{10,... | collective-permute-start | bytes 405512 | tf_op jit(solution)/shard_map/ppermute | solution.py:820
  131.7 14.7 %collective-permute-start.29 = (bf16[528,128]{1,0:T(8,128)(2,1)S(1)}, bf16[528,128]{1,0:T(8,128)(2,1)S(1)}, u32[]{:S(2)}, u32[]{:S(2)}) collective-permute-start(bf16[528,128]{1,0:T(8,128)(2,1)S(1)} %get-tuple-element.146), channel_id=1, source_target_pairs={{0,3},{1,0},{2,1},{3,2},{4,7},{5,4},{6,5},{7,6},{8,11},{9,8},{10,9... | collective-permute-start | bytes 405512 | tf_op jit(solution)/shard_map/ppermute | solution.py:820
  150.2 37.2 %collective-permute-start.46 = (bf16[384,128]{1,0:T(8,128)(2,1)S(1)}, bf16[384,128]{1,0:T(8,128)(2,1)S(1)}, u32[]{:S(2)}, u32[]{:S(2)}) collective-permute-start(bf16[384,128]{1,0:T(8,128)(2,1)S(1)} %get-tuple-element.186), channel_id=1, source_target_pairs={{0,4},{4,0},{8,12},{12,8},{16,20},{20,16},{24,28},{28,24},{1,5},{5... | collective-permute-start | bytes 294920 | tf_op jit(solution)/shard_map/ppermute | solution.py:825
  152.5 47.8 %collective-permute-start.37 = (bf16[256,768]{1,0:T(8,128)(2,1)S(1)}, bf16[256,768]{1,0:T(8,128)(2,1)S(1)}, u32[]{:S(2)}, u32[]{:S(2)}) collective-permute-start(bf16[256,768]{1,0:T(8,128)(2,1)S(1)} %get-tuple-element.173), channel_id=1, source_target_pairs={{0,1},{1,2},{2,3},{3,0},{4,5},{5,6},{6,7},{7,4},{8,9},{9,10},{10,1... | collective-permute-start | bytes 1179656 | tf_op jit(solution)/shard_map/ppermute | solution.py:820
  152.9 49.4 %collective-permute-start.38 = (bf16[256,768]{1,0:T(8,128)(2,1)S(1)}, bf16[256,768]{1,0:T(8,128)(2,1)S(1)}, u32[]{:S(2)}, u32[]{:S(2)}) collective-permute-start(bf16[256,768]{1,0:T(8,128)(2,1)S(1)} %get-tuple-element.174), channel_id=1, source_target_pairs={{0,2},{1,3},{2,0},{3,1},{4,6},{5,7},{6,4},{7,5},{8,10},{9,11},{10,... | collective-permute-start | bytes 1179656 | tf_op jit(solution)/shard_map/ppermute | solution.py:820
  154.5 16.5 %collective-permute-start.32 = (f32[8,768]{1,0:T(8,128)S(1)}, f32[8,768]{1,0:T(8,128)S(1)}, u32[]{:S(2)}, u32[]{:S(2)}) collective-permute-start(f32[8,768]{1,0:T(8,128)S(1)} %get-tuple-element.165.refs_1_), channel_id=1, source_target_pairs={{0,3},{1,0},{2,1},{3,2},{4,7},{5,4},{6,5},{7,6},{8,11},{9,8},{10,9... | collective-permute-start | bytes 73736 | tf_op jit(solution)/shard_map/ppermute | solution.py:820
  171.0 13.1 %collective-permute-start.31 = (f32[8,768]{1,0:T(8,128)S(1)}, f32[8,768]{1,0:T(8,128)S(1)}, u32[]{:S(2)}, u32[]{:S(2)}) collective-permute-start(f32[8,768]{1,0:T(8,128)S(1)} %get-tuple-element.165.refs_1_), channel_id=1, source_target_pairs={{0,2},{1,3},{2,0},{3,1},{4,6},{5,7},{6,4},{7,5},{8,10},{9,11},{10,... | collective-permute-start | bytes 73736 | tf_op jit(solution)/shard_map/ppermute | solution.py:820
  184.1 19.1 %collective-permute-start.39 = (bf16[256,768]{1,0:T(8,128)(2,1)S(1)}, bf16[256,768]{1,0:T(8,128)(2,1)S(1)}, u32[]{:S(2)}, u32[]{:S(2)}) collective-permute-start(bf16[256,768]{1,0:T(8,128)(2,1)S(1)} %get-tuple-element.175), channel_id=1, source_target_pairs={{0,3},{1,0},{2,1},{3,2},{4,7},{5,4},{6,5},{7,6},{8,11},{9,8},{10,9... | collective-permute-start | bytes 1179656 | tf_op jit(solution)/shard_map/ppermute | solution.py:820
  189.9 25.4 %collective-permute-start.34 = (bf16[256,768]{1,0:T(8,128)(2,1)S(1)}, bf16[256,768]{1,0:T(8,128)(2,1)S(1)}, u32[]{:S(2)}, u32[]{:S(2)}) collective-permute-start(bf16[256,768]{1,0:T(8,128)(2,1)S(1)} %get-tuple-element.168), channel_id=1, source_target_pairs={{0,1},{1,2},{2,3},{3,0},{4,5},{5,6},{6,7},{7,4},{8,9},{9,10},{10,1... | collective-permute-start | bytes 1179656 | tf_op jit(solution)/shard_map/ppermute | solution.py:820
  205.2 21.4 %collective-permute-start.35 = (bf16[256,768]{1,0:T(8,128)(2,1)S(1)}, bf16[256,768]{1,0:T(8,128)(2,1)S(1)}, u32[]{:S(2)}, u32[]{:S(2)}) collective-permute-start(bf16[256,768]{1,0:T(8,128)(2,1)S(1)} %get-tuple-element.169), channel_id=1, source_target_pairs={{0,2},{1,3},{2,0},{3,1},{4,6},{5,7},{6,4},{7,5},{8,10},{9,11},{10,... | collective-permute-start | bytes 1179656 | tf_op jit(solution)/shard_map/ppermute | solution.py:820
  211.5 15.0 %collective-permute-start.52 = (bf16[96,1280]{1,0:T(8,128)(2,1)S(1)}, bf16[96,1280]{1,0:T(8,128)(2,1)S(1)}, u32[]{:S(2)}, u32[]{:S(2)}) collective-permute-start(bf16[96,1280]{1,0:T(8,128)(2,1)S(1)} %shard_map.353.refs_1_), channel_id=1, source_target_pairs={{0,24},{4,28},{8,0},{12,4},{16,8},{20,12},{24,16},{28,20},{1,25},{... | collective-permute-start | bytes 737288 | tf_op jit(solution)/shard_map/ppermute | solution.py:1126
  214.7 12.3 %collective-permute-start.51 = (bf16[96,1280]{1,0:T(8,128)(2,1)S(1)}, bf16[96,1280]{1,0:T(8,128)(2,1)S(1)}, u32[]{:S(2)}, u32[]{:S(2)}) collective-permute-start(bf16[96,1280]{1,0:T(8,128)(2,1)S(1)} %shard_map.353.refs_1_), channel_id=1, source_target_pairs={{0,16},{4,20},{8,24},{12,28},{16,0},{20,4},{24,8},{28,12},{1,17},{... | collective-permute-start | bytes 737288 | tf_op jit(solution)/shard_map/ppermute | solution.py:1126
  215.3 17.2 %collective-permute-start.36 = (bf16[256,768]{1,0:T(8,128)(2,1)S(1)}, bf16[256,768]{1,0:T(8,128)(2,1)S(1)}, u32[]{:S(2)}, u32[]{:S(2)}) collective-permute-start(bf16[256,768]{1,0:T(8,128)(2,1)S(1)} %get-tuple-element.170), channel_id=1, source_target_pairs={{0,3},{1,0},{2,1},{3,2},{4,7},{5,4},{6,5},{7,6},{8,11},{9,8},{10,9... | collective-permute-start | bytes 1179656 | tf_op jit(solution)/shard_map/ppermute | solution.py:820
  (60 other events, 324.7 us)
where the time goes:
time: 240 us; the launch traced here: 237 us
  starting transfers between devices  101 us (42%)
  waiting for transfers between devices  60.5 us (25%)
  Pallas kernels  59.7 us (25%)
  local copies, waits for them, and re-layouts  14.2 us (6%)
    ppermute x24, starting transfers between devices, ring(): lax.ppermute(value, axis, [(i, (i + distance) % count) for i in range(cou...  61.4 us
    pallas_call x22, Pallas kernels, call(): pl.pallas_call(body, out_shape=outs, grid_spec=pltpu.PrefetchScalarGridSp...  59.7 us
    ppermute x24, waiting for transfers between devices, ring(): lax.ppermute(value, axis, [(i, (i + distance) % count) for i in range(cou...  51.6 us
    unnamed x55, local copies, waits for them, and re-layouts  13.5 us
    ppermute x9, starting transfers between devices, pair_ring(): lax.ppermute(value, 'seq', [(i, (i + 2 * k) % n_seq) for i in range(n_seq)])  13 us
    ppermute x6, starting transfers between devices, states(): got.append(lax.ppermute(both, 'seq', pairs))  11.5 us
    ppermute x13, starting transfers between devices, swap(): return lax.ppermute(value, axis, [(i, i ^ 1 << bit) for i in range(count)])  11.4 us
    ppermute x13, waiting for transfers between devices, swap(): return lax.ppermute(value, axis, [(i, i ^ 1 << bit) for i in range(count)])  7.13 us
  transfers between devices with their start and end apart: 57, of which 16 were waited for; matrix products, arithmetic and copies ran while one was open for 1% of the time, Pallas kernels for 21%

commit v1 on v0

--- a/solution.py
+++ b/solution.py
@@ -9,6 +9,7 @@
 from jax.sharding import PartitionSpec as P
 
 VMEM = pl.BlockSpec(memory_space=pltpu.VMEM)
+HBM = pl.BlockSpec(memory_space=pltpu.HBM)
 LIMIT = 16 << 20
 Q = 256
 HALF = Q // 2
@@ -303,7 +304,8 @@
 
 def join_kernel(n, m, place, y, gate, bc, pk2, sent, dp, keep, *refs):
     others, cots = refs[:m], refs[m : m + n]
-    (w_out, vec, e_enter, ssd_o, inter_o, gn_o, stats_o, s_in, cot_o) = refs[m + n :]
+    w_out, vec, e_enter, ssd_o, inter_o, gn_o, stats_o, s_in, cot_o = refs[m + n : m + n + 9]
+    mixes = refs[m + n + 9 :]
     c = pl.program_id(0)
     inner = y.shape[1]
 
@@ -323,6 +325,13 @@
     ssd = y[...] + inter
     ssd_o[...] = ssd
     gated = ssd * silu(gate[...])
+    mixed = nn((gated * vec[1:2, :]).astype(B16), w_out[...]).astype(B16)
+    for k in range(n):
+
+        @pl.when(lax.rem(c - place[0] + n, n) == k)
+        def _(k=k):
+            mixes[k][...] = mixed
+
     gn = nt(cot_o[...], w_out[...])
     gn_o[...] = gn
     lane = iota((inner, 128), 1)
@@ -335,7 +344,7 @@
 
 def gate_kernel(n, width_all, ssd, gate, gn, vec, pre, bc, pk2, e_enter, *refs):
     stats = refs[:n]
-    norm_o, gate_o, gs_o, sums_o, sb_o, db_o, fin_o, state, prod = refs[n:]
+    norm_o, gate_o, gs_o, sums_o, sb_o, db_o, fin_o, rms_o, state, prod = refs[n:]
     i = pl.program_id(0)
 
     @pl.when(i == 0)
@@ -349,6 +358,7 @@
     pull = rms * rms * rms * st[1:2, :] / width_all
     st = jnp.concatenate([rms, pull, jnp.zeros((126, Q), F32)], axis=0).T
     rms, pull = st[:, 0:1], st[:, 1:2]
+    rms_o[...] = st[:, 0:8]
     g = gate[...]
     sig = jax.nn.sigmoid(g)
     s = ssd[...]
@@ -558,15 +568,6 @@
     )
 
 
-def mix_kernel(n, gnorm, w_out, *mixes):
-    mixed = nn(gnorm[...], w_out[...]).astype(B16)
-    for k in range(n):
-
-        @pl.when(pl.program_id(0) == k)
-        def _(k=k):
-            mixes[k][...] = mixed
-
-
 def gate_grads_kernel(place, gnorm, normed, gate16, cot, keep_o, send_o):
     r = pl.program_id(0)
     core = lax.rem(place[1], 2)
@@ -673,13 +674,14 @@
     edge_o[3:8, :] = both[3:8, :]
 
 
-def last_kernel(n, x, cot, gain, edge, *refs):
+def last_kernel(n, place, x, cot, gain, edge, rms, *refs):
     parts, mixes, (grad_o, block_o) = refs[:n], refs[n : 2 * n], refs[2 * n :]
     sums = total(parts)
     rows = sums.shape[0]
     sums = jnp.concatenate([sums[: rows - 8], sums[rows - 8 :] + edge[...]], axis=0)
     wide = x[...].astype(F32)
-    block_o[...] = (wide + total(mixes)).astype(B16)
+    own = rms[pl.ds(pl.multiple_of(place[0] * rows, rows), rows), 0:1]
+    block_o[...] = (wide + own * total(mixes)).astype(B16)
     scale = rms_scale(wide)
     scaled = gain[0:1, :] * sums
     dot = jnp.sum(scaled * wide, axis=1, keepdims=True)
@@ -780,15 +782,48 @@
     return jax.ShapeDtypeStruct(dims, dtype)
 
 
-def call(kernel, grid, ins, in_specs, outs, out_specs, scratch=(), scalars=(), flops=0):
+def call(
+    kernel, grid, ins, in_specs, outs, out_specs, scratch=(), scalars=(), flops=0,
+    fetch=(),
+):
     size = sum(a.size * a.dtype.itemsize for a in ins) + sum(
         o.size * o.dtype.itemsize for o in outs
     )
     views = list(in_specs) + list(out_specs)
+    ins = [
+        pltpu.with_memory_space_constraint(a, pltpu.HBM) if k in fetch else a
+        for k, a in enumerate(ins)
+    ]
+
+    landing = [pltpu.VMEM(ins[k].shape, ins[k].dtype) for k in fetch]
+    landing += [pltpu.SemaphoreType.DMA((len(fetch),))] if fetch else []
 
     def body(*refs):
         first = len(scalars)
         step = pl.program_id(0) if grid else 0
+        if fetch:
+            refs, local, sems = list(refs[: -len(landing)]), refs[-len(landing) : -1], refs[-1]
+
+            sources = [refs[first + k] for k in fetch]
+
+            def copies():
+                return [
+                    pltpu.make_async_copy(source, local[j], sems.at[j])
+                    for j, source in enumerate(sources)
+                ]
+
+            def bring():
+                for copy in copies():
+                    copy.start()
+                for copy in copies():
+                    copy.wait()
+
+            if grid:
+                pl.when(step == 0)(bring)
+            else:
+                bring()
+            for j, k in enumerate(fetch):
+                refs[first + k] = local[j]
         seen = [
             view(ref, step, refs[:first]) if view else ref
             for view, ref in zip(views, refs[first:])
@@ -801,9 +836,9 @@
         grid_spec=pltpu.PrefetchScalarGridSpec(
             num_scalar_prefetch=len(scalars),
             grid=grid,
-            in_specs=[VMEM] * len(ins),
+            in_specs=[HBM if k in fetch else VMEM for k in range(len(ins))],
             out_specs=[VMEM] * len(outs),
-            scratch_shapes=list(scratch),
+            scratch_shapes=list(scratch) + landing,
         ),
         compiler_params=pltpu.CompilerParams(
             dimension_semantics=("arbitrary",) * len(grid) or None,
@@ -891,6 +926,7 @@
     (early,) = call(
         prep_kernel, (), [w_bt_own, conv_bcoef, conv_bcoef_bias, in_gain], [None] * 4,
         [shape((quarter + 16, d), B16)], [None], scalars=(place,),
+        fetch=tuple(range(4)),
     )
     earlies = spread(early, "wt")
     rows = spread(block_in, "wt")
@@ -979,6 +1015,7 @@
                  pltpu.VMEM((8, inner), F32), pltpu.VMEM((span * n_wt, d), B16),
                  pltpu.VMEM((Q, d), B16)],
         scalars=scalars, flops=2e9,
+        fetch=(0, *range(3 * n_wt + 4, 3 * n_wt + 16)),
     )
     keep, got = states(fin, place, False)
     gate, y = call(
@@ -990,28 +1027,29 @@
         [by_rows(), by_rows()], flops=2e9,
     )
     got_spec = [whole(136, inner)] + [fin_spec] * (pairs - 1)
-    ssd, inter, gn, stats, s_in, cot = call(
+    ssd, inter, gn, stats, s_in, cot, *mixes = call(
         functools.partial(join_kernel, n_wt, pairs - 1), grid,
         [y, gate, bc, pk2, sent, dp, keep, *got, *cots, proj_out, vec, e_enter],
         [by_rows(), by_rows(), by_rows(), by_rows(),
          by_chunk(128, inner), by_chunk(8, inner), *got_spec]
         + [whole(Q, d)] * n_wt + [whole(inner, d), whole(1, inner), e_spec],
         [shape((length, inner))] * 3
-        + [shape((8, length)), shape((128, inner)), shape((length, d), B16)],
-        [by_rows()] * 3 + [by_cols, state_spec, by_rows()],
+        + [shape((8, length)), shape((128, inner)), shape((length, d), B16)]
+        + [shape((Q, d), B16)] * n_wt,
+        [by_rows()] * 3 + [by_cols, state_spec, by_rows()] + [None] * n_wt,
         scalars=(place,), flops=2e9,
     )
-    gnorm, gate16, gs, nsums, sb, db, back_fin = call(
+    gnorm, gate16, gs, nsums, sb, db, back_fin, rms = call(
         functools.partial(gate_kernel, n_wt, width_all), grid,
         [ssd, gate, gn, vec, pre, bc, pk2, e_enter, *spread(stats, "wt")],
         [by_rows(True)] * 3
         + [whole(1, inner), by_rows(True), by_rows(True), by_rows(True), e_spec]
         + [by_cols_back] * n_wt,
         [shape((length, inner), B16), shape((length, inner), B16), shape((length, inner)),
-         shape((8, inner)), *states_out],
+         shape((8, inner)), *states_out, shape((length, 8))],
         [by_rows(True)] * 3
         + [whole(8, inner), by_chunk(128, inner, reverse=True), by_chunk(8, inner, reverse=True),
-           fin_spec],
+           fin_spec, by_rows(True)],
         scratch=[pltpu.VMEM((128, inner), F32), pltpu.VMEM((8, inner), F32)],
         flops=1e9,
     )
@@ -1029,11 +1067,6 @@
 
     half = d // 2
     d_half = by_lanes(half)
-    mixes = call(
-        lambda p, *refs: mix_kernel(n_wt, *refs), grid, [gnorm, proj_out],
-        [by_turn(), whole(inner, d)], [shape((Q, d), B16)] * n_wt, [whole(Q, d)] * n_wt,
-        scalars=(place,), flops=1e9,
-    )
     keep_a, send_a = call(
         gate_grads_kernel, (2,), [gnorm, normed, gate16, cot],
         [whole(length, inner), d_half, whole(length, inner), d_half],
@@ -1118,8 +1151,8 @@
     )
     input_grad, block_out = call(
         functools.partial(last_kernel, n_wt), (),
-        [block_in, out_grad, gain, edge, *parts, *mixes], [None] * (4 + 2 * n_wt),
-        [shape((rows_own, d)), shape((rows_own, d), B16)], [None] * 2,
+        [block_in, out_grad, gain, edge, rms, *parts, *mixes], [None] * (5 + 2 * n_wt),
+        [shape((rows_own, d)), shape((rows_own, d), B16)], [None] * 2, scalars=(place,),
     )
 
     def pair_ring(value, k):

time: 240 us -> 233 us (0.971)
  local copies, waits for them, and re-layouts: 14.2 us -> 2.31 us
  waiting for transfers between devices: 60.5 us -> 69.1 us
  starting transfers between devices: 101 us -> 95.3 us
  Pallas kernels: 59.7 us -> 63.3 us
    ppermute x24, starting transfers between devices: 61.4 us -> 49.4 us  [ring(): lax.ppermute(value, axis, [(i, (i + distance) % count) for i in range(cou...]
    unnamed x55 -> x23, local copies, waits for them, and re-layouts: 13.5 us -> 1.6 us
    ppermute x9, starting transfers between devices: 13 us -> 20.2 us  [pair_ring(): lax.ppermute(value, 'seq', [(i, (i + 2 * k) % n_seq) for i in range(n_seq)])]
    ppermute x24, waiting for transfers between devices: 51.6 us -> 58.5 us  [ring(): lax.ppermute(value, axis, [(i, (i + distance) % count) for i in range(cou...]
    pallas_call x22 -> x21, Pallas kernels: 59.7 us -> 63.3 us  [call(): pl.pallas_call(body, out_shape=outs, grid_spec=pltpu.PrefetchScalarGridSp...]
  transfers between devices with their start and end apart: 57 -> 57, of which waited for: 16 -> 18; matrix products, arithmetic and copies ran while one was open for 1% -> 1% of each run, Pallas kernels for 21% -> 20%
where the time goes in v1:
time: 233 us; the launch traced here: 232 us
  starting transfers between devices  95.3 us (41%)
  waiting for transfers between devices  69.1 us (30%)
  Pallas kernels  63.3 us (27%)
    pallas_call x21, Pallas kernels, call(): pl.pallas_call(body, out_shape=outs, grid_spec=pltpu.PrefetchScalarGridSp...  63.3 us
    ppermute x24, waiting for transfers between devices, ring(): lax.ppermute(value, axis, [(i, (i + distance) % count) for i in range(cou...  58.5 us
    ppermute x24, starting transfers between devices, ring(): lax.ppermute(value, axis, [(i, (i + distance) % count) for i in range(cou...  49.4 us
    ppermute x9, starting transfers between devices, pair_ring(): lax.ppermute(value, 'seq', [(i, (i + 2 * k) % n_seq) for i in range(n_seq)])  20.2 us
    ppermute x6, starting transfers between devices, states(): got.append(lax.ppermute(both, 'seq', pairs))  11.5 us
    ppermute x13, starting transfers between devices, swap(): return lax.ppermute(value, axis, [(i, i ^ 1 << bit) for i in range(count)])  11 us
    ppermute x13, waiting for transfers between devices, swap(): return lax.ppermute(value, axis, [(i, i ^ 1 << bit) for i in range(count)])  6.38 us
  transfers between devices with their start and end apart: 57, of which 18 were waited for; matrix products, arithmetic and copies ran while one was open for 1% of the time, Pallas kernels for 20%

profile of v1, /device:TPU:0, one launch (start us, length us, event | category | flops | bytes accessed | tf_op | source)
XLA Modules:
  0.0 231.9 jit_solution(10934424735592791619)
XLA Ops:
  0.6 5.1 %collective-permute-start.2 = (bf16[256,768]{1,0:T(8,128)(2,1)}, bf16[256,768]{1,0:T(8,128)(2,1)S(1)}, u32[]{:S(2)}, u32[]{:S(2)}) collective-permute-start(bf16[256,768]{1,0:T(8,128)(2,1)} %refs_1_.6), channel_id=1, source_target_pairs={{0,3},{1,0},{2,1},{3,2},{4,7},{5,4},{6,5},{7,6},{8,11},{9,8},{10,9... | collective-permute-start | bytes 1179656 | tf_op jit(solution)/shard_map/ppermute | solution.py:855
  14.5 17.8 %collective-permute-done.9.refs_3_.refs_13_ = bf16[32,768]{1,0:T(8,128)(2,1)S(1)} collective-permute-done((bf16[32,768]{1,0:T(8,128)(2,1)S(1)}, bf16[32,768]{1,0:T(8,128)(2,1)S(1)}, u32[]{:S(2)}, u32[]{:S(2)}) %collective-permute-start.9) | collective-permute-done | bytes 49184 | tf_op jit(solution)/shard_map/ppermute | solution.py:855
  32.4 11.4 %collective-permute-start.7 = (bf16[32,768]{1,0:T(8,128)(2,1)S(1)}, bf16[32,768]{1,0:T(8,128)(2,1)S(1)}, u32[]{:S(2)}, u32[]{:S(2)}) collective-permute-start(bf16[32,768]{1,0:T(8,128)(2,1)S(1)} %shard_map.333.refs_0_.refs_10_), channel_id=1, source_target_pairs={{0,1},{1,2},{2,3},{3,0},{4,5},{5,6},{6,7},{7,4},{8,9},{9,10},{10,1... | collective-permute-start | bytes 147464 | tf_op jit(solution)/shard_map/ppermute | solution.py:855
  48.4 7.3 %collective-permute-start.11 = (bf16[64,768]{1,0:T(8,128)(2,1)S(1)}, bf16[64,768]{1,0:T(8,128)(2,1)S(1)}, u32[]{:S(2)}, u32[]{:S(2)}) collective-permute-start(bf16[64,768]{1,0:T(8,128)(2,1)S(1)} %shard_map.334.refs_14_), channel_id=1, source_target_pairs={{0,16},{4,20},{8,24},{12,28},{16,0},{20,4},{24,8},{28,12},{1,17},{... | collective-permute-start | bytes 294920 | tf_op jit(solution)/shard_map/ppermute | solution.py:860
  62.7 11.8 %shard_map.335 = (bf16[1024,768]{1,0:T(8,128)(2,1)S(1)}, bf16[1024,384]{1,0:T(8,128)(2,1)S(1)}, bf16[1024,256]{1,0:T(8,128)(2,1)S(1)}, f32[1024,384]{1,0:T(8,128...) custom-call(s32[2]{0:T(128)S(1)} %pad_add_fusion.refs_0_, ...), custom_call_target="tpu_custom_call" | custom-call | flops 2000000000 | bytes 12183624 | tf_op jit(solution)/shard_map/pallas_call | solution.py:833
  76.4 3.9 %collective-permute-start.16 = (bf16[144,384]{1,0:T(8,128)(2,1)S(1)}, bf16[144,384]{1,0:T(8,128)(2,1)S(1)}, u32[]{:S(2)}, u32[]{:S(2)}) collective-permute-start(bf16[144,384]{1,0:T(8,128)(2,1)S(1)} %get-tuple-element.128), channel_id=1, source_target_pairs={{0,24},{4,28},{1,25},{5,29},{2,26},{6,30},{3,27},{7,31}} | collective-permute-start | bytes 331784 | tf_op jit(solution)/shard_map/ppermute | solution.py:887
  84.1 3.5 %shard_map.336 = (f32[1024,384]{1,0:T(8,128)S(1)}, f32[1024,384]{1,0:T(8,128)S(1)}) custom-call(bf16[1024,768]{1,0:T(8,128)(2,1)S(1)} %get-tuple-element.112.refs_0_.refs_7_.refs_8_.refs_2_, bf16[768,384]{1,0:T(8,128)(2,1)S(1)} %copy-done.10, f32[1024,384]{1,0:T(8,128)S(1)} %get-tuple-element.113.refs_2_.refs_4_.refs_6_, ...), custom_call_target="tpu_custom_call" | custom-call | flops 2000000000 | bytes 8826880 | tf_op jit(solution)/shard_map/pallas_call | solution.py:833
  91.1 6.5 %shard_map.338 = (f32[1024,384]{1,0:T(8,128)S(1)}, f32[1024,384]{1,0:T(8,128)S(1)}, f32[1024,384]{1,0:T(8,128)S(1)}, f32[8,1024]{1,0:T(8,128)S(1)}, f32[128,384]...) custom-call(s32[2]{0:T(128)S(1)} %pad_add_fusion.refs_0_, ...), custom_call_target="tpu_custom_call" | custom-call | flops 2000000000 | bytes 15675392 | tf_op jit(solution)/shard_map/pallas_call | solution.py:833
  97.7 3.6 %collective-permute-start.21 = (f32[8,1024]{1,0:T(8,128)S(1)}, f32[8,1024]{1,0:T(8,128)S(1)}, u32[]{:S(2)}, u32[]{:S(2)}) collective-permute-start(f32[8,1024]{1,0:T(8,128)S(1)} %get-tuple-element.131.refs_8_), channel_id=1, source_target_pairs={{0,2},{1,3},{2,0},{3,1},{4,6},{5,7},{6,4},{7,5},{8,10},{9,11},{10,... | collective-permute-start | bytes 98312 | tf_op jit(solution)/shard_map/ppermute | solution.py:855
  103.5 3.5 %collective-permute-done.20.refs_9_ = f32[8,1024]{1,0:T(8,128)S(1)} collective-permute-done((f32[8,1024]{1,0:T(8,128)S(1)}, f32[8,1024]{1,0:T(8,128)S(1)}, u32[]{:S(2)}, u32[]{:S(2)}) %collective-permute-start.20) | collective-permute-done | bytes 32800 | tf_op jit(solution)/shard_map/ppermute | solution.py:855
  116.0 4.7 %shard_map.340 = (f32[1024,384]{1,0:T(8,128)S(1)}, f32[1024,128]{1,0:T(8,128)S(1)}, f32[1024,256]{1,0:T(8,128)S(1)}) custom-call(f32[1024,384]{1,0:T(8,128)S(1)} %get-tuple-element.132.refs_0_.refs_2_, bf16[1024,256]{1,0:T(8,128)(2,1)S(1)} %get-tuple-element.114.refs_3_.refs_5_.refs_1_.refs_8_, f32[1024,128]{1,0:T(8,128)S(1)} %get-tuple-element.115.refs_4_.refs_2_.refs_9_, ...), custom_call_target="tpu_custom_call" | custom-call | flops 4000000000 | bytes 8044544 | tf_op jit(solution)/shard_map/pallas_call | solution.py:833
  122.4 4.8 %shard_map.342 = (bf16[528,128]{1,0:T(8,128)(2,1)S(1)}, bf16[528,128]{1,0:T(8,128)(2,1)S(1)}, bf16[528,128]{1,0:T(8,128)(2,1)S(1)}, bf16[528,128]{1,0:T(8,128)(2...) custom-call(s32[2]{0:T(128)S(1)} %pad_add_fusion.refs_0_, s32[1]{0:T(128)S(6)} %copy.39.refs_1_, ...), custom_call_target="tpu_custom_call" | custom-call | flops 1000000000 | bytes 5963776 | tf_op jit(solution)/shard_map/pallas_call | solution.py:833
  131.3 3.4 %collective-permute-start.37 = (bf16[256,768]{1,0:T(8,128)(2,1)S(1)}, bf16[256,768]{1,0:T(8,128)(2,1)S(1)}, u32[]{:S(2)}, u32[]{:S(2)}) collective-permute-start(bf16[256,768]{1,0:T(8,128)(2,1)S(1)} %get-tuple-element.174), channel_id=1, source_target_pairs={{0,1},{1,2},{2,3},{3,0},{4,5},{5,6},{6,7},{7,4},{8,9},{9,10},{10,1... | collective-permute-start | bytes 1179656 | tf_op jit(solution)/shard_map/ppermute | solution.py:855
  134.8 8.3 %shard_map.343 = (bf16[1024,384]{1,0:T(8,128)(2,1)S(1)}, bf16[1024,128]{1,0:T(8,128)(2,1)S(1)}, f32[8,384]{1,0:T(8,128)S(1)}, f32[8,384]{1,0:T(8,128)S(1)}, f32[8,128]{1,0:T(8,128)S(1)}) custom-call(s32[2]{0:T(128)S(1)} %pad_add_fusion.refs_0_, s32[1]{0:T(128)S(6)} %copy.39.refs_1_, f32[1024,384]{1,0:T(8,128)S(1)} %get-tuple-element.132.refs_0_.refs_2_, ...), custom_call_target="tpu_custom_call" | custom-call | flops 1000000000 | bytes 13455360 | tf_op jit(solution)/shard_map/pallas_call | solution.py:833
  145.5 12.1 %collective-permute-done.28.refs_3_ = bf16[528,128]{1,0:T(8,128)(2,1)S(1)} collective-permute-done((bf16[528,128]{1,0:T(8,128)(2,1)S(1)}, bf16[528,128]{1,0:T(8,128)(2,1)S(1)}, u32[]{:S(2)}, u32[]{:S(2)}) %collective-permute-start.28) | collective-permute-done | bytes 135200 | tf_op jit(solution)/shard_map/ppermute | solution.py:855
  157.6 4.0 %shard_map.344 = (f32[1024,768]{1,0:T(8,128)S(1)}, bf16[384,384]{1,0:T(8,128)(2,1)S(1)}, bf16[384,384]{1,0:T(8,128)(2,1)S(1)}) custom-call(s32[2]{0:T(128)S(1)} %pad_add_fusion.refs_0_, bf16[1024,384]{1,0:T(8,128)(2,1)S(1)} %get-tuple-element.156.refs_1_.refs_2_, bf16[1024,384]{1,0:T(8,128)(2,1)S(1)} %get-tuple-element.156.refs_1_.refs_2_, ...), custom_call_target="tpu_custom_call" | custom-call | flops 2000000000 | bytes 9330688 | tf_op jit(solution)/shard_map/pallas_call | solution.py:833
  161.7 6.6 %collective-permute-done.29.refs_4_ = bf16[528,128]{1,0:T(8,128)(2,1)S(1)} collective-permute-done((bf16[528,128]{1,0:T(8,128)(2,1)S(1)}, bf16[528,128]{1,0:T(8,128)(2,1)S(1)}, u32[]{:S(2)}, u32[]{:S(2)}) %collective-permute-start.29) | collective-permute-done | bytes 135200 | tf_op jit(solution)/shard_map/ppermute | solution.py:855
  168.2 3.8 %shard_map.345 = (bf16[256,768]{1,0:T(8,128)(2,1)S(1)}, bf16[256,768]{1,0:T(8,128)(2,1)S(1)}, bf16[256,768]{1,0:T(8,128)(2,1)S(1)}, bf16[256,768]{1,0:T(8,128)(2...) custom-call(s32[2]{0:T(128)S(1)} %pad_add_fusion.refs_0_, ...), custom_call_target="tpu_custom_call" | custom-call | flops 1000000000 | bytes 8114176 | tf_op jit(solution)/shard_map/pallas_call | solution.py:833
  172.6 4.2 %collective-permute-start.32 = (f32[8,768]{1,0:T(8,128)S(1)}, f32[8,768]{1,0:T(8,128)S(1)}, u32[]{:S(2)}, u32[]{:S(2)}) collective-permute-start(f32[8,768]{1,0:T(8,128)S(1)} %get-tuple-element.166.refs_1_), channel_id=1, source_target_pairs={{0,3},{1,0},{2,1},{3,2},{4,7},{5,4},{6,5},{7,6},{8,11},{9,8},{10,9... | collective-permute-start | bytes 73736 | tf_op jit(solution)/shard_map/ppermute | solution.py:855
  176.8 5.4 %collective-permute-start.34 = (bf16[256,768]{1,0:T(8,128)(2,1)S(1)}, bf16[256,768]{1,0:T(8,128)(2,1)S(1)}, u32[]{:S(2)}, u32[]{:S(2)}) collective-permute-start(bf16[256,768]{1,0:T(8,128)(2,1)S(1)} %get-tuple-element.170), channel_id=1, source_target_pairs={{0,1},{1,2},{2,3},{3,0},{4,5},{5,6},{6,7},{7,4},{8,9},{9,10},{10,1... | collective-permute-start | bytes 1179656 | tf_op jit(solution)/shard_map/ppermute | solution.py:855
  185.2 8.1 %collective-permute-done.31.refs_3_ = f32[8,768]{1,0:T(8,128)S(1)} collective-permute-done((f32[8,768]{1,0:T(8,128)S(1)}, f32[8,768]{1,0:T(8,128)S(1)}, u32[]{:S(2)}, u32[]{:S(2)}) %collective-permute-start.31) | collective-permute-done | bytes 24608 | tf_op jit(solution)/shard_map/ppermute | solution.py:855
  202.6 7.5 %collective-permute-start.41 = (f32[8,768]{1,0:T(8,128)S(1)}, f32[8,768]{1,0:T(8,128)S(1)}, u32[]{:S(2)}, u32[]{:S(2)}) collective-permute-start(f32[8,768]{1,0:T(8,128)S(1)} %shard_map.348.refs_1_), channel_id=1, source_target_pairs={{0,8},{4,12},{8,16},{12,20},{16,24},{20,28},{24,0},{28,4},{1,9},{5... | collective-permute-start | bytes 73736 | tf_op jit(solution)/shard_map/ppermute | solution.py:1159
  211.9 5.1 %collective-permute-start.50 = (bf16[96,1280]{1,0:T(8,128)(2,1)S(1)}, bf16[96,1280]{1,0:T(8,128)(2,1)S(1)}, u32[]{:S(2)}, u32[]{:S(2)}) collective-permute-start(bf16[96,1280]{1,0:T(8,128)(2,1)S(1)} %shard_map.352.refs_1_), channel_id=1, source_target_pairs={{0,8},{4,12},{8,16},{12,20},{16,24},{20,28},{24,0},{28,4},{1,9},{5... | collective-permute-start | bytes 737288 | tf_op jit(solution)/shard_map/ppermute | solution.py:1159
  223.5 3.4 %collective-permute-done.36.refs_9_ = bf16[256,768]{1,0:T(8,128)(2,1)S(1)} collective-permute-done((bf16[256,768]{1,0:T(8,128)(2,1)S(1)}, bf16[256,768]{1,0:T(8,128)(2,1)S(1)}, u32[]{:S(2)}, u32[]{:S(2)}) %collective-permute-start.36) | collective-permute-done | bytes 393248 | tf_op jit(solution)/shard_map/ppermute | solution.py:855
  (136 shorter events, 74.2 us)
Async XLA Ops:
  0.6 61.0 %collective-permute-start.2 = (bf16[256,768]{1,0:T(8,128)(2,1)}, bf16[256,768]{1,0:T(8,128)(2,1)S(1)}, u32[]{:S(2)}, u32[]{:S(2)}) collective-permute-start(bf16[256,768]{1,0:T(8,128)(2,1)} %refs_1_.6), channel_id=1, source_target_pairs={{0,3},{1,0},{2,1},{3,2},{4,7},{5,4},{6,5},{7,6},{8,11},{9,8},{10,9... | collective-permute-start | bytes 1179656 | tf_op jit(solution)/shard_map/ppermute | solution.py:855
  5.8 56.9 %collective-permute-start.1 = (bf16[256,768]{1,0:T(8,128)(2,1)}, bf16[256,768]{1,0:T(8,128)(2,1)S(1)}, u32[]{:S(2)}, u32[]{:S(2)}) collective-permute-start(bf16[256,768]{1,0:T(8,128)(2,1)} %refs_1_.6), channel_id=1, source_target_pairs={{0,2},{1,3},{2,0},{3,1},{4,6},{5,7},{6,4},{7,5},{8,10},{9,11},{10,... | collective-permute-start | bytes 1179656 | tf_op jit(solution)/shard_map/ppermute | solution.py:855
  5.8 56.9 %collective-permute-start = (bf16[256,768]{1,0:T(8,128)(2,1)}, bf16[256,768]{1,0:T(8,128)(2,1)S(1)}, u32[]{:S(2)}, u32[]{:S(2)}) collective-permute-start(bf16[256,768]{1,0:T(8,128)(2,1)} %refs_1_.6), channel_id=1, source_target_pairs={{0,1},{1,2},{2,3},{3,0},{4,5},{5,6},{6,7},{7,4},{8,9},{9,10},{10,1... | collective-permute-start | bytes 1179656 | tf_op jit(solution)/shard_map/ppermute | solution.py:855
  8.4 23.9 %collective-permute-start.9 = (bf16[32,768]{1,0:T(8,128)(2,1)S(1)}, bf16[32,768]{1,0:T(8,128)(2,1)S(1)}, u32[]{:S(2)}, u32[]{:S(2)}) collective-permute-start(bf16[32,768]{1,0:T(8,128)(2,1)S(1)} %shard_map.333.refs_0_.refs_10_), channel_id=1, source_target_pairs={{0,3},{1,0},{2,1},{3,2},{4,7},{5,4},{6,5},{7,6},{8,11},{9,8},{10,9... | collective-permute-start | bytes 147464 | tf_op jit(solution)/shard_map/ppermute | solution.py:855
  13.3 30.4 %collective-permute-start.8 = (bf16[32,768]{1,0:T(8,128)(2,1)S(1)}, bf16[32,768]{1,0:T(8,128)(2,1)S(1)}, u32[]{:S(2)}, u32[]{:S(2)}) collective-permute-start(bf16[32,768]{1,0:T(8,128)(2,1)S(1)} %shard_map.333.refs_0_.refs_10_), channel_id=1, source_target_pairs={{0,2},{1,3},{2,0},{3,1},{4,6},{5,7},{6,4},{7,5},{8,10},{9,11},{10,... | collective-permute-start | bytes 147464 | tf_op jit(solution)/shard_map/ppermute | solution.py:855
  32.4 13.2 %collective-permute-start.7 = (bf16[32,768]{1,0:T(8,128)(2,1)S(1)}, bf16[32,768]{1,0:T(8,128)(2,1)S(1)}, u32[]{:S(2)}, u32[]{:S(2)}) collective-permute-start(bf16[32,768]{1,0:T(8,128)(2,1)S(1)} %shard_map.333.refs_0_.refs_10_), channel_id=1, source_target_pairs={{0,1},{1,2},{2,3},{3,0},{4,5},{5,6},{6,7},{7,4},{8,9},{9,10},{10,1... | collective-permute-start | bytes 147464 | tf_op jit(solution)/shard_map/ppermute | solution.py:855
  58.3 23.3 %collective-permute-start.19 = (bf16[256,768]{1,0:T(8,128)(2,1)}, bf16[256,768]{1,0:T(8,128)(2,1)S(1)}, u32[]{:S(2)}, u32[]{:S(2)}) collective-permute-start(bf16[256,768]{1,0:T(8,128)(2,1)} %refs_2_.5), channel_id=1, source_target_pairs={{0,3},{1,0},{2,1},{3,2},{4,7},{5,4},{6,5},{7,6},{8,11},{9,8},{10,9... | collective-permute-start | bytes 1179656 | tf_op jit(solution)/shard_map/ppermute | solution.py:855
  60.6 30.5 %collective-permute-start.18 = (bf16[256,768]{1,0:T(8,128)(2,1)}, bf16[256,768]{1,0:T(8,128)(2,1)S(1)}, u32[]{:S(2)}, u32[]{:S(2)}) collective-permute-start(bf16[256,768]{1,0:T(8,128)(2,1)} %refs_2_.5), channel_id=1, source_target_pairs={{0,2},{1,3},{2,0},{3,1},{4,6},{5,7},{6,4},{7,5},{8,10},{9,11},{10,... | collective-permute-start | bytes 1179656 | tf_op jit(solution)/shard_map/ppermute | solution.py:855
  61.6 29.4 %collective-permute-start.17 = (bf16[256,768]{1,0:T(8,128)(2,1)}, bf16[256,768]{1,0:T(8,128)(2,1)S(1)}, u32[]{:S(2)}, u32[]{:S(2)}) collective-permute-start(bf16[256,768]{1,0:T(8,128)(2,1)} %refs_2_.5), channel_id=1, source_target_pairs={{0,1},{1,2},{2,3},{3,0},{4,5},{5,6},{6,7},{7,4},{8,9},{9,10},{10,1... | collective-permute-start | bytes 1179656 | tf_op jit(solution)/shard_map/ppermute | solution.py:855
  76.4 14.6 %collective-permute-start.16 = (bf16[144,384]{1,0:T(8,128)(2,1)S(1)}, bf16[144,384]{1,0:T(8,128)(2,1)S(1)}, u32[]{:S(2)}, u32[]{:S(2)}) collective-permute-start(bf16[144,384]{1,0:T(8,128)(2,1)S(1)} %get-tuple-element.128), channel_id=1, source_target_pairs={{0,24},{4,28},{1,25},{5,29},{2,26},{6,30},{3,27},{7,31}} | collective-permute-start | bytes 331784 | tf_op jit(solution)/shard_map/ppermute | solution.py:887
  80.3 10.8 %collective-permute-start.15 = (bf16[144,384]{1,0:T(8,128)(2,1)S(1)}, bf16[144,384]{1,0:T(8,128)(2,1)S(1)}, u32[]{:S(2)}, u32[]{:S(2)}) collective-permute-start(bf16[144,384]{1,0:T(8,128)(2,1)S(1)} %get-tuple-element.128), channel_id=1, source_target_pairs={{0,16},{4,20},{8,24},{12,28},{1,17},{5,21},{9,25},{13,29},{2,18},{... | collective-permute-start | bytes 331784 | tf_op jit(solution)/shard_map/ppermute | solution.py:887
  127.2 15.8 %collective-permute-start.27 = (bf16[528,128]{1,0:T(8,128)(2,1)S(1)}, bf16[528,128]{1,0:T(8,128)(2,1)S(1)}, u32[]{:S(2)}, u32[]{:S(2)}) collective-permute-start(bf16[528,128]{1,0:T(8,128)(2,1)S(1)} %get-tuple-element.145), channel_id=1, source_target_pairs={{0,1},{1,2},{2,3},{3,0},{4,5},{5,6},{6,7},{7,4},{8,9},{9,10},{10,1... | collective-permute-start | bytes 405512 | tf_op jit(solution)/shard_map/ppermute | solution.py:855
  127.6 30.0 %collective-permute-start.28 = (bf16[528,128]{1,0:T(8,128)(2,1)S(1)}, bf16[528,128]{1,0:T(8,128)(2,1)S(1)}, u32[]{:S(2)}, u32[]{:S(2)}) collective-permute-start(bf16[528,128]{1,0:T(8,128)(2,1)S(1)} %get-tuple-element.146), channel_id=1, source_target_pairs={{0,2},{1,3},{2,0},{3,1},{4,6},{5,7},{6,4},{7,5},{8,10},{9,11},{10,... | collective-permute-start | bytes 405512 | tf_op jit(solution)/shard_map/ppermute | solution.py:855
  131.2 51.7 %collective-permute-start.44 = (bf16[384,768]{1,0:T(8,128)(2,1)S(1)}, bf16[384,768]{1,0:T(8,128)(2,1)S(1)}, u32[]{:S(2)}, u32[]{:S(2)}) collective-permute-start(bf16[384,768]{1,0:T(8,128)(2,1)S(1)} %get-tuple-element.184), channel_id=1, source_target_pairs={{0,4},{4,0},{8,12},{12,8},{16,20},{20,16},{24,28},{28,24},{1,5},{5... | collective-permute-start | bytes 1769480 | tf_op jit(solution)/shard_map/ppermute | solution.py:860
  131.3 40.7 %collective-permute-start.37 = (bf16[256,768]{1,0:T(8,128)(2,1)S(1)}, bf16[256,768]{1,0:T(8,128)(2,1)S(1)}, u32[]{:S(2)}, u32[]{:S(2)}) collective-permute-start(bf16[256,768]{1,0:T(8,128)(2,1)S(1)} %get-tuple-element.174), channel_id=1, source_target_pairs={{0,1},{1,2},{2,3},{3,0},{4,5},{5,6},{6,7},{7,4},{8,9},{9,10},{10,1... | collective-permute-start | bytes 1179656 | tf_op jit(solution)/shard_map/ppermute | solution.py:855
  134.7 37.9 %collective-permute-start.38 = (bf16[256,768]{1,0:T(8,128)(2,1)S(1)}, bf16[256,768]{1,0:T(8,128)(2,1)S(1)}, u32[]{:S(2)}, u32[]{:S(2)}) collective-permute-start(bf16[256,768]{1,0:T(8,128)(2,1)S(1)} %get-tuple-element.175), channel_id=1, source_target_pairs={{0,2},{1,3},{2,0},{3,1},{4,6},{5,7},{6,4},{7,5},{8,10},{9,11},{10,... | collective-permute-start | bytes 1179656 | tf_op jit(solution)/shard_map/ppermute | solution.py:855
  143.0 53.0 %collective-permute-start.39 = (bf16[256,768]{1,0:T(8,128)(2,1)S(1)}, bf16[256,768]{1,0:T(8,128)(2,1)S(1)}, u32[]{:S(2)}, u32[]{:S(2)}) collective-permute-start(bf16[256,768]{1,0:T(8,128)(2,1)S(1)} %get-tuple-element.176), channel_id=1, source_target_pairs={{0,3},{1,0},{2,1},{3,2},{4,7},{5,4},{6,5},{7,6},{8,11},{9,8},{10,9... | collective-permute-start | bytes 1179656 | tf_op jit(solution)/shard_map/ppermute | solution.py:855
  168.2 14.1 %collective-permute-start.45 = (bf16[384,384]{1,0:T(8,128)(2,1)S(1)}, bf16[384,384]{1,0:T(8,128)(2,1)S(1)}, u32[]{:S(2)}, u32[]{:S(2)}) collective-permute-start(bf16[384,384]{1,0:T(8,128)(2,1)S(1)} %get-tuple-element.186), channel_id=1, source_target_pairs={{0,4},{4,0},{8,12},{12,8},{16,20},{20,16},{24,28},{28,24},{1,5},{5... | collective-permute-start | bytes 884744 | tf_op jit(solution)/shard_map/ppermute | solution.py:860
  172.6 11.6 %collective-permute-start.32 = (f32[8,768]{1,0:T(8,128)S(1)}, f32[8,768]{1,0:T(8,128)S(1)}, u32[]{:S(2)}, u32[]{:S(2)}) collective-permute-start(f32[8,768]{1,0:T(8,128)S(1)} %get-tuple-element.166.refs_1_), channel_id=1, source_target_pairs={{0,3},{1,0},{2,1},{3,2},{4,7},{5,4},{6,5},{7,6},{8,11},{9,8},{10,9... | collective-permute-start | bytes 73736 | tf_op jit(solution)/shard_map/ppermute | solution.py:855
  176.8 40.1 %collective-permute-start.34 = (bf16[256,768]{1,0:T(8,128)(2,1)S(1)}, bf16[256,768]{1,0:T(8,128)(2,1)S(1)}, u32[]{:S(2)}, u32[]{:S(2)}) collective-permute-start(bf16[256,768]{1,0:T(8,128)(2,1)S(1)} %get-tuple-element.170), channel_id=1, source_target_pairs={{0,1},{1,2},{2,3},{3,0},{4,5},{5,6},{6,7},{7,4},{8,9},{9,10},{10,1... | collective-permute-start | bytes 1179656 | tf_op jit(solution)/shard_map/ppermute | solution.py:855
  182.3 11.0 %collective-permute-start.31 = (f32[8,768]{1,0:T(8,128)S(1)}, f32[8,768]{1,0:T(8,128)S(1)}, u32[]{:S(2)}, u32[]{:S(2)}) collective-permute-start(f32[8,768]{1,0:T(8,128)S(1)} %get-tuple-element.166.refs_1_), channel_id=1, source_target_pairs={{0,2},{1,3},{2,0},{3,1},{4,6},{5,7},{6,4},{7,5},{8,10},{9,11},{10,... | collective-permute-start | bytes 73736 | tf_op jit(solution)/shard_map/ppermute | solution.py:855
  182.9 11.9 %collective-permute-start.30 = (f32[8,768]{1,0:T(8,128)S(1)}, f32[8,768]{1,0:T(8,128)S(1)}, u32[]{:S(2)}, u32[]{:S(2)}) collective-permute-start(f32[8,768]{1,0:T(8,128)S(1)} %get-tuple-element.166.refs_1_), channel_id=1, source_target_pairs={{0,1},{1,2},{2,3},{3,0},{4,5},{5,6},{6,7},{7,4},{8,9},{9,10},{10,1... | collective-permute-start | bytes 73736 | tf_op jit(solution)/shard_map/ppermute | solution.py:855
  184.3 15.8 %collective-permute-start.47 = (bf16[96,1280]{1,0:T(8,128)(2,1)S(1)}, bf16[96,1280]{1,0:T(8,128)(2,1)S(1)}, u32[]{:S(2)}, u32[]{:S(2)}) collective-permute-start(bf16[96,1280]{1,0:T(8,128)(2,1)S(1)} %get-tuple-element.190), channel_id=1, source_target_pairs={{0,8},{4,12},{8,16},{12,20},{16,24},{20,28},{24,0},{28,4},{1,9},{5... | collective-permute-start | bytes 737288 | tf_op jit(solution)/shard_map/ppermute | solution.py:1159
  198.0 21.4 %collective-permute-start.35 = (bf16[256,768]{1,0:T(8,128)(2,1)S(1)}, bf16[256,768]{1,0:T(8,128)(2,1)S(1)}, u32[]{:S(2)}, u32[]{:S(2)}) collective-permute-start(bf16[256,768]{1,0:T(8,128)(2,1)S(1)} %get-tuple-element.171), channel_id=1, source_target_pairs={{0,2},{1,3},{2,0},{3,1},{4,6},{5,7},{6,4},{7,5},{8,10},{9,11},{10,... | collective-permute-start | bytes 1179656 | tf_op jit(solution)/shard_map/ppermute | solution.py:855
  (44 other events, 368.2 us)

commit v2 on v1

--- a/solution.py
+++ b/solution.py
@@ -115,23 +115,65 @@
         out[k * rows : (k + 1) * rows, :] = ref[0:rows, :]
 
 
-def front_kernel(heads, n, place, starts, *refs):
-    xs, halos, earlies = refs[:n], refs[n : 2 * n], refs[2 * n : 3 * n]
-    bts = refs[3 * n : 3 * n + 4]
+def setup_kernel(heads, n, place, *refs):
+    earlies, bts = refs[:n], refs[n : n + 4]
     (
-        w_in, w_step, conv_i, bias_i, sbias, dlog, skips, ngain, tri, e_step, e_enter, e_end,
-        normed_o, vals_o, bvals_o, pre_o, bpre_o, bc_o, pk_o, pk2_o, cumt_o, scaled_o, sent_o,
-        dp_o, fin_o, hv_o, hn_o, tok_o, docrow_o, taps, gain, hp, w_s, vec,
-        ext, state, prod, w_bt, x,
-    ) = refs[3 * n + 4 :]
-    c = pl.program_id(0)
-    inner = w_in.shape[1]
-    full = ext.shape[1]
+        w_step, conv_i, bias_i, sbias, dlog, skips, ngain, w_bt, taps, gain, hp, w_s, vec,
+    ) = refs[n + 4 :]
+    inner = conv_i.shape[1]
+    full = taps.shape[1]
     span = w_bt.shape[0] // n
     quarter = span // 4
     gain_own = gain.shape[1] // n
     w = place[0]
     side = lax.rem(lax.div(place[1], 2), 4)
+    taps[0:4, 0:inner] = conv_i[...]
+    taps[4:5, 0:inner] = bias_i[...].reshape(1, inner)
+    taps[5:8, :] = jnp.zeros((3, full), F32)
+    hp[...] = jnp.zeros_like(hp)
+    for g in range(16):
+        lanes = slice(8 * g, 8 * g + heads)
+        hp[0:1, lanes] = sbias[...].reshape(1, heads)
+        hp[1:2, lanes] = jnp.exp(dlog[...].reshape(1, heads))
+    low = iota((1, 128), 1) < 64
+    for p in range(heads // 2):
+        one, two = (jnp.broadcast_to(skips[...].reshape(1, heads)[:, h : h + 1], (1, 128)) for h in (2 * p, 2 * p + 1))
+        vec[0:1, p * 128 : (p + 1) * 128] = jnp.where(low, one, two)
+    vec[1:2, :] = ngain[...].reshape(1, inner)
+    copies = (iota((heads, 128), 0) == lax.rem(iota((heads, 128), 1), 8)).astype(F32)
+    w_s[...] = nn(w_step[...], copies.astype(B16)).astype(B16)
+    for k in range(n):
+        v = lax.rem(w - k + n, n)
+        for q in range(4):
+            at = v * span + (side ^ q) * quarter
+            w_bt[pl.ds(pl.multiple_of(at, quarter), quarter), :] = bts[q][
+                k * quarter : (k + 1) * quarter, :
+            ]
+    for v in range(n):
+        for k in range(n):
+
+            @pl.when(lax.rem(w - v + n, n) == k)
+            def _(v=v, k=k):
+                low = inner + v * span
+                small = earlies[k][quarter:, :].astype(F32)
+                taps[0:5, low : low + span] = (
+                    small[0:5, 0:span] + small[0:5, span : 2 * span]
+                ) + small[0:5, 2 * span : 3 * span]
+                gain[0:1, v * gain_own : (v + 1) * gain_own] = small[5:6, 0:gain_own]
+
+
+def front_kernel(n, place, starts, *refs):
+    xs, halos = refs[:n], refs[n : 2 * n]
+    (
+        w_bt, taps, gain, hp, w_s, w_in, tri, e_step, e_enter, e_end,
+        normed_o, vals_o, bvals_o, pre_o, bpre_o, bc_o, pk_o, pk2_o, cumt_o, scaled_o, sent_o,
+        dp_o, fin_o, hv_o, hn_o, tok_o, docrow_o,
+        ext, state, prod, x,
+    ) = refs[2 * n :]
+    c = pl.program_id(0)
+    inner = w_in.shape[1]
+    full = ext.shape[1]
+    w = place[0]
 
     def project(values):
         wide = values.astype(F32)
@@ -139,40 +181,6 @@
 
     @pl.when(c == 0)
     def _():
-        taps[0:4, 0:inner] = conv_i[...]
-        taps[4:5, 0:inner] = bias_i[...].reshape(1, inner)
-        taps[5:8, :] = jnp.zeros((3, full), F32)
-        hp[...] = jnp.zeros_like(hp)
-        for g in range(16):
-            lanes = slice(8 * g, 8 * g + heads)
-            hp[0:1, lanes] = sbias[...].reshape(1, heads)
-            hp[1:2, lanes] = jnp.exp(dlog[...].reshape(1, heads))
-        low = iota((1, 128), 1) < 64
-        for p in range(heads // 2):
-            one, two = (jnp.broadcast_to(skips[...].reshape(1, heads)[:, h : h + 1], (1, 128)) for h in (2 * p, 2 * p + 1))
-            vec[0:1, p * 128 : (p + 1) * 128] = jnp.where(low, one, two)
-        vec[1:2, :] = ngain[...].reshape(1, inner)
-        copies = (iota((heads, 128), 0) == lax.rem(iota((heads, 128), 1), 8)).astype(F32)
-        w_s[...] = nn(w_step[...], copies.astype(B16)).astype(B16)
-        for k in range(n):
-            v = lax.rem(w - k + n, n)
-            for q in range(4):
-                at = v * span + (side ^ q) * quarter
-                w_bt[pl.ds(pl.multiple_of(at, quarter), quarter), :] = bts[q][
-                    k * quarter : (k + 1) * quarter, :
-                ]
-        for v in range(n):
-            for k in range(n):
-
-                @pl.when(lax.rem(w - v + n, n) == k)
-                def _(v=v, k=k):
-                    low = inner + v * span
-                    small = earlies[k][quarter:, :].astype(F32)
-                    taps[0:5, low : low + span] = (
-                        small[0:5, 0:span] + small[0:5, span : 2 * span]
-                    ) + small[0:5, 2 * span : 3 * span]
-                    gain[0:1, v * gain_own : (v + 1) * gain_own] = small[5:6, 0:gain_own]
-
         hn = project(total(halos))
         hn_o[...] = hn
         ext[0:8, 0:inner] = nn(hn, w_in[...])
@@ -303,21 +311,15 @@
 
 
 def join_kernel(n, m, place, y, gate, bc, pk2, sent, dp, keep, *refs):
-    others, cots = refs[:m], refs[m : m + n]
-    w_out, vec, e_enter, ssd_o, inter_o, gn_o, stats_o, s_in, cot_o = refs[m + n : m + n + 9]
-    mixes = refs[m + n + 9 :]
+    others = refs[:m]
+    w_out, vec, e_enter, ssd_o, inter_o, gated_o, squares_o, s_in = refs[m : m + 8]
+    mixes = refs[m + 8 :]
     c = pl.program_id(0)
     inner = y.shape[1]
 
     @pl.when(c == 0)
     def _():
         fold_states(keep, others, s_in)
-
-    for k in range(n):
-
-        @pl.when(lax.rem(place[0] - c + n, n) == k)
-        def _(k=k):
-            cot_o[...] = cots[k][...]
 
     entering = sent[0] + dp[0, 0:1, :] * s_in[...]
     inter = nn(pk2[...], e_enter[...]) * nn(bc[:, 128:], entering.astype(B16))
@@ -325,6 +327,7 @@
     ssd = y[...] + inter
     ssd_o[...] = ssd
     gated = ssd * silu(gate[...])
+    gated_o[...] = gated
     mixed = nn((gated * vec[1:2, :]).astype(B16), w_out[...]).astype(B16)
     for k in range(n):
 
@@ -332,14 +335,25 @@
         def _(k=k):
             mixes[k][...] = mixed
 
+    first = (iota((inner, 128), 1) == 0).astype(F32).astype(B16)
+    squares_o[...] = two_dot(gated * gated, first).T[0:8, :]
+
+
+def dots_kernel(n, place, gated, squares, *refs):
+    cots = refs[:n]
+    w_out, vec, gn_o, stats_o, cot_o = refs[n:]
+    c = pl.program_id(0)
+    inner = gated.shape[1]
+    for k in range(n):
+
+        @pl.when(lax.rem(place[0] - c + n, n) == k)
+        def _(k=k):
+            cot_o[...] = cots[k][...]
+
     gn = nt(cot_o[...], w_out[...])
     gn_o[...] = gn
-    lane = iota((inner, 128), 1)
-    first = (lane == 0).astype(F32).astype(B16)
-    second = (lane == 1).astype(F32).astype(B16)
-    both = two_dot(gated * gated, first)
-    both = both + two_dot(vec[1:2, :] * gn * gated, second)
-    stats_o[...] = both.T[0:8, :]
+    second = (iota((inner, 128), 1) == 1).astype(F32).astype(B16)
+    stats_o[...] = squares[...] + two_dot(vec[1:2, :] * gn * gated[...], second).T[0:8, :]
 
 
 def gate_kernel(n, width_all, ssd, gate, gn, vec, pre, bc, pk2, e_enter, *refs):
@@ -992,30 +1006,33 @@
     fin_spec, state_spec = whole(144, inner), whole(128, inner)
     e_spec = whole(128, inner)
     states_out = [shape((count, 128, inner)), shape((count, 8, inner)), shape((144, inner), B16)]
+    w_bt, taps, gain, hp, w_s, vec = call(
+        functools.partial(setup_kernel, heads, n_wt), (),
+        [*earlies, bts, bts_x, *bts_y, proj_step, conv_inner, conv_inner_bias, step_bias,
+         decay_log, skip_gain, norm_gain],
+        [None] * (n_wt + 11),
+        [shape((span * n_wt, d), B16), shape((8, full)), shape((8, d)), shape((8, 128)),
+         shape((d, 128), B16), shape((8, inner))],
+        [None] * 6, scalars=(place,), fetch=tuple(range(n_wt + 4, n_wt + 11)),
+    )
     (normed, vals, bvals, pre, bpre, bc, pk, pk2, cumt, scaled, sent, dp, fin, hv, hn, tok,
-     docrow, taps, gain, hp, w_s, vec) = call(
-        functools.partial(front_kernel, heads, n_wt), grid,
-        [*rows, *halos, *earlies, bts, bts_x, *bts_y, proj_inner, proj_step, conv_inner,
-         conv_inner_bias, step_bias, decay_log, skip_gain, norm_gain, tri, e_step, e_enter,
-         e_end],
-        [None] * (3 * n_wt + 16),
+     docrow) = call(
+        functools.partial(front_kernel, n_wt), grid,
+        [*rows, *halos, w_bt, taps, gain, hp, w_s, proj_inner, tri, e_step, e_enter, e_end],
+        [None] * (2 * n_wt + 10),
         [shape((length, d), B16), shape((length, inner), B16), shape((length, 256), B16),
          shape((length, inner)), shape((length, 256)),
          shape((length, 256), B16), shape((length, 128)), shape((length, 128), B16),
          shape((8, length)), shape((length, inner), B16), *states_out,
-         shape((8, full)), shape((8, d), B16), shape((length, 8)), shape((8, length)),
-         shape((8, full)), shape((8, d)), shape((8, 128)), shape((d, 128), B16),
-         shape((8, inner))],
+         shape((8, full)), shape((8, d), B16), shape((length, 8)), shape((8, length))],
         [by_rows(), by_rows(), by_rows(), by_rows(), by_rows(), by_rows(),
          by_rows(), by_rows(),
          by_cols, by_rows(), by_chunk(128, inner), by_chunk(8, inner), fin_spec,
-         whole(8, full), whole(8, d), by_rows(), by_cols, whole(8, full), whole(8, d),
-         None, None, None],
+         whole(8, full), whole(8, d), by_rows(), by_cols],
         scratch=[pltpu.VMEM((Q + 8, full), F32), pltpu.VMEM((128, inner), F32),
-                 pltpu.VMEM((8, inner), F32), pltpu.VMEM((span * n_wt, d), B16),
-                 pltpu.VMEM((Q, d), B16)],
+                 pltpu.VMEM((8, inner), F32), pltpu.VMEM((Q, d), B16)],
         scalars=scalars, flops=2e9,
-        fetch=(0, *range(3 * n_wt + 4, 3 * n_wt + 16)),
+        fetch=(0, *range(2 * n_wt + 5, 2 * n_wt + 10)),
     )
     keep, got = states(fin, place, False)
     gate, y = call(
@@ -1027,17 +1044,24 @@
         [by_rows(), by_rows()], flops=2e9,
     )
     got_spec = [whole(136, inner)] + [fin_spec] * (pairs - 1)
-    ssd, inter, gn, stats, s_in, cot, *mixes = call(
+    ssd, inter, gated, squares, s_in, *mixes = call(
         functools.partial(join_kernel, n_wt, pairs - 1), grid,
-        [y, gate, bc, pk2, sent, dp, keep, *got, *cots, proj_out, vec, e_enter],
+        [y, gate, bc, pk2, sent, dp, keep, *got, proj_out, vec, e_enter],
         [by_rows(), by_rows(), by_rows(), by_rows(),
          by_chunk(128, inner), by_chunk(8, inner), *got_spec]
-        + [whole(Q, d)] * n_wt + [whole(inner, d), whole(1, inner), e_spec],
-        [shape((length, inner))] * 3
-        + [shape((8, length)), shape((128, inner)), shape((length, d), B16)]
+        + [whole(inner, d), whole(1, inner), e_spec],
+        [shape((length, inner))] * 3 + [shape((8, length)), shape((128, inner))]
         + [shape((Q, d), B16)] * n_wt,
-        [by_rows()] * 3 + [by_cols, state_spec, by_rows()] + [None] * n_wt,
+        [by_rows()] * 3 + [by_cols, state_spec] + [None] * n_wt,
         scalars=(place,), flops=2e9,
+    )
+    gn, stats, cot = call(
+        functools.partial(dots_kernel, n_wt), grid,
+        [gated, squares, *cots, proj_out, vec],
+        [by_rows(), by_cols] + [None] * (n_wt + 2),
+        [shape((length, inner)), shape((8, length)), shape((length, d), B16)],
+        [by_rows(), by_cols, by_rows()],
+        scalars=(place,), flops=1e9,
     )
     gnorm, gate16, gs, nsums, sb, db, back_fin, rms = call(
         functools.partial(gate_kernel, n_wt, width_all), grid,

time: 233 us -> 258 us (1.11)
  waiting for transfers between devices: 69.1 us -> 88.9 us
  Pallas kernels: 63.3 us -> 66.5 us
    ppermute x24, waiting for transfers between devices: 58.5 us -> 78.4 us  [ring(): lax.ppermute(value, axis, [(i, (i + distance) % count) for i in range(cou...]
    pallas_call x21 -> x23, Pallas kernels: 63.3 us -> 66.5 us  [call(): pl.pallas_call(body, out_shape=outs, grid_spec=pltpu.PrefetchScalarGridSp...]
  transfers between devices with their start and end apart: 57 -> 57, of which waited for: 18 -> 19; matrix products, arithmetic and copies ran while one was open for 1% -> 1% of each run, Pallas kernels for 20% -> 16%
where the time goes in v2:
time: 258 us; the launch traced here: 256 us
  starting transfers between devices  96.8 us (38%)
  waiting for transfers between devices  88.9 us (34%)
  Pallas kernels  66.5 us (26%)
    ppermute x24, waiting for transfers between devices, ring(): lax.ppermute(value, axis, [(i, (i + distance) % count) for i in range(cou...  78.4 us
    pallas_call x23, Pallas kernels, call(): pl.pallas_call(body, out_shape=outs, grid_spec=pltpu.PrefetchScalarGridSp...  66.5 us
    ppermute x24, starting transfers between devices, ring(): lax.ppermute(value, axis, [(i, (i + distance) % count) for i in range(cou...  51.2 us
    ppermute x9, starting transfers between devices, pair_ring(): lax.ppermute(value, 'seq', [(i, (i + 2 * k) % n_seq) for i in range(n_seq)])  20.5 us
    ppermute x13, starting transfers between devices, swap(): return lax.ppermute(value, axis, [(i, i ^ 1 << bit) for i in range(count)])  11.8 us
    ppermute x6, starting transfers between devices, states(): got.append(lax.ppermute(both, 'seq', pairs))  9.92 us
    ppermute x13, waiting for transfers between devices, swap(): return lax.ppermute(value, axis, [(i, i ^ 1 << bit) for i in range(count)])  6.43 us
  transfers between devices with their start and end apart: 57, of which 19 were waited for; matrix products, arithmetic and copies ran while one was open for 1% of the time, Pallas kernels for 16%

profile of v2, /device:TPU:0, one launch (start us, length us, event | category | flops | bytes accessed | tf_op | source)
XLA Modules:
  0.0 256.3 jit_solution(11523475645929023360)
XLA Ops:
  0.6 5.1 %collective-permute-start.8 = (bf16[256,768]{1,0:T(8,128)(2,1)}, bf16[256,768]{1,0:T(8,128)(2,1)S(1)}, u32[]{:S(2)}, u32[]{:S(2)}) collective-permute-start(bf16[256,768]{1,0:T(8,128)(2,1)} %refs_1_.6), channel_id=1, source_target_pairs={{0,3},{1,0},{2,1},{3,2},{4,7},{5,4},{6,5},{7,6},{8,11},{9,8},{10,9... | collective-permute-start | bytes 1179656 | tf_op jit(solution)/shard_map/ppermute | solution.py:869
  12.4 20.5 %collective-permute-done.2.refs_3_.refs_4_ = bf16[32,768]{1,0:T(8,128)(2,1)S(1)} collective-permute-done((bf16[32,768]{1,0:T(8,128)(2,1)S(1)}, bf16[32,768]{1,0:T(8,128)(2,1)S(1)}, u32[]{:S(2)}, u32[]{:S(2)}) %collective-permute-start.2) | collective-permute-done | bytes 49184 | tf_op jit(solution)/shard_map/ppermute | solution.py:869
  32.9 10.9 %collective-permute-start = (bf16[32,768]{1,0:T(8,128)(2,1)S(1)}, bf16[32,768]{1,0:T(8,128)(2,1)S(1)}, u32[]{:S(2)}, u32[]{:S(2)}) collective-permute-start(bf16[32,768]{1,0:T(8,128)(2,1)S(1)} %shard_map.333.refs_0_.refs_1_), channel_id=1, source_target_pairs={{0,1},{1,2},{2,3},{3,0},{4,5},{5,6},{6,7},{7,4},{8,9},{9,10},{10,1... | collective-permute-start | bytes 147464 | tf_op jit(solution)/shard_map/ppermute | solution.py:869
  60.4 10.9 %shard_map.336 = (bf16[1024,768]{1,0:T(8,128)(2,1)S(1)}, bf16[1024,384]{1,0:T(8,128)(2,1)S(1)}, bf16[1024,256]{1,0:T(8,128)(2,1)S(1)}, f32[1024,384]{1,0:T(8,128...) custom-call(s32[2]{0:T(128)S(1)} %pad_add_fusion.refs_0_, ...), custom_call_target="tpu_custom_call" | custom-call | flops 2000000000 | bytes 11956224 | tf_op jit(solution)/shard_map/pallas_call | solution.py:847
  71.3 6.4 %collective-permute-start.13 = (bf16[144,384]{1,0:T(8,128)(2,1)S(1)}, bf16[144,384]{1,0:T(8,128)(2,1)S(1)}, u32[]{:S(2)}, u32[]{:S(2)}) collective-permute-start(bf16[144,384]{1,0:T(8,128)(2,1)S(1)} %get-tuple-element.133.refs_1_), channel_id=1, source_target_pairs={{0,4},{4,0},{8,12},{12,8},{16,20},{20,16},{24,28},{28,24},{1,5},{5... | collective-permute-start | bytes 331784 | tf_op jit(solution)/shard_map/ppermute | solution.py:874
  81.6 3.4 %collective-permute-start.19 = (bf16[256,768]{1,0:T(8,128)(2,1)S(1)}, bf16[256,768]{1,0:T(8,128)(2,1)S(1)}, u32[]{:S(2)}, u32[]{:S(2)}) collective-permute-start(bf16[256,768]{1,0:T(8,128)(2,1)S(1)} %copy-done), channel_id=1, source_target_pairs={{0,3},{1,0},{2,1},{3,2},{4,7},{5,4},{6,5},{7,6},{8,11},{9,8},{10,9... | collective-permute-start | bytes 1179656 | tf_op jit(solution)/shard_map/ppermute | solution.py:869
  91.2 3.6 %shard_map.337 = (f32[1024,384]{1,0:T(8,128)S(1)}, f32[1024,384]{1,0:T(8,128)S(1)}) custom-call(bf16[1024,768]{1,0:T(8,128)(2,1)S(1)} %get-tuple-element.119.refs_0_.refs_7_.refs_8_.refs_2_, bf16[768,384]{1,0:T(8,128)(2,1)S(1)} %copy-done.10, f32[1024,384]{1,0:T(8,128)S(1)} %get-tuple-element.120.refs_2_.refs_4_.refs_6_, ...), custom_call_target="tpu_custom_call" | custom-call | flops 2000000000 | bytes 8826880 | tf_op jit(solution)/shard_map/pallas_call | solution.py:847
  94.8 4.9 %shard_map.339 = (f32[1024,384]{1,0:T(8,128)S(1)}, f32[1024,384]{1,0:T(8,128)S(1)}, f32[1024,384]{1,0:T(8,128)S(1)}, f32[8,1024]{1,0:T(8,128)S(1)}, f32[128,384]...) custom-call(s32[2]{0:T(128)S(1)} %pad_add_fusion.refs_0_, ...), custom_call_target="tpu_custom_call" | custom-call | flops 2000000000 | bytes 12529664 | tf_op jit(solution)/shard_map/pallas_call | solution.py:847
  99.6 20.1 %collective-permute-done.18.refs_5_ = bf16[256,768]{1,0:T(8,128)(2,1)S(1)} collective-permute-done((bf16[256,768]{1,0:T(8,128)(2,1)S(1)}, bf16[256,768]{1,0:T(8,128)(2,1)S(1)}, u32[]{:S(2)}, u32[]{:S(2)}) %collective-permute-start.18) | collective-permute-done | bytes 393248 | tf_op jit(solution)/shard_map/ppermute | solution.py:869
  119.8 3.2 %shard_map.340 = (f32[1024,384]{1,0:T(8,128)S(1)}, f32[8,1024]{1,0:T(8,128)S(1)}, bf16[1024,768]{1,0:T(8,128)(2,1)S(1)}) custom-call(s32[2]{0:T(128)S(1)} %pad_add_fusion.refs_0_, f32[1024,384]{1,0:T(8,128)S(1)} %get-tuple-element.137.refs_1_, f32[8,1024]{1,0:T(8,128)S(1)} %get-tuple-element.138.refs_2_, bf16[256,768]{1,0:T(8,128)(2,1)S(1)} %copy-done, ...), custom_call_target="tpu_custom_call" | custom-call | flops 1000000000 | bytes 6959104 | tf_op jit(solution)/shard_map/pallas_call | solution.py:847
  140.2 4.9 %shard_map.342 = (f32[1024,384]{1,0:T(8,128)S(1)}, f32[1024,128]{1,0:T(8,128)S(1)}, f32[1024,256]{1,0:T(8,128)S(1)}) custom-call(f32[1024,384]{1,0:T(8,128)S(1)} %get-tuple-element.141.refs_0_.refs_2_, bf16[1024,256]{1,0:T(8,128)(2,1)S(1)} %get-tuple-element.121.refs_3_.refs_5_.refs_1_.refs_8_, f32[1024,128]{1,0:T(8,128)S(1)} %get-tuple-element.122.refs_4_.refs_2_.refs_9_, ...), custom_call_target="tpu_custom_call" | custom-call | flops 4000000000 | bytes 8044544 | tf_op jit(solution)/shard_map/pallas_call | solution.py:847
  146.6 4.8 %shard_map.344 = (bf16[528,128]{1,0:T(8,128)(2,1)S(1)}, bf16[528,128]{1,0:T(8,128)(2,1)S(1)}, bf16[528,128]{1,0:T(8,128)(2,1)S(1)}, bf16[528,128]{1,0:T(8,128)(2...) custom-call(s32[2]{0:T(128)S(1)} %pad_add_fusion.refs_0_, s32[1]{0:T(128)S(6)} %copy.39.refs_1_, ...), custom_call_target="tpu_custom_call" | custom-call | flops 1000000000 | bytes 5963776 | tf_op jit(solution)/shard_map/pallas_call | solution.py:847
  155.5 3.3 %collective-permute-start.37 = (bf16[256,768]{1,0:T(8,128)(2,1)S(1)}, bf16[256,768]{1,0:T(8,128)(2,1)S(1)}, u32[]{:S(2)}, u32[]{:S(2)}) collective-permute-start(bf16[256,768]{1,0:T(8,128)(2,1)S(1)} %get-tuple-element.180), channel_id=1, source_target_pairs={{0,1},{1,2},{2,3},{3,0},{4,5},{5,6},{6,7},{7,4},{8,9},{9,10},{10,1... | collective-permute-start | bytes 1179656 | tf_op jit(solution)/shard_map/ppermute | solution.py:869
  158.9 8.3 %shard_map.345 = (bf16[1024,384]{1,0:T(8,128)(2,1)S(1)}, bf16[1024,128]{1,0:T(8,128)(2,1)S(1)}, f32[8,384]{1,0:T(8,128)S(1)}, f32[8,384]{1,0:T(8,128)S(1)}, f32[8,128]{1,0:T(8,128)S(1)}) custom-call(s32[2]{0:T(128)S(1)} %pad_add_fusion.refs_0_, s32[1]{0:T(128)S(6)} %copy.39.refs_1_, f32[1024,384]{1,0:T(8,128)S(1)} %get-tuple-element.141.refs_0_.refs_2_, ...), custom_call_target="tpu_custom_call" | custom-call | flops 1000000000 | bytes 13455360 | tf_op jit(solution)/shard_map/pallas_call | solution.py:847
  169.7 12.0 %collective-permute-done.28.refs_3_ = bf16[528,128]{1,0:T(8,128)(2,1)S(1)} collective-permute-done((bf16[528,128]{1,0:T(8,128)(2,1)S(1)}, bf16[528,128]{1,0:T(8,128)(2,1)S(1)}, u32[]{:S(2)}, u32[]{:S(2)}) %collective-permute-start.28) | collective-permute-done | bytes 135200 | tf_op jit(solution)/shard_map/ppermute | solution.py:869
  181.8 4.0 %shard_map.346 = (f32[1024,768]{1,0:T(8,128)S(1)}, bf16[384,384]{1,0:T(8,128)(2,1)S(1)}, bf16[384,384]{1,0:T(8,128)(2,1)S(1)}) custom-call(s32[2]{0:T(128)S(1)} %pad_add_fusion.refs_0_, bf16[1024,384]{1,0:T(8,128)(2,1)S(1)} %get-tuple-element.163.refs_1_.refs_2_, bf16[1024,384]{1,0:T(8,128)(2,1)S(1)} %get-tuple-element.163.refs_1_.refs_2_, ...), custom_call_target="tpu_custom_call" | custom-call | flops 2000000000 | bytes 9330688 | tf_op jit(solution)/shard_map/pallas_call | solution.py:847
  185.8 6.6 %collective-permute-done.29.refs_4_ = bf16[528,128]{1,0:T(8,128)(2,1)S(1)} collective-permute-done((bf16[528,128]{1,0:T(8,128)(2,1)S(1)}, bf16[528,128]{1,0:T(8,128)(2,1)S(1)}, u32[]{:S(2)}, u32[]{:S(2)}) %collective-permute-start.29) | collective-permute-done | bytes 135200 | tf_op jit(solution)/shard_map/ppermute | solution.py:869
  192.4 3.8 %shard_map.347 = (bf16[256,768]{1,0:T(8,128)(2,1)S(1)}, bf16[256,768]{1,0:T(8,128)(2,1)S(1)}, bf16[256,768]{1,0:T(8,128)(2,1)S(1)}, bf16[256,768]{1,0:T(8,128)(2...) custom-call(s32[2]{0:T(128)S(1)} %pad_add_fusion.refs_0_, ...), custom_call_target="tpu_custom_call" | custom-call | flops 1000000000 | bytes 8114176 | tf_op jit(solution)/shard_map/pallas_call | solution.py:847
  196.8 4.2 %collective-permute-start.32 = (f32[8,768]{1,0:T(8,128)S(1)}, f32[8,768]{1,0:T(8,128)S(1)}, u32[]{:S(2)}, u32[]{:S(2)}) collective-permute-start(f32[8,768]{1,0:T(8,128)S(1)} %get-tuple-element.172.refs_1_), channel_id=1, source_target_pairs={{0,3},{1,0},{2,1},{3,2},{4,7},{5,4},{6,5},{7,6},{8,11},{9,8},{10,9... | collective-permute-start | bytes 73736 | tf_op jit(solution)/shard_map/ppermute | solution.py:869
  201.0 5.5 %collective-permute-start.34 = (bf16[256,768]{1,0:T(8,128)(2,1)S(1)}, bf16[256,768]{1,0:T(8,128)(2,1)S(1)}, u32[]{:S(2)}, u32[]{:S(2)}) collective-permute-start(bf16[256,768]{1,0:T(8,128)(2,1)S(1)} %get-tuple-element.176), channel_id=1, source_target_pairs={{0,1},{1,2},{2,3},{3,0},{4,5},{5,6},{6,7},{7,4},{8,9},{9,10},{10,1... | collective-permute-start | bytes 1179656 | tf_op jit(solution)/shard_map/ppermute | solution.py:869
  209.6 7.9 %collective-permute-done.31.refs_3_ = f32[8,768]{1,0:T(8,128)S(1)} collective-permute-done((f32[8,768]{1,0:T(8,128)S(1)}, f32[8,768]{1,0:T(8,128)S(1)}, u32[]{:S(2)}, u32[]{:S(2)}) %collective-permute-start.31) | collective-permute-done | bytes 24608 | tf_op jit(solution)/shard_map/ppermute | solution.py:869
  227.0 7.5 %collective-permute-start.41 = (f32[8,768]{1,0:T(8,128)S(1)}, f32[8,768]{1,0:T(8,128)S(1)}, u32[]{:S(2)}, u32[]{:S(2)}) collective-permute-start(f32[8,768]{1,0:T(8,128)S(1)} %shard_map.350.refs_1_), channel_id=1, source_target_pairs={{0,8},{4,12},{8,16},{12,20},{16,24},{20,28},{24,0},{28,4},{1,9},{5... | collective-permute-start | bytes 73736 | tf_op jit(solution)/shard_map/ppermute | solution.py:1183
  236.3 5.1 %collective-permute-start.50 = (bf16[96,1280]{1,0:T(8,128)(2,1)S(1)}, bf16[96,1280]{1,0:T(8,128)(2,1)S(1)}, u32[]{:S(2)}, u32[]{:S(2)}) collective-permute-start(bf16[96,1280]{1,0:T(8,128)(2,1)S(1)} %shard_map.354.refs_1_), channel_id=1, source_target_pairs={{0,8},{4,12},{8,16},{12,20},{16,24},{20,28},{24,0},{28,4},{1,9},{5... | collective-permute-start | bytes 737288 | tf_op jit(solution)/shard_map/ppermute | solution.py:1183
  247.9 3.4 %collective-permute-done.36.refs_9_ = bf16[256,768]{1,0:T(8,128)(2,1)S(1)} collective-permute-done((bf16[256,768]{1,0:T(8,128)(2,1)S(1)}, bf16[256,768]{1,0:T(8,128)(2,1)S(1)}, u32[]{:S(2)}, u32[]{:S(2)}) %collective-permute-start.36) | collective-permute-done | bytes 393248 | tf_op jit(solution)/shard_map/ppermute | solution.py:869
  (138 shorter events, 84.2 us)
Async XLA Ops:
  0.6 59.7 %collective-permute-start.8 = (bf16[256,768]{1,0:T(8,128)(2,1)}, bf16[256,768]{1,0:T(8,128)(2,1)S(1)}, u32[]{:S(2)}, u32[]{:S(2)}) collective-permute-start(bf16[256,768]{1,0:T(8,128)(2,1)} %refs_1_.6), channel_id=1, source_target_pairs={{0,3},{1,0},{2,1},{3,2},{4,7},{5,4},{6,5},{7,6},{8,11},{9,8},{10,9... | collective-permute-start | bytes 1179656 | tf_op jit(solution)/shard_map/ppermute | solution.py:869
  5.8 54.6 %collective-permute-start.7 = (bf16[256,768]{1,0:T(8,128)(2,1)}, bf16[256,768]{1,0:T(8,128)(2,1)S(1)}, u32[]{:S(2)}, u32[]{:S(2)}) collective-permute-start(bf16[256,768]{1,0:T(8,128)(2,1)} %refs_1_.6), channel_id=1, source_target_pairs={{0,2},{1,3},{2,0},{3,1},{4,6},{5,7},{6,4},{7,5},{8,10},{9,11},{10,... | collective-permute-start | bytes 1179656 | tf_op jit(solution)/shard_map/ppermute | solution.py:869
  5.8 54.6 %collective-permute-start.6 = (bf16[256,768]{1,0:T(8,128)(2,1)}, bf16[256,768]{1,0:T(8,128)(2,1)S(1)}, u32[]{:S(2)}, u32[]{:S(2)}) collective-permute-start(bf16[256,768]{1,0:T(8,128)(2,1)} %refs_1_.6), channel_id=1, source_target_pairs={{0,1},{1,2},{2,3},{3,0},{4,5},{5,6},{6,7},{7,4},{8,9},{9,10},{10,1... | collective-permute-start | bytes 1179656 | tf_op jit(solution)/shard_map/ppermute | solution.py:869
  8.4 24.5 %collective-permute-start.2 = (bf16[32,768]{1,0:T(8,128)(2,1)S(1)}, bf16[32,768]{1,0:T(8,128)(2,1)S(1)}, u32[]{:S(2)}, u32[]{:S(2)}) collective-permute-start(bf16[32,768]{1,0:T(8,128)(2,1)S(1)} %shard_map.333.refs_0_.refs_1_), channel_id=1, source_target_pairs={{0,3},{1,0},{2,1},{3,2},{4,7},{5,4},{6,5},{7,6},{8,11},{9,8},{10,9... | collective-permute-start | bytes 147464 | tf_op jit(solution)/shard_map/ppermute | solution.py:869
  11.3 32.5 %collective-permute-start.1 = (bf16[32,768]{1,0:T(8,128)(2,1)S(1)}, bf16[32,768]{1,0:T(8,128)(2,1)S(1)}, u32[]{:S(2)}, u32[]{:S(2)}) collective-permute-start(bf16[32,768]{1,0:T(8,128)(2,1)S(1)} %shard_map.333.refs_0_.refs_1_), channel_id=1, source_target_pairs={{0,2},{1,3},{2,0},{3,1},{4,6},{5,7},{6,4},{7,5},{8,10},{9,11},{10,... | collective-permute-start | bytes 147464 | tf_op jit(solution)/shard_map/ppermute | solution.py:869
  32.9 12.7 %collective-permute-start = (bf16[32,768]{1,0:T(8,128)(2,1)S(1)}, bf16[32,768]{1,0:T(8,128)(2,1)S(1)}, u32[]{:S(2)}, u32[]{:S(2)}) collective-permute-start(bf16[32,768]{1,0:T(8,128)(2,1)S(1)} %shard_map.333.refs_0_.refs_1_), channel_id=1, source_target_pairs={{0,1},{1,2},{2,3},{3,0},{4,5},{5,6},{6,7},{7,4},{8,9},{9,10},{10,1... | collective-permute-start | bytes 147464 | tf_op jit(solution)/shard_map/ppermute | solution.py:869
  81.6 18.1 %collective-permute-start.19 = (bf16[256,768]{1,0:T(8,128)(2,1)S(1)}, bf16[256,768]{1,0:T(8,128)(2,1)S(1)}, u32[]{:S(2)}, u32[]{:S(2)}) collective-permute-start(bf16[256,768]{1,0:T(8,128)(2,1)S(1)} %copy-done), channel_id=1, source_target_pairs={{0,3},{1,0},{2,1},{3,2},{4,7},{5,4},{6,5},{7,6},{8,11},{9,8},{10,9... | collective-permute-start | bytes 1179656 | tf_op jit(solution)/shard_map/ppermute | solution.py:869
  85.0 34.8 %collective-permute-start.18 = (bf16[256,768]{1,0:T(8,128)(2,1)S(1)}, bf16[256,768]{1,0:T(8,128)(2,1)S(1)}, u32[]{:S(2)}, u32[]{:S(2)}) collective-permute-start(bf16[256,768]{1,0:T(8,128)(2,1)S(1)} %copy-done), channel_id=1, source_target_pairs={{0,2},{1,3},{2,0},{3,1},{4,6},{5,7},{6,4},{7,5},{8,10},{9,11},{10,... | collective-permute-start | bytes 1179656 | tf_op jit(solution)/shard_map/ppermute | solution.py:869
  85.4 34.4 %collective-permute-start.17 = (bf16[256,768]{1,0:T(8,128)(2,1)S(1)}, bf16[256,768]{1,0:T(8,128)(2,1)S(1)}, u32[]{:S(2)}, u32[]{:S(2)}) collective-permute-start(bf16[256,768]{1,0:T(8,128)(2,1)S(1)} %copy-done), channel_id=1, source_target_pairs={{0,1},{1,2},{2,3},{3,0},{4,5},{5,6},{6,7},{7,4},{8,9},{9,10},{10,1... | collective-permute-start | bytes 1179656 | tf_op jit(solution)/shard_map/ppermute | solution.py:869
  151.4 15.9 %collective-permute-start.27 = (bf16[528,128]{1,0:T(8,128)(2,1)S(1)}, bf16[528,128]{1,0:T(8,128)(2,1)S(1)}, u32[]{:S(2)}, u32[]{:S(2)}) collective-permute-start(bf16[528,128]{1,0:T(8,128)(2,1)S(1)} %get-tuple-element.153), channel_id=1, source_target_pairs={{0,1},{1,2},{2,3},{3,0},{4,5},{5,6},{6,7},{7,4},{8,9},{9,10},{10,1... | collective-permute-start | bytes 405512 | tf_op jit(solution)/shard_map/ppermute | solution.py:869
  151.7 30.0 %collective-permute-start.28 = (bf16[528,128]{1,0:T(8,128)(2,1)S(1)}, bf16[528,128]{1,0:T(8,128)(2,1)S(1)}, u32[]{:S(2)}, u32[]{:S(2)}) collective-permute-start(bf16[528,128]{1,0:T(8,128)(2,1)S(1)} %get-tuple-element.154), channel_id=1, source_target_pairs={{0,2},{1,3},{2,0},{3,1},{4,6},{5,7},{6,4},{7,5},{8,10},{9,11},{10,... | collective-permute-start | bytes 405512 | tf_op jit(solution)/shard_map/ppermute | solution.py:869
  155.5 51.6 %collective-permute-start.44 = (bf16[384,768]{1,0:T(8,128)(2,1)S(1)}, bf16[384,768]{1,0:T(8,128)(2,1)S(1)}, u32[]{:S(2)}, u32[]{:S(2)}) collective-permute-start(bf16[384,768]{1,0:T(8,128)(2,1)S(1)} %get-tuple-element.190), channel_id=1, source_target_pairs={{0,4},{4,0},{8,12},{12,8},{16,20},{20,16},{24,28},{28,24},{1,5},{5... | collective-permute-start | bytes 1769480 | tf_op jit(solution)/shard_map/ppermute | solution.py:874
  155.5 40.7 %collective-permute-start.37 = (bf16[256,768]{1,0:T(8,128)(2,1)S(1)}, bf16[256,768]{1,0:T(8,128)(2,1)S(1)}, u32[]{:S(2)}, u32[]{:S(2)}) collective-permute-start(bf16[256,768]{1,0:T(8,128)(2,1)S(1)} %get-tuple-element.180), channel_id=1, source_target_pairs={{0,1},{1,2},{2,3},{3,0},{4,5},{5,6},{6,7},{7,4},{8,9},{9,10},{10,1... | collective-permute-start | bytes 1179656 | tf_op jit(solution)/shard_map/ppermute | solution.py:869
  158.9 37.9 %collective-permute-start.38 = (bf16[256,768]{1,0:T(8,128)(2,1)S(1)}, bf16[256,768]{1,0:T(8,128)(2,1)S(1)}, u32[]{:S(2)}, u32[]{:S(2)}) collective-permute-start(bf16[256,768]{1,0:T(8,128)(2,1)S(1)} %get-tuple-element.181), channel_id=1, source_target_pairs={{0,2},{1,3},{2,0},{3,1},{4,6},{5,7},{6,4},{7,5},{8,10},{9,11},{10,... | collective-permute-start | bytes 1179656 | tf_op jit(solution)/shard_map/ppermute | solution.py:869
  167.3 53.1 %collective-permute-start.39 = (bf16[256,768]{1,0:T(8,128)(2,1)S(1)}, bf16[256,768]{1,0:T(8,128)(2,1)S(1)}, u32[]{:S(2)}, u32[]{:S(2)}) collective-permute-start(bf16[256,768]{1,0:T(8,128)(2,1)S(1)} %get-tuple-element.182), channel_id=1, source_target_pairs={{0,3},{1,0},{2,1},{3,2},{4,7},{5,4},{6,5},{7,6},{8,11},{9,8},{10,9... | collective-permute-start | bytes 1179656 | tf_op jit(solution)/shard_map/ppermute | solution.py:869
  181.8 10.6 %collective-permute-start.29 = (bf16[528,128]{1,0:T(8,128)(2,1)S(1)}, bf16[528,128]{1,0:T(8,128)(2,1)S(1)}, u32[]{:S(2)}, u32[]{:S(2)}) collective-permute-start(bf16[528,128]{1,0:T(8,128)(2,1)S(1)} %get-tuple-element.155), channel_id=1, source_target_pairs={{0,3},{1,0},{2,1},{3,2},{4,7},{5,4},{6,5},{7,6},{8,11},{9,8},{10,9... | collective-permute-start | bytes 405512 | tf_op jit(solution)/shard_map/ppermute | solution.py:869
  192.4 14.1 %collective-permute-start.45 = (bf16[384,384]{1,0:T(8,128)(2,1)S(1)}, bf16[384,384]{1,0:T(8,128)(2,1)S(1)}, u32[]{:S(2)}, u32[]{:S(2)}) collective-permute-start(bf16[384,384]{1,0:T(8,128)(2,1)S(1)} %get-tuple-element.192), channel_id=1, source_target_pairs={{0,4},{4,0},{8,12},{12,8},{16,20},{20,16},{24,28},{28,24},{1,5},{5... | collective-permute-start | bytes 884744 | tf_op jit(solution)/shard_map/ppermute | solution.py:874
  196.8 11.6 %collective-permute-start.32 = (f32[8,768]{1,0:T(8,128)S(1)}, f32[8,768]{1,0:T(8,128)S(1)}, u32[]{:S(2)}, u32[]{:S(2)}) collective-permute-start(f32[8,768]{1,0:T(8,128)S(1)} %get-tuple-element.172.refs_1_), channel_id=1, source_target_pairs={{0,3},{1,0},{2,1},{3,2},{4,7},{5,4},{6,5},{7,6},{8,11},{9,8},{10,9... | collective-permute-start | bytes 73736 | tf_op jit(solution)/shard_map/ppermute | solution.py:869
  201.0 40.4 %collective-permute-start.34 = (bf16[256,768]{1,0:T(8,128)(2,1)S(1)}, bf16[256,768]{1,0:T(8,128)(2,1)S(1)}, u32[]{:S(2)}, u32[]{:S(2)}) collective-permute-start(bf16[256,768]{1,0:T(8,128)(2,1)S(1)} %get-tuple-element.176), channel_id=1, source_target_pairs={{0,1},{1,2},{2,3},{3,0},{4,5},{5,6},{6,7},{7,4},{8,9},{9,10},{10,1... | collective-permute-start | bytes 1179656 | tf_op jit(solution)/shard_map/ppermute | solution.py:869
  206.5 11.0 %collective-permute-start.31 = (f32[8,768]{1,0:T(8,128)S(1)}, f32[8,768]{1,0:T(8,128)S(1)}, u32[]{:S(2)}, u32[]{:S(2)}) collective-permute-start(f32[8,768]{1,0:T(8,128)S(1)} %get-tuple-element.172.refs_1_), channel_id=1, source_target_pairs={{0,2},{1,3},{2,0},{3,1},{4,6},{5,7},{6,4},{7,5},{8,10},{9,11},{10,... | collective-permute-start | bytes 73736 | tf_op jit(solution)/shard_map/ppermute | solution.py:869
  207.1 12.2 %collective-permute-start.30 = (f32[8,768]{1,0:T(8,128)S(1)}, f32[8,768]{1,0:T(8,128)S(1)}, u32[]{:S(2)}, u32[]{:S(2)}) collective-permute-start(f32[8,768]{1,0:T(8,128)S(1)} %get-tuple-element.172.refs_1_), channel_id=1, source_target_pairs={{0,1},{1,2},{2,3},{3,0},{4,5},{5,6},{6,7},{7,4},{8,9},{9,10},{10,1... | collective-permute-start | bytes 73736 | tf_op jit(solution)/shard_map/ppermute | solution.py:869
  208.4 16.0 %collective-permute-start.47 = (bf16[96,1280]{1,0:T(8,128)(2,1)S(1)}, bf16[96,1280]{1,0:T(8,128)(2,1)S(1)}, u32[]{:S(2)}, u32[]{:S(2)}) collective-permute-start(bf16[96,1280]{1,0:T(8,128)(2,1)S(1)} %get-tuple-element.196), channel_id=1, source_target_pairs={{0,8},{4,12},{8,16},{12,20},{16,24},{20,28},{24,0},{28,4},{1,9},{5... | collective-permute-start | bytes 737288 | tf_op jit(solution)/shard_map/ppermute | solution.py:1183
  222.4 21.4 %collective-permute-start.35 = (bf16[256,768]{1,0:T(8,128)(2,1)S(1)}, bf16[256,768]{1,0:T(8,128)(2,1)S(1)}, u32[]{:S(2)}, u32[]{:S(2)}) collective-permute-start(bf16[256,768]{1,0:T(8,128)(2,1)S(1)} %get-tuple-element.177), channel_id=1, source_target_pairs={{0,2},{1,3},{2,0},{3,1},{4,6},{5,7},{6,4},{7,5},{8,10},{9,11},{10,... | collective-permute-start | bytes 1179656 | tf_op jit(solution)/shard_map/ppermute | solution.py:869
  236.3 10.4 %collective-permute-start.50 = (bf16[96,1280]{1,0:T(8,128)(2,1)S(1)}, bf16[96,1280]{1,0:T(8,128)(2,1)S(1)}, u32[]{:S(2)}, u32[]{:S(2)}) collective-permute-start(bf16[96,1280]{1,0:T(8,128)(2,1)S(1)} %shard_map.354.refs_1_), channel_id=1, source_target_pairs={{0,8},{4,12},{8,16},{12,20},{16,24},{20,28},{24,0},{28,4},{1,9},{5... | collective-permute-start | bytes 737288 | tf_op jit(solution)/shard_map/ppermute | solution.py:1183
  (44 other events, 376.5 us)

commit v3 on v2

--- a/solution.py
+++ b/solution.py
@@ -94,17 +94,17 @@
     quarter = span // 4
     side = lax.rem(lax.div(place[1], 2), 4)
     out[0:quarter, :] = w_bt[pl.ds(pl.multiple_of(side * quarter, quarter), quarter), :]
-    rows = jnp.concatenate([conv[...], bias[...].reshape(1, span), jnp.zeros((11, span), F32)], axis=0)
+    rows = jnp.concatenate([conv[...], bias[...].reshape(1, span), jnp.zeros((3, span), F32)], axis=0)
     high, rest = split(rows)
     mid, rest = split(rest)
     wide = jnp.concatenate(
-        [high.astype(F32), mid.astype(F32), rest, jnp.zeros((16, d - 3 * span), F32)], axis=1
+        [high.astype(F32), mid.astype(F32), rest, jnp.zeros((8, d - 3 * span), F32)], axis=1
     )
     row = jnp.concatenate(
         [gain[...].astype(F32).reshape(1, gain.shape[0]), jnp.zeros((1, d - gain.shape[0]), F32)],
         axis=1,
     )
-    wide = jnp.where(iota((16, d), 0) == 5, row, wide)
+    wide = jnp.where(iota((8, d), 0) == 5, row, wide)
     out[quarter:, :] = wide.astype(B16)
 
 
@@ -939,7 +939,7 @@
     quarter = span // 4
     (early,) = call(
         prep_kernel, (), [w_bt_own, conv_bcoef, conv_bcoef_bias, in_gain], [None] * 4,
-        [shape((quarter + 16, d), B16)], [None], scalars=(place,),
+        [shape((quarter + 8, d), B16)], [None], scalars=(place,),
         fetch=tuple(range(4)),
     )
     earlies = spread(early, "wt")

time: 258 us -> 257 us (level)
  no operation moved by 1% of the time
where the time goes in v3:
time: 257 us; the launch traced here: 255 us
  starting transfers between devices  96.4 us (38%)
  waiting for transfers between devices  88.3 us (34%)
  Pallas kernels  66.5 us (26%)
    ppermute x24, waiting for transfers between devices, ring(): lax.ppermute(value, axis, [(i, (i + distance) % count) for i in range(cou...  77.8 us
    pallas_call x23, Pallas kernels, call(): pl.pallas_call(body, out_shape=outs, grid_spec=pltpu.PrefetchScalarGridSp...  66.5 us
    ppermute x24, starting transfers between devices, ring(): lax.ppermute(value, axis, [(i, (i + distance) % count) for i in range(cou...  50.6 us
    ppermute x9, starting transfers between devices, pair_ring(): lax.ppermute(value, 'seq', [(i, (i + 2 * k) % n_seq) for i in range(n_seq)])  20.5 us
    ppermute x13, starting transfers between devices, swap(): return lax.ppermute(value, axis, [(i, i ^ 1 << bit) for i in range(count)])  12 us
    ppermute x6, starting transfers between devices, states(): got.append(lax.ppermute(both, 'seq', pairs))  9.93 us
    ppermute x13, waiting for transfers between devices, swap(): return lax.ppermute(value, axis, [(i, i ^ 1 << bit) for i in range(count)])  6.43 us
  transfers between devices with their start and end apart: 57, of which 19 were waited for; matrix products, arithmetic and copies ran while one was open for 1% of the time, Pallas kernels for 16%

profile of v3, /device:TPU:0, one launch (start us, length us, event | category | flops | bytes accessed | tf_op | source)
XLA Modules:
  0.0 255.4 jit_solution(543204932548017372)
XLA Ops:
  0.6 5.1 %collective-permute-start.8 = (bf16[256,768]{1,0:T(8,128)(2,1)}, bf16[256,768]{1,0:T(8,128)(2,1)S(1)}, u32[]{:S(2)}, u32[]{:S(2)}) collective-permute-start(bf16[256,768]{1,0:T(8,128)(2,1)} %refs_1_.6), channel_id=1, source_target_pairs={{0,3},{1,0},{2,1},{3,2},{4,7},{5,4},{6,5},{7,6},{8,11},{9,8},{10,9... | collective-permute-start | bytes 1179656 | tf_op jit(solution)/shard_map/ppermute | solution.py:869
  12.4 20.1 %collective-permute-done.2.refs_3_.refs_4_ = bf16[24,768]{1,0:T(8,128)(2,1)S(1)} collective-permute-done((bf16[24,768]{1,0:T(8,128)(2,1)S(1)}, bf16[24,768]{1,0:T(8,128)(2,1)S(1)}, u32[]{:S(2)}, u32[]{:S(2)}) %collective-permute-start.2) | collective-permute-done | bytes 36896 | tf_op jit(solution)/shard_map/ppermute | solution.py:869
  32.5 10.4 %collective-permute-start = (bf16[24,768]{1,0:T(8,128)(2,1)S(1)}, bf16[24,768]{1,0:T(8,128)(2,1)S(1)}, u32[]{:S(2)}, u32[]{:S(2)}) collective-permute-start(bf16[24,768]{1,0:T(8,128)(2,1)S(1)} %shard_map.333.refs_0_.refs_1_), channel_id=1, source_target_pairs={{0,1},{1,2},{2,3},{3,0},{4,5},{5,6},{6,7},{7,4},{8,9},{9,10},{10,1... | collective-permute-start | bytes 110600 | tf_op jit(solution)/shard_map/ppermute | solution.py:869
  59.4 10.9 %shard_map.336 = (bf16[1024,768]{1,0:T(8,128)(2,1)S(1)}, bf16[1024,384]{1,0:T(8,128)(2,1)S(1)}, bf16[1024,256]{1,0:T(8,128)(2,1)S(1)}, f32[1024,384]{1,0:T(8,128...) custom-call(s32[2]{0:T(128)S(1)} %pad_add_fusion.refs_0_, ...), custom_call_target="tpu_custom_call" | custom-call | flops 2000000000 | bytes 11956224 | tf_op jit(solution)/shard_map/pallas_call | solution.py:847
  70.3 6.5 %collective-permute-start.13 = (bf16[144,384]{1,0:T(8,128)(2,1)S(1)}, bf16[144,384]{1,0:T(8,128)(2,1)S(1)}, u32[]{:S(2)}, u32[]{:S(2)}) collective-permute-start(bf16[144,384]{1,0:T(8,128)(2,1)S(1)} %get-tuple-element.133.refs_1_), channel_id=1, source_target_pairs={{0,4},{4,0},{8,12},{12,8},{16,20},{20,16},{24,28},{28,24},{1,5},{5... | collective-permute-start | bytes 331784 | tf_op jit(solution)/shard_map/ppermute | solution.py:874
  80.7 3.4 %collective-permute-start.19 = (bf16[256,768]{1,0:T(8,128)(2,1)S(1)}, bf16[256,768]{1,0:T(8,128)(2,1)S(1)}, u32[]{:S(2)}, u32[]{:S(2)}) collective-permute-start(bf16[256,768]{1,0:T(8,128)(2,1)S(1)} %copy-done), channel_id=1, source_target_pairs={{0,3},{1,0},{2,1},{3,2},{4,7},{5,4},{6,5},{7,6},{8,11},{9,8},{10,9... | collective-permute-start | bytes 1179656 | tf_op jit(solution)/shard_map/ppermute | solution.py:869
  90.2 3.6 %shard_map.337 = (f32[1024,384]{1,0:T(8,128)S(1)}, f32[1024,384]{1,0:T(8,128)S(1)}) custom-call(bf16[1024,768]{1,0:T(8,128)(2,1)S(1)} %get-tuple-element.119.refs_0_.refs_7_.refs_8_.refs_2_, bf16[768,384]{1,0:T(8,128)(2,1)S(1)} %copy-done.10, f32[1024,384]{1,0:T(8,128)S(1)} %get-tuple-element.120.refs_2_.refs_4_.refs_6_, ...), custom_call_target="tpu_custom_call" | custom-call | flops 2000000000 | bytes 8826880 | tf_op jit(solution)/shard_map/pallas_call | solution.py:847
  93.9 4.9 %shard_map.339 = (f32[1024,384]{1,0:T(8,128)S(1)}, f32[1024,384]{1,0:T(8,128)S(1)}, f32[1024,384]{1,0:T(8,128)S(1)}, f32[8,1024]{1,0:T(8,128)S(1)}, f32[128,384]...) custom-call(s32[2]{0:T(128)S(1)} %pad_add_fusion.refs_0_, ...), custom_call_target="tpu_custom_call" | custom-call | flops 2000000000 | bytes 12529664 | tf_op jit(solution)/shard_map/pallas_call | solution.py:847
  98.8 20.1 %collective-permute-done.18.refs_5_ = bf16[256,768]{1,0:T(8,128)(2,1)S(1)} collective-permute-done((bf16[256,768]{1,0:T(8,128)(2,1)S(1)}, bf16[256,768]{1,0:T(8,128)(2,1)S(1)}, u32[]{:S(2)}, u32[]{:S(2)}) %collective-permute-start.18) | collective-permute-done | bytes 393248 | tf_op jit(solution)/shard_map/ppermute | solution.py:869
  118.8 3.2 %shard_map.340 = (f32[1024,384]{1,0:T(8,128)S(1)}, f32[8,1024]{1,0:T(8,128)S(1)}, bf16[1024,768]{1,0:T(8,128)(2,1)S(1)}) custom-call(s32[2]{0:T(128)S(1)} %pad_add_fusion.refs_0_, f32[1024,384]{1,0:T(8,128)S(1)} %get-tuple-element.137.refs_1_, f32[8,1024]{1,0:T(8,128)S(1)} %get-tuple-element.138.refs_2_, bf16[256,768]{1,0:T(8,128)(2,1)S(1)} %copy-done, ...), custom_call_target="tpu_custom_call" | custom-call | flops 1000000000 | bytes 6959104 | tf_op jit(solution)/shard_map/pallas_call | solution.py:847
  139.3 4.9 %shard_map.342 = (f32[1024,384]{1,0:T(8,128)S(1)}, f32[1024,128]{1,0:T(8,128)S(1)}, f32[1024,256]{1,0:T(8,128)S(1)}) custom-call(f32[1024,384]{1,0:T(8,128)S(1)} %get-tuple-element.141.refs_0_.refs_2_, bf16[1024,256]{1,0:T(8,128)(2,1)S(1)} %get-tuple-element.121.refs_3_.refs_5_.refs_1_.refs_8_, f32[1024,128]{1,0:T(8,128)S(1)} %get-tuple-element.122.refs_4_.refs_2_.refs_9_, ...), custom_call_target="tpu_custom_call" | custom-call | flops 4000000000 | bytes 8044544 | tf_op jit(solution)/shard_map/pallas_call | solution.py:847
  145.6 4.8 %shard_map.344 = (bf16[528,128]{1,0:T(8,128)(2,1)S(1)}, bf16[528,128]{1,0:T(8,128)(2,1)S(1)}, bf16[528,128]{1,0:T(8,128)(2,1)S(1)}, bf16[528,128]{1,0:T(8,128)(2...) custom-call(s32[2]{0:T(128)S(1)} %pad_add_fusion.refs_0_, s32[1]{0:T(128)S(6)} %copy.39.refs_1_, ...), custom_call_target="tpu_custom_call" | custom-call | flops 1000000000 | bytes 5963776 | tf_op jit(solution)/shard_map/pallas_call | solution.py:847
  154.6 3.3 %collective-permute-start.37 = (bf16[256,768]{1,0:T(8,128)(2,1)S(1)}, bf16[256,768]{1,0:T(8,128)(2,1)S(1)}, u32[]{:S(2)}, u32[]{:S(2)}) collective-permute-start(bf16[256,768]{1,0:T(8,128)(2,1)S(1)} %get-tuple-element.180), channel_id=1, source_target_pairs={{0,1},{1,2},{2,3},{3,0},{4,5},{5,6},{6,7},{7,4},{8,9},{9,10},{10,1... | collective-permute-start | bytes 1179656 | tf_op jit(solution)/shard_map/ppermute | solution.py:869
  158.0 8.3 %shard_map.345 = (bf16[1024,384]{1,0:T(8,128)(2,1)S(1)}, bf16[1024,128]{1,0:T(8,128)(2,1)S(1)}, f32[8,384]{1,0:T(8,128)S(1)}, f32[8,384]{1,0:T(8,128)S(1)}, f32[8,128]{1,0:T(8,128)S(1)}) custom-call(s32[2]{0:T(128)S(1)} %pad_add_fusion.refs_0_, s32[1]{0:T(128)S(6)} %copy.39.refs_1_, f32[1024,384]{1,0:T(8,128)S(1)} %get-tuple-element.141.refs_0_.refs_2_, ...), custom_call_target="tpu_custom_call" | custom-call | flops 1000000000 | bytes 13455360 | tf_op jit(solution)/shard_map/pallas_call | solution.py:847
  168.8 12.0 %collective-permute-done.28.refs_3_ = bf16[528,128]{1,0:T(8,128)(2,1)S(1)} collective-permute-done((bf16[528,128]{1,0:T(8,128)(2,1)S(1)}, bf16[528,128]{1,0:T(8,128)(2,1)S(1)}, u32[]{:S(2)}, u32[]{:S(2)}) %collective-permute-start.28) | collective-permute-done | bytes 135200 | tf_op jit(solution)/shard_map/ppermute | solution.py:869
  180.9 4.0 %shard_map.346 = (f32[1024,768]{1,0:T(8,128)S(1)}, bf16[384,384]{1,0:T(8,128)(2,1)S(1)}, bf16[384,384]{1,0:T(8,128)(2,1)S(1)}) custom-call(s32[2]{0:T(128)S(1)} %pad_add_fusion.refs_0_, bf16[1024,384]{1,0:T(8,128)(2,1)S(1)} %get-tuple-element.163.refs_1_.refs_2_, bf16[1024,384]{1,0:T(8,128)(2,1)S(1)} %get-tuple-element.163.refs_1_.refs_2_, ...), custom_call_target="tpu_custom_call" | custom-call | flops 2000000000 | bytes 9330688 | tf_op jit(solution)/shard_map/pallas_call | solution.py:847
  184.9 6.6 %collective-permute-done.29.refs_4_ = bf16[528,128]{1,0:T(8,128)(2,1)S(1)} collective-permute-done((bf16[528,128]{1,0:T(8,128)(2,1)S(1)}, bf16[528,128]{1,0:T(8,128)(2,1)S(1)}, u32[]{:S(2)}, u32[]{:S(2)}) %collective-permute-start.29) | collective-permute-done | bytes 135200 | tf_op jit(solution)/shard_map/ppermute | solution.py:869
  191.5 3.8 %shard_map.347 = (bf16[256,768]{1,0:T(8,128)(2,1)S(1)}, bf16[256,768]{1,0:T(8,128)(2,1)S(1)}, bf16[256,768]{1,0:T(8,128)(2,1)S(1)}, bf16[256,768]{1,0:T(8,128)(2...) custom-call(s32[2]{0:T(128)S(1)} %pad_add_fusion.refs_0_, ...), custom_call_target="tpu_custom_call" | custom-call | flops 1000000000 | bytes 8114176 | tf_op jit(solution)/shard_map/pallas_call | solution.py:847
  195.9 4.2 %collective-permute-start.32 = (f32[8,768]{1,0:T(8,128)S(1)}, f32[8,768]{1,0:T(8,128)S(1)}, u32[]{:S(2)}, u32[]{:S(2)}) collective-permute-start(f32[8,768]{1,0:T(8,128)S(1)} %get-tuple-element.172.refs_1_), channel_id=1, source_target_pairs={{0,3},{1,0},{2,1},{3,2},{4,7},{5,4},{6,5},{7,6},{8,11},{9,8},{10,9... | collective-permute-start | bytes 73736 | tf_op jit(solution)/shard_map/ppermute | solution.py:869
  200.1 5.5 %collective-permute-start.34 = (bf16[256,768]{1,0:T(8,128)(2,1)S(1)}, bf16[256,768]{1,0:T(8,128)(2,1)S(1)}, u32[]{:S(2)}, u32[]{:S(2)}) collective-permute-start(bf16[256,768]{1,0:T(8,128)(2,1)S(1)} %get-tuple-element.176), channel_id=1, source_target_pairs={{0,1},{1,2},{2,3},{3,0},{4,5},{5,6},{6,7},{7,4},{8,9},{9,10},{10,1... | collective-permute-start | bytes 1179656 | tf_op jit(solution)/shard_map/ppermute | solution.py:869
  208.7 7.9 %collective-permute-done.31.refs_3_ = f32[8,768]{1,0:T(8,128)S(1)} collective-permute-done((f32[8,768]{1,0:T(8,128)S(1)}, f32[8,768]{1,0:T(8,128)S(1)}, u32[]{:S(2)}, u32[]{:S(2)}) %collective-permute-start.31) | collective-permute-done | bytes 24608 | tf_op jit(solution)/shard_map/ppermute | solution.py:869
  226.0 7.5 %collective-permute-start.41 = (f32[8,768]{1,0:T(8,128)S(1)}, f32[8,768]{1,0:T(8,128)S(1)}, u32[]{:S(2)}, u32[]{:S(2)}) collective-permute-start(f32[8,768]{1,0:T(8,128)S(1)} %shard_map.350.refs_1_), channel_id=1, source_target_pairs={{0,8},{4,12},{8,16},{12,20},{16,24},{20,28},{24,0},{28,4},{1,9},{5... | collective-permute-start | bytes 73736 | tf_op jit(solution)/shard_map/ppermute | solution.py:1183
  235.4 5.1 %collective-permute-start.50 = (bf16[96,1280]{1,0:T(8,128)(2,1)S(1)}, bf16[96,1280]{1,0:T(8,128)(2,1)S(1)}, u32[]{:S(2)}, u32[]{:S(2)}) collective-permute-start(bf16[96,1280]{1,0:T(8,128)(2,1)S(1)} %shard_map.354.refs_1_), channel_id=1, source_target_pairs={{0,8},{4,12},{8,16},{12,20},{16,24},{20,28},{24,0},{28,4},{1,9},{5... | collective-permute-start | bytes 737288 | tf_op jit(solution)/shard_map/ppermute | solution.py:1183
  247.0 3.4 %collective-permute-done.36.refs_9_ = bf16[256,768]{1,0:T(8,128)(2,1)S(1)} collective-permute-done((bf16[256,768]{1,0:T(8,128)(2,1)S(1)}, bf16[256,768]{1,0:T(8,128)(2,1)S(1)}, u32[]{:S(2)}, u32[]{:S(2)}) %collective-permute-start.36) | collective-permute-done | bytes 393248 | tf_op jit(solution)/shard_map/ppermute | solution.py:869
  (138 shorter events, 84.1 us)
Async XLA Ops:
  0.6 58.7 %collective-permute-start.8 = (bf16[256,768]{1,0:T(8,128)(2,1)}, bf16[256,768]{1,0:T(8,128)(2,1)S(1)}, u32[]{:S(2)}, u32[]{:S(2)}) collective-permute-start(bf16[256,768]{1,0:T(8,128)(2,1)} %refs_1_.6), channel_id=1, source_target_pairs={{0,3},{1,0},{2,1},{3,2},{4,7},{5,4},{6,5},{7,6},{8,11},{9,8},{10,9... | collective-permute-start | bytes 1179656 | tf_op jit(solution)/shard_map/ppermute | solution.py:869
  5.8 53.5 %collective-permute-start.7 = (bf16[256,768]{1,0:T(8,128)(2,1)}, bf16[256,768]{1,0:T(8,128)(2,1)S(1)}, u32[]{:S(2)}, u32[]{:S(2)}) collective-permute-start(bf16[256,768]{1,0:T(8,128)(2,1)} %refs_1_.6), channel_id=1, source_target_pairs={{0,2},{1,3},{2,0},{3,1},{4,6},{5,7},{6,4},{7,5},{8,10},{9,11},{10,... | collective-permute-start | bytes 1179656 | tf_op jit(solution)/shard_map/ppermute | solution.py:869
  5.8 53.5 %collective-permute-start.6 = (bf16[256,768]{1,0:T(8,128)(2,1)}, bf16[256,768]{1,0:T(8,128)(2,1)S(1)}, u32[]{:S(2)}, u32[]{:S(2)}) collective-permute-start(bf16[256,768]{1,0:T(8,128)(2,1)} %refs_1_.6), channel_id=1, source_target_pairs={{0,1},{1,2},{2,3},{3,0},{4,5},{5,6},{6,7},{7,4},{8,9},{9,10},{10,1... | collective-permute-start | bytes 1179656 | tf_op jit(solution)/shard_map/ppermute | solution.py:869
  8.4 24.1 %collective-permute-start.2 = (bf16[24,768]{1,0:T(8,128)(2,1)S(1)}, bf16[24,768]{1,0:T(8,128)(2,1)S(1)}, u32[]{:S(2)}, u32[]{:S(2)}) collective-permute-start(bf16[24,768]{1,0:T(8,128)(2,1)S(1)} %shard_map.333.refs_0_.refs_1_), channel_id=1, source_target_pairs={{0,3},{1,0},{2,1},{3,2},{4,7},{5,4},{6,5},{7,6},{8,11},{9,8},{10,9... | collective-permute-start | bytes 110600 | tf_op jit(solution)/shard_map/ppermute | solution.py:869
  11.3 31.6 %collective-permute-start.1 = (bf16[24,768]{1,0:T(8,128)(2,1)S(1)}, bf16[24,768]{1,0:T(8,128)(2,1)S(1)}, u32[]{:S(2)}, u32[]{:S(2)}) collective-permute-start(bf16[24,768]{1,0:T(8,128)(2,1)S(1)} %shard_map.333.refs_0_.refs_1_), channel_id=1, source_target_pairs={{0,2},{1,3},{2,0},{3,1},{4,6},{5,7},{6,4},{7,5},{8,10},{9,11},{10,... | collective-permute-start | bytes 110600 | tf_op jit(solution)/shard_map/ppermute | solution.py:869
  32.5 12.0 %collective-permute-start = (bf16[24,768]{1,0:T(8,128)(2,1)S(1)}, bf16[24,768]{1,0:T(8,128)(2,1)S(1)}, u32[]{:S(2)}, u32[]{:S(2)}) collective-permute-start(bf16[24,768]{1,0:T(8,128)(2,1)S(1)} %shard_map.333.refs_0_.refs_1_), channel_id=1, source_target_pairs={{0,1},{1,2},{2,3},{3,0},{4,5},{5,6},{6,7},{7,4},{8,9},{9,10},{10,1... | collective-permute-start | bytes 110600 | tf_op jit(solution)/shard_map/ppermute | solution.py:869
  80.7 18.1 %collective-permute-start.19 = (bf16[256,768]{1,0:T(8,128)(2,1)S(1)}, bf16[256,768]{1,0:T(8,128)(2,1)S(1)}, u32[]{:S(2)}, u32[]{:S(2)}) collective-permute-start(bf16[256,768]{1,0:T(8,128)(2,1)S(1)} %copy-done), channel_id=1, source_target_pairs={{0,3},{1,0},{2,1},{3,2},{4,7},{5,4},{6,5},{7,6},{8,11},{9,8},{10,9... | collective-permute-start | bytes 1179656 | tf_op jit(solution)/shard_map/ppermute | solution.py:869
  84.0 34.8 %collective-permute-start.18 = (bf16[256,768]{1,0:T(8,128)(2,1)S(1)}, bf16[256,768]{1,0:T(8,128)(2,1)S(1)}, u32[]{:S(2)}, u32[]{:S(2)}) collective-permute-start(bf16[256,768]{1,0:T(8,128)(2,1)S(1)} %copy-done), channel_id=1, source_target_pairs={{0,2},{1,3},{2,0},{3,1},{4,6},{5,7},{6,4},{7,5},{8,10},{9,11},{10,... | collective-permute-start | bytes 1179656 | tf_op jit(solution)/shard_map/ppermute | solution.py:869
  84.5 34.4 %collective-permute-start.17 = (bf16[256,768]{1,0:T(8,128)(2,1)S(1)}, bf16[256,768]{1,0:T(8,128)(2,1)S(1)}, u32[]{:S(2)}, u32[]{:S(2)}) collective-permute-start(bf16[256,768]{1,0:T(8,128)(2,1)S(1)} %copy-done), channel_id=1, source_target_pairs={{0,1},{1,2},{2,3},{3,0},{4,5},{5,6},{6,7},{7,4},{8,9},{9,10},{10,1... | collective-permute-start | bytes 1179656 | tf_op jit(solution)/shard_map/ppermute | solution.py:869
  150.5 15.9 %collective-permute-start.27 = (bf16[528,128]{1,0:T(8,128)(2,1)S(1)}, bf16[528,128]{1,0:T(8,128)(2,1)S(1)}, u32[]{:S(2)}, u32[]{:S(2)}) collective-permute-start(bf16[528,128]{1,0:T(8,128)(2,1)S(1)} %get-tuple-element.153), channel_id=1, source_target_pairs={{0,1},{1,2},{2,3},{3,0},{4,5},{5,6},{6,7},{7,4},{8,9},{9,10},{10,1... | collective-permute-start | bytes 405512 | tf_op jit(solution)/shard_map/ppermute | solution.py:869
  150.8 30.0 %collective-permute-start.28 = (bf16[528,128]{1,0:T(8,128)(2,1)S(1)}, bf16[528,128]{1,0:T(8,128)(2,1)S(1)}, u32[]{:S(2)}, u32[]{:S(2)}) collective-permute-start(bf16[528,128]{1,0:T(8,128)(2,1)S(1)} %get-tuple-element.154), channel_id=1, source_target_pairs={{0,2},{1,3},{2,0},{3,1},{4,6},{5,7},{6,4},{7,5},{8,10},{9,11},{10,... | collective-permute-start | bytes 405512 | tf_op jit(solution)/shard_map/ppermute | solution.py:869
  154.5 51.6 %collective-permute-start.44 = (bf16[384,768]{1,0:T(8,128)(2,1)S(1)}, bf16[384,768]{1,0:T(8,128)(2,1)S(1)}, u32[]{:S(2)}, u32[]{:S(2)}) collective-permute-start(bf16[384,768]{1,0:T(8,128)(2,1)S(1)} %get-tuple-element.190), channel_id=1, source_target_pairs={{0,4},{4,0},{8,12},{12,8},{16,20},{20,16},{24,28},{28,24},{1,5},{5... | collective-permute-start | bytes 1769480 | tf_op jit(solution)/shard_map/ppermute | solution.py:874
  154.6 40.7 %collective-permute-start.37 = (bf16[256,768]{1,0:T(8,128)(2,1)S(1)}, bf16[256,768]{1,0:T(8,128)(2,1)S(1)}, u32[]{:S(2)}, u32[]{:S(2)}) collective-permute-start(bf16[256,768]{1,0:T(8,128)(2,1)S(1)} %get-tuple-element.180), channel_id=1, source_target_pairs={{0,1},{1,2},{2,3},{3,0},{4,5},{5,6},{6,7},{7,4},{8,9},{9,10},{10,1... | collective-permute-start | bytes 1179656 | tf_op jit(solution)/shard_map/ppermute | solution.py:869
  157.9 37.9 %collective-permute-start.38 = (bf16[256,768]{1,0:T(8,128)(2,1)S(1)}, bf16[256,768]{1,0:T(8,128)(2,1)S(1)}, u32[]{:S(2)}, u32[]{:S(2)}) collective-permute-start(bf16[256,768]{1,0:T(8,128)(2,1)S(1)} %get-tuple-element.181), channel_id=1, source_target_pairs={{0,2},{1,3},{2,0},{3,1},{4,6},{5,7},{6,4},{7,5},{8,10},{9,11},{10,... | collective-permute-start | bytes 1179656 | tf_op jit(solution)/shard_map/ppermute | solution.py:869
  166.3 53.1 %collective-permute-start.39 = (bf16[256,768]{1,0:T(8,128)(2,1)S(1)}, bf16[256,768]{1,0:T(8,128)(2,1)S(1)}, u32[]{:S(2)}, u32[]{:S(2)}) collective-permute-start(bf16[256,768]{1,0:T(8,128)(2,1)S(1)} %get-tuple-element.182), channel_id=1, source_target_pairs={{0,3},{1,0},{2,1},{3,2},{4,7},{5,4},{6,5},{7,6},{8,11},{9,8},{10,9... | collective-permute-start | bytes 1179656 | tf_op jit(solution)/shard_map/ppermute | solution.py:869
  180.9 10.6 %collective-permute-start.29 = (bf16[528,128]{1,0:T(8,128)(2,1)S(1)}, bf16[528,128]{1,0:T(8,128)(2,1)S(1)}, u32[]{:S(2)}, u32[]{:S(2)}) collective-permute-start(bf16[528,128]{1,0:T(8,128)(2,1)S(1)} %get-tuple-element.155), channel_id=1, source_target_pairs={{0,3},{1,0},{2,1},{3,2},{4,7},{5,4},{6,5},{7,6},{8,11},{9,8},{10,9... | collective-permute-start | bytes 405512 | tf_op jit(solution)/shard_map/ppermute | solution.py:869
  191.5 14.1 %collective-permute-start.45 = (bf16[384,384]{1,0:T(8,128)(2,1)S(1)}, bf16[384,384]{1,0:T(8,128)(2,1)S(1)}, u32[]{:S(2)}, u32[]{:S(2)}) collective-permute-start(bf16[384,384]{1,0:T(8,128)(2,1)S(1)} %get-tuple-element.192), channel_id=1, source_target_pairs={{0,4},{4,0},{8,12},{12,8},{16,20},{20,16},{24,28},{28,24},{1,5},{5... | collective-permute-start | bytes 884744 | tf_op jit(solution)/shard_map/ppermute | solution.py:874
  195.9 11.6 %collective-permute-start.32 = (f32[8,768]{1,0:T(8,128)S(1)}, f32[8,768]{1,0:T(8,128)S(1)}, u32[]{:S(2)}, u32[]{:S(2)}) collective-permute-start(f32[8,768]{1,0:T(8,128)S(1)} %get-tuple-element.172.refs_1_), channel_id=1, source_target_pairs={{0,3},{1,0},{2,1},{3,2},{4,7},{5,4},{6,5},{7,6},{8,11},{9,8},{10,9... | collective-permute-start | bytes 73736 | tf_op jit(solution)/shard_map/ppermute | solution.py:869
  200.1 40.4 %collective-permute-start.34 = (bf16[256,768]{1,0:T(8,128)(2,1)S(1)}, bf16[256,768]{1,0:T(8,128)(2,1)S(1)}, u32[]{:S(2)}, u32[]{:S(2)}) collective-permute-start(bf16[256,768]{1,0:T(8,128)(2,1)S(1)} %get-tuple-element.176), channel_id=1, source_target_pairs={{0,1},{1,2},{2,3},{3,0},{4,5},{5,6},{6,7},{7,4},{8,9},{9,10},{10,1... | collective-permute-start | bytes 1179656 | tf_op jit(solution)/shard_map/ppermute | solution.py:869
  205.5 11.0 %collective-permute-start.31 = (f32[8,768]{1,0:T(8,128)S(1)}, f32[8,768]{1,0:T(8,128)S(1)}, u32[]{:S(2)}, u32[]{:S(2)}) collective-permute-start(f32[8,768]{1,0:T(8,128)S(1)} %get-tuple-element.172.refs_1_), channel_id=1, source_target_pairs={{0,2},{1,3},{2,0},{3,1},{4,6},{5,7},{6,4},{7,5},{8,10},{9,11},{10,... | collective-permute-start | bytes 73736 | tf_op jit(solution)/shard_map/ppermute | solution.py:869
  206.1 12.2 %collective-permute-start.30 = (f32[8,768]{1,0:T(8,128)S(1)}, f32[8,768]{1,0:T(8,128)S(1)}, u32[]{:S(2)}, u32[]{:S(2)}) collective-permute-start(f32[8,768]{1,0:T(8,128)S(1)} %get-tuple-element.172.refs_1_), channel_id=1, source_target_pairs={{0,1},{1,2},{2,3},{3,0},{4,5},{5,6},{6,7},{7,4},{8,9},{9,10},{10,1... | collective-permute-start | bytes 73736 | tf_op jit(solution)/shard_map/ppermute | solution.py:869
  207.5 16.0 %collective-permute-start.47 = (bf16[96,1280]{1,0:T(8,128)(2,1)S(1)}, bf16[96,1280]{1,0:T(8,128)(2,1)S(1)}, u32[]{:S(2)}, u32[]{:S(2)}) collective-permute-start(bf16[96,1280]{1,0:T(8,128)(2,1)S(1)} %get-tuple-element.196), channel_id=1, source_target_pairs={{0,8},{4,12},{8,16},{12,20},{16,24},{20,28},{24,0},{28,4},{1,9},{5... | collective-permute-start | bytes 737288 | tf_op jit(solution)/shard_map/ppermute | solution.py:1183
  221.4 21.4 %collective-permute-start.35 = (bf16[256,768]{1,0:T(8,128)(2,1)S(1)}, bf16[256,768]{1,0:T(8,128)(2,1)S(1)}, u32[]{:S(2)}, u32[]{:S(2)}) collective-permute-start(bf16[256,768]{1,0:T(8,128)(2,1)S(1)} %get-tuple-element.177), channel_id=1, source_target_pairs={{0,2},{1,3},{2,0},{3,1},{4,6},{5,7},{6,4},{7,5},{8,10},{9,11},{10,... | collective-permute-start | bytes 1179656 | tf_op jit(solution)/shard_map/ppermute | solution.py:869
  235.4 10.4 %collective-permute-start.50 = (bf16[96,1280]{1,0:T(8,128)(2,1)S(1)}, bf16[96,1280]{1,0:T(8,128)(2,1)S(1)}, u32[]{:S(2)}, u32[]{:S(2)}) collective-permute-start(bf16[96,1280]{1,0:T(8,128)(2,1)S(1)} %shard_map.354.refs_1_), channel_id=1, source_target_pairs={{0,8},{4,12},{8,16},{12,20},{16,24},{20,28},{24,0},{28,4},{1,9},{5... | collective-permute-start | bytes 737288 | tf_op jit(solution)/shard_map/ppermute | solution.py:1183
  (44 other events, 376.9 us)
